TPU v7x, 32 devices: a whole 2x2x4 slice. The times are simulated.
32 devices in a mesh: dp: 8 (over z, y), ctx: 4 (over x, core).
Axes of the slice: x: 2, y: 2, z: 4, core: 2. Of those that a mesh axis runs over, the one named last changes fastest.
Arguments:
- layer_input: bfloat16 [4096, 2048], P(('dp', 'ctx')), may hold values from -6 to 6
- lengths: int32 [8], P('dp'), may hold values from 128 to 512, as said below
- cotangent: bfloat16 [4096, 2048], P(('dp', 'ctx')), may hold values from -6 to 6
- qkv_weight: bfloat16 [2048, 6144], P(('dp', 'ctx')), may hold values from -0.125 to 0.125
- qkv_bias: bfloat16 [6144], P(('dp', 'ctx')), may hold values from -1 to 1
- out_weight: bfloat16 [2048, 2048], P(('dp', 'ctx')), may hold values from -0.75 to 0.75
- out_bias: bfloat16 [2048], P(('dp', 'ctx')), may hold values from -1 to 1
- up_weight: bfloat16 [2048, 8192], P(('dp', 'ctx')), may hold values from -0.125 to 0.125
- up_bias: bfloat16 [8192], P(('dp', 'ctx')), may hold values from -1 to 1
- down_weight: bfloat16 [8192, 2048], P(('dp', 'ctx')), may hold values from -0.0625 to 0.0625
- down_bias: bfloat16 [2048], P(('dp', 'ctx')), may hold values from -1 to 1
- first_gain: bfloat16 [2048], P(('dp', 'ctx')), may hold values from 0.5 to 1.5
- first_bias: bfloat16 [2048], P(('dp', 'ctx')), may hold values from -1 to 1
- second_gain: bfloat16 [2048], P(('dp', 'ctx')), may hold values from 0.5 to 1.5
- second_bias: bfloat16 [2048], P(('dp', 'ctx')), may hold values from -1 to 1
Outputs:
- output: bfloat16 [4096, 2048], P(('dp', 'ctx'))
- input_grad: bfloat16 [4096, 2048], P(('dp', 'ctx'))
- qkv_weight_grad: float32 [2048, 6144], P(('dp', 'ctx'))
- qkv_bias_grad: float32 [6144], P(('dp', 'ctx'))
- out_weight_grad: float32 [2048, 2048], P(('dp', 'ctx'))
- out_bias_grad: float32 [2048], P(('dp', 'ctx'))
- up_weight_grad: float32 [2048, 8192], P(('dp', 'ctx'))
- up_bias_grad: float32 [8192], P(('dp', 'ctx'))
- down_weight_grad: float32 [8192, 2048], P(('dp', 'ctx'))
- down_bias_grad: float32 [2048], P(('dp', 'ctx'))
- first_gain_grad: float32 [2048], P(('dp', 'ctx'))
- first_bias_grad: float32 [2048], P(('dp', 'ctx'))
- second_gain_grad: float32 [2048], P(('dp', 'ctx'))
- second_bias_grad: float32 [2048], P(('dp', 'ctx'))
Inputs may be any that keep to these rules, and one draw needn't show every extreme that they name: `lengths`: every slot's live positions come first; one slot has exactly 512 live positions and another exactly 128.
All inputs are finite; a program needn't handle non-finite values.
Results may differ from a plain program's by a relative error of at most 0.009.
Values may be sent and summed in bfloat16 or wider, within the bound.
A program may use at most 384 MiB of HBM per device.

v0:
```python
import math

import jax
import jax.numpy as jnp
from jax import lax
from jax.sharding import PartitionSpec as P

D = 2048
HEADS = 8
HEAD_DIM = 256
ROT = 64


def normalize(values, gain_vec, shift_vec):
    center = jnp.mean(values, axis=-1, keepdims=True)
    spread = jnp.mean(jnp.square(values - center), axis=-1, keepdims=True)
    inv_std = lax.rsqrt(spread + 1e-05)
    centered = (values - center) * inv_std
    return (centered * gain_vec + shift_vec, centered, inv_std)


def norm_back(d_normed, centered, inv_std, gain_vec):
    gain_grad = jnp.sum(d_normed * centered, axis=0)
    shift_grad = jnp.sum(d_normed, axis=0)
    scaled = d_normed * gain_vec
    d_values = inv_std * (
        scaled
        - jnp.mean(scaled, axis=-1, keepdims=True)
        - centered * jnp.mean(scaled * centered, axis=-1, keepdims=True)
    )
    return (gain_grad, shift_grad, d_values)


def tables(positions):
    half_rot = ROT // 2
    frequency = 10000.0 ** (-2.0 * jnp.arange(half_rot, dtype=jnp.float32) / ROT)
    angles = positions.astype(jnp.float32)[:, None] * frequency[None, :]
    return (jnp.cos(angles)[:, None, :], jnp.sin(angles)[:, None, :])


def rotate(vectors, cosine_tab, sine_tab):
    half_rot = ROT // 2
    low_half = vectors[..., :half_rot]
    high_half = vectors[..., half_rot:ROT]
    return jnp.concatenate(
        [
            low_half * cosine_tab - high_half * sine_tab,
            high_half * cosine_tab + low_half * sine_tab,
            vectors[..., ROT:],
        ],
        axis=-1,
    )


def rotate_back(grads, cosine_tab, sine_tab):
    half_rot = ROT // 2
    low_half = grads[..., :half_rot]
    high_half = grads[..., half_rot:ROT]
    return jnp.concatenate(
        [
            low_half * cosine_tab + high_half * sine_tab,
            high_half * cosine_tab - low_half * sine_tab,
            grads[..., ROT:],
        ],
        axis=-1,
    )


def gelu_slope(values):
    cumulative = 0.5 * (1.0 + lax.erf(values * (1.0 / math.sqrt(2.0))))
    density = jnp.exp(-0.5 * values * values) * (1.0 / math.sqrt(2.0 * math.pi))
    return cumulative + values * density


def local(
    layer_input,
    lengths,
    cotangent,
    qkv_weight,
    qkv_bias,
    out_weight,
    out_bias,
    up_weight,
    up_bias,
    down_weight,
    down_bias,
    first_gain,
    first_bias,
    second_gain,
    second_bias,
):
    gathered = (
        lax.all_gather(qkv_weight, ("dp", "ctx"), axis=0, tiled=True),
        lax.all_gather(qkv_bias, ("dp", "ctx"), axis=0, tiled=True),
        lax.all_gather(out_weight, ("dp", "ctx"), axis=0, tiled=True),
        lax.all_gather(out_bias, ("dp", "ctx"), axis=0, tiled=True),
        lax.all_gather(up_weight, ("dp", "ctx"), axis=0, tiled=True),
        lax.all_gather(up_bias, ("dp", "ctx"), axis=0, tiled=True),
        lax.all_gather(down_weight, ("dp", "ctx"), axis=0, tiled=True),
        lax.all_gather(down_bias, ("dp", "ctx"), axis=0, tiled=True),
        lax.all_gather(first_gain, ("dp", "ctx"), axis=0, tiled=True),
        lax.all_gather(first_bias, ("dp", "ctx"), axis=0, tiled=True),
        lax.all_gather(second_gain, ("dp", "ctx"), axis=0, tiled=True),
        lax.all_gather(second_bias, ("dp", "ctx"), axis=0, tiled=True),
    )
    (
        qkv_full,
        qkvb_full,
        out_full,
        outb_full,
        up_full,
        upb_full,
        down_full,
        downb_full,
        gain_one,
        shift_one,
        gain_two,
        shift_two,
    ) = gathered
    tok_rows = layer_input.shape[0]
    positions = lax.axis_index("ctx") * tok_rows + jnp.arange(tok_rows, dtype=jnp.int32)
    length = lengths[0]
    valid_rows = positions < length
    inputs_f = layer_input.astype(jnp.float32)
    score_scale = 1.0 / math.sqrt(HEAD_DIM)
    normed_one, centered_one, inv_one = normalize(
        inputs_f, gain_one.astype(jnp.float32), shift_one.astype(jnp.float32)
    )
    normed_first = normed_one.astype(jnp.bfloat16)
    joint_proj = jnp.dot(
        normed_first, qkv_full, preferred_element_type=jnp.float32
    ) + qkvb_full.astype(jnp.float32)
    cosine_tab, sine_tab = tables(positions)
    queries = rotate(
        joint_proj[:, :D].reshape(tok_rows, HEADS, HEAD_DIM), cosine_tab, sine_tab
    ).astype(jnp.bfloat16)
    key_local = rotate(
        joint_proj[:, D : 2 * D].reshape(tok_rows, HEADS, HEAD_DIM), cosine_tab, sine_tab
    ).astype(jnp.bfloat16)
    value_local = joint_proj[:, 2 * D :].reshape(tok_rows, HEADS, HEAD_DIM).astype(jnp.bfloat16)
    key_all, value_all = (
        lax.all_gather(key_local, "ctx", axis=0, tiled=True),
        lax.all_gather(value_local, "ctx", axis=0, tiled=True),
    )
    slot_rows = key_all.shape[0]
    key_pos = jnp.arange(slot_rows, dtype=jnp.int32)
    allowed = ((key_pos[None, :] <= positions[:, None]) & (key_pos < length)[None, :])[None]
    scores = (
        jnp.einsum("qhd,khd->hqk", queries, key_all, preferred_element_type=jnp.float32)
        * score_scale
    )
    scores = jnp.where(allowed, scores, -1e30)
    row_max = jnp.max(scores, axis=-1, keepdims=True)
    expo = jnp.exp(scores - row_max)
    row_total = jnp.sum(expo, axis=-1, keepdims=True)
    attention = expo / row_total
    log_total = row_max + jnp.log(row_total)
    mixed = jnp.einsum(
        "hqk,khd->qhd",
        attention.astype(jnp.bfloat16),
        value_all,
        preferred_element_type=jnp.float32,
    )
    head_out = mixed.reshape(tok_rows, D).astype(jnp.bfloat16)
    attn_out = jnp.dot(head_out, out_full, preferred_element_type=jnp.float32) + outb_full.astype(
        jnp.float32
    )
    normed_two, centered_two, inv_two = normalize(
        inputs_f, gain_two.astype(jnp.float32), shift_two.astype(jnp.float32)
    )
    normed_second = normed_two.astype(jnp.bfloat16)
    pre_act = jnp.dot(normed_second, up_full, preferred_element_type=jnp.float32) + upb_full.astype(
        jnp.float32
    )
    hidden = jax.nn.gelu(pre_act, approximate=False).astype(jnp.bfloat16)
    ffn_out = jnp.dot(hidden, down_full, preferred_element_type=jnp.float32) + downb_full.astype(
        jnp.float32
    )
    output = jnp.where(valid_rows[:, None], inputs_f + attn_out + ffn_out, 0.0).astype(jnp.bfloat16)
    back_weights = (
        lax.all_gather(qkv_weight, ("dp", "ctx"), axis=0, tiled=True),
        lax.all_gather(qkv_bias, ("dp", "ctx"), axis=0, tiled=True),
        lax.all_gather(out_weight, ("dp", "ctx"), axis=0, tiled=True),
        lax.all_gather(out_bias, ("dp", "ctx"), axis=0, tiled=True),
        lax.all_gather(up_weight, ("dp", "ctx"), axis=0, tiled=True),
        lax.all_gather(up_bias, ("dp", "ctx"), axis=0, tiled=True),
        lax.all_gather(down_weight, ("dp", "ctx"), axis=0, tiled=True),
        lax.all_gather(down_bias, ("dp", "ctx"), axis=0, tiled=True),
        lax.all_gather(first_gain, ("dp", "ctx"), axis=0, tiled=True),
        lax.all_gather(first_bias, ("dp", "ctx"), axis=0, tiled=True),
        lax.all_gather(second_gain, ("dp", "ctx"), axis=0, tiled=True),
        lax.all_gather(second_bias, ("dp", "ctx"), axis=0, tiled=True),
    )
    qkv_back = back_weights[0]
    out_back = back_weights[2]
    up_back = back_weights[4]
    down_back = back_weights[6]
    gain_one_back = back_weights[8].astype(jnp.float32)
    gain_two_back = back_weights[10].astype(jnp.float32)
    grad_out = jnp.where(valid_rows[:, None], cotangent, jnp.zeros_like(cotangent))
    grad_out_f = grad_out.astype(jnp.float32)
    bias_total = jnp.sum(grad_out_f, axis=0)
    down_grad = jnp.einsum("tf,td->fd", hidden, grad_out, preferred_element_type=jnp.float32)
    d_hidden = jnp.einsum("td,fd->tf", grad_out, down_back, preferred_element_type=jnp.float32)
    d_pre = (d_hidden * gelu_slope(pre_act)).astype(jnp.bfloat16)
    up_grad = jnp.einsum("td,tf->df", normed_second, d_pre, preferred_element_type=jnp.float32)
    up_bias_grad = jnp.sum(d_pre.astype(jnp.float32), axis=0)
    d_second = jnp.einsum("tf,df->td", d_pre, up_back, preferred_element_type=jnp.float32)
    gain_two_grad, shift_two_grad, dx_second = norm_back(
        d_second, centered_two, inv_two, gain_two_back
    )
    mlp_shards = (
        lax.psum_scatter(up_grad, ("dp", "ctx"), scatter_dimension=0, tiled=True),
        lax.psum_scatter(up_bias_grad, ("dp", "ctx"), scatter_dimension=0, tiled=True),
        lax.psum_scatter(down_grad, ("dp", "ctx"), scatter_dimension=0, tiled=True),
        lax.psum_scatter(bias_total, ("dp", "ctx"), scatter_dimension=0, tiled=True),
        lax.psum_scatter(gain_two_grad, ("dp", "ctx"), scatter_dimension=0, tiled=True),
        lax.psum_scatter(shift_two_grad, ("dp", "ctx"), scatter_dimension=0, tiled=True),
    )
    out_grad = jnp.einsum("td,te->de", head_out, grad_out, preferred_element_type=jnp.float32)
    d_heads = jnp.einsum("te,de->td", grad_out, out_back, preferred_element_type=jnp.float32)
    d_heads = d_heads.astype(jnp.bfloat16).reshape(tok_rows, HEADS, HEAD_DIM)
    key_back, value_back = (
        lax.all_gather(key_local, "ctx", axis=0, tiled=True),
        lax.all_gather(value_local, "ctx", axis=0, tiled=True),
    )
    scores_again = (
        jnp.einsum("qhd,khd->hqk", queries, key_back, preferred_element_type=jnp.float32)
        * score_scale
    )
    attention_again = jnp.where(allowed, jnp.exp(scores_again - log_total), 0.0)
    probs_low = attention_again.astype(jnp.bfloat16)
    value_grad_all = jnp.einsum(
        "hqk,qhd->khd", probs_low, d_heads, preferred_element_type=jnp.float32
    )
    d_probs = jnp.einsum("qhd,khd->hqk", d_heads, value_back, preferred_element_type=jnp.float32)
    delta = jnp.sum(attention_again * d_probs, axis=-1, keepdims=True)
    d_scores = (attention_again * (d_probs - delta)).astype(jnp.bfloat16)
    query_grad = (
        jnp.einsum("hqk,khd->qhd", d_scores, key_back, preferred_element_type=jnp.float32)
        * score_scale
    )
    key_grad_all = (
        jnp.einsum("hqk,qhd->khd", d_scores, queries, preferred_element_type=jnp.float32)
        * score_scale
    )
    key_grad, value_grad = (
        lax.psum_scatter(key_grad_all, "ctx", scatter_dimension=0, tiled=True),
        lax.psum_scatter(value_grad_all, "ctx", scatter_dimension=0, tiled=True),
    )
    d_joint = jnp.concatenate(
        [
            rotate_back(query_grad, cosine_tab, sine_tab).reshape(tok_rows, D),
            rotate_back(key_grad, cosine_tab, sine_tab).reshape(tok_rows, D),
            value_grad.reshape(tok_rows, D),
        ],
        axis=1,
    ).astype(jnp.bfloat16)
    qkv_grad = jnp.einsum("td,te->de", normed_first, d_joint, preferred_element_type=jnp.float32)
    qkv_bias_grad = jnp.sum(d_joint.astype(jnp.float32), axis=0)
    d_first = jnp.einsum("te,de->td", d_joint, qkv_back, preferred_element_type=jnp.float32)
    gain_one_grad, shift_one_grad, dx_first = norm_back(
        d_first, centered_one, inv_one, gain_one_back
    )
    attn_shards = (
        lax.psum_scatter(qkv_grad, ("dp", "ctx"), scatter_dimension=0, tiled=True),
        lax.psum_scatter(qkv_bias_grad, ("dp", "ctx"), scatter_dimension=0, tiled=True),
        lax.psum_scatter(out_grad, ("dp", "ctx"), scatter_dimension=0, tiled=True),
        lax.psum_scatter(bias_total, ("dp", "ctx"), scatter_dimension=0, tiled=True),
        lax.psum_scatter(gain_one_grad, ("dp", "ctx"), scatter_dimension=0, tiled=True),
        lax.psum_scatter(shift_one_grad, ("dp", "ctx"), scatter_dimension=0, tiled=True),
    )
    input_grad = (grad_out_f + dx_first + dx_second).astype(jnp.bfloat16)
    return (
        output,
        input_grad,
        attn_shards[0],
        attn_shards[1],
        attn_shards[2],
        attn_shards[3],
        mlp_shards[0],
        mlp_shards[1],
        mlp_shards[2],
        mlp_shards[3],
        attn_shards[4],
        attn_shards[5],
        mlp_shards[4],
        mlp_shards[5],
    )


def solution(mesh):
    return jax.shard_map(
        local,
        mesh=mesh,
        in_specs=(
            P(("dp", "ctx"), None),
            P("dp"),
            P(("dp", "ctx"), None),
            P(("dp", "ctx"), None),
            P(("dp", "ctx")),
            P(("dp", "ctx"), None),
            P(("dp", "ctx")),
            P(("dp", "ctx"), None),
            P(("dp", "ctx")),
            P(("dp", "ctx"), None),
            P(("dp", "ctx")),
            P(("dp", "ctx")),
            P(("dp", "ctx")),
            P(("dp", "ctx")),
            P(("dp", "ctx")),
        ),
        out_specs=(
            P(("dp", "ctx"), None),
            P(("dp", "ctx"), None),
            P(("dp", "ctx"), None),
            P(("dp", "ctx")),
            P(("dp", "ctx"), None),
            P(("dp", "ctx")),
            P(("dp", "ctx"), None),
            P(("dp", "ctx")),
            P(("dp", "ctx"), None),
            P(("dp", "ctx")),
            P(("dp", "ctx")),
            P(("dp", "ctx")),
            P(("dp", "ctx")),
            P(("dp", "ctx")),
        ),
        check_vma=False,
    )
```

profile of v0, /device:TPU:16, one launch (start us, length us, event | category | flops | bytes accessed | tf_op | source)
XLA Modules:
  0.0 3016.9 jit_solution(2042068466536097112)
XLA Ops:
  14.6 42.3 %all-reduce.15 = (bf16[6144]{0:T(1024)(128)(2,1)S(1)}, bf16[2048]{0:T(1024)(128)(2,1)S(1)}, bf16[2048]{0:T(1024)(128)(2,1)S(1)}, bf16[2048]{0:T(1024)(128)(2,1)}...) all-reduce(bf16[6144]{0:T(1024)(128)(2,1)S(1)} %dynamic-update-slic, ...), channel_id=1, replica_groups=mesh['dp'=8,'ctx'=4] {'dp','ctx'}, use_global_device_ids=true, to_apply=%add.2 | all-reduce | flops 18432 | bytes 73728
  59.8 107.4 %all-gather.8.cloned.1.call-done = bf16[2048,6144]{1,0:T(8,128)(2,1)} async-done(((bf16[64,6144]{1,0:T(8,128)(2,1)}), bf16[2048,6144]{1,0:T(8,128)(2,1)}) %all-gather.8.cloned.1.call-update) | async-done | bytes 25165840 | tf_op jit(solution)/shard_map/all_gather | solution.py:93
  167.2 10.3 convolution_add_fusion.1
  185.6 60.5 %all-gather.14.cloned.1.call-done = bf16[2048,2048]{1,0:T(8,128)(2,1)} async-done(((bf16[64,2048]{1,0:T(8,128)(2,1)}), bf16[2048,2048]{1,0:T(8,128)(2,1)}) %all-gather.14.cloned.1.call-update) | async-done | bytes 8388624 | tf_op jit(solution)/shard_map/all_gather | solution.py:95
  246.1 6.5 convolution_convert_fusion
  253.3 16.7 all-gather.12.cloned.1.call-done
  270.0 2.7 select_reduce_fusion
  274.5 20.3 all-gather.10.cloned.1.call-done
  294.8 2.5 multiply_reduce_fusion
  298.5 3.0 multiply_bitcast_fusion
  302.1 3.9 convolution_bitcast_fusion
  308.8 31.0 %all-gather = bf16[32,1,256]{2,1,0:T(2,128)(2,1)S(1)} all-gather(bf16[1,1,256]{2,1,0:T(2,128)(2,1)S(1)} %reshape.220), channel_id=1, replica_groups=mesh['dp'=8,'ctx'=4] {'dp','ctx'}, dimensions={0}, use_global_device_ids=true | all-gather | bytes 16896 | tf_op jit(solution)/shard_map/all_gather | solution.py:98
  347.8 2.3 add_convert_fusion.1
  352.9 40.5 %reduce-scatter.9.cloned.1.call-done = f32[128,8,256]{0,2,1:T(8,128)} async-done(((f32[512,8,256]{0,2,1:T(8,128)}), f32[128,8,256]{0,2,1:T(8,128)}) %reduce-scatter.9.cloned.1.call-update) | async-done | bytes 1048592 | tf_op jit(solution)/shard_map/reduce_scatter | solution.py:249
  395.8 194.4 %all-gather.16.cloned.1.call-done = bf16[2048,8192]{1,0:T(8,128)(2,1)} async-done(((bf16[64,8192]{1,0:T(8,128)(2,1)}), bf16[2048,8192]{1,0:T(8,128)(2,1)}) %all-gather.16.cloned.1.call-update) | async-done | bytes 33554448 | tf_op jit(solution)/shard_map/all_gather | solution.py:97
  590.2 17.4 convolution_add_fusion
  607.6 178.4 %all-gather.18.cloned.1.call-done = bf16[8192,2048]{1,0:T(8,128)(2,1)} async-done(((bf16[256,2048]{1,0:T(8,128)(2,1)}), bf16[8192,2048]{1,0:T(8,128)(2,1)}) %all-gather.18.cloned.1.call-update) | async-done | bytes 33554448 | tf_op jit(solution)/shard_map/all_gather | solution.py:99
  786.0 17.9 convert_reduce_fusion
  804.0 16.9 fusion.77
  820.8 15.2 fusion.45
  836.1 4.0 convert_reduce_fusion.3
  840.2 9.4 fusion.71
  849.7 21.1 fusion.66
  871.8 28.8 fusion.70
  900.7 23.6 fusion.63
  925.4 4.8 fusion.17
  930.2 17.9 fusion.18
  948.1 16.3 all-reduce.18.cloned.1.call-done
  972.8 175.2 %reduce-scatter.13.cloned.1.call-done = f32[64,2048]{1,0:T(8,128)} async-done(((f32[2048,2048]{1,0:T(8,128)}), f32[64,2048]{1,0:T(8,128)}) %reduce-scatter.13.cloned.1.call-update) | async-done | bytes 524304 | tf_op jit(solution)/shard_map/reduce_scatter | solution.py:268
  1148.0 442.3 %reduce-scatter.11.cloned.1.call-done = f32[64,6144]{1,0:T(8,128)} async-done(((f32[2048,6144]{1,0:T(8,128)}), f32[64,6144]{1,0:T(8,128)}) %reduce-scatter.11.cloned.1.call-update) | async-done | bytes 1572880 | tf_op jit(solution)/shard_map/reduce_scatter | solution.py:266
  1590.3 705.8 %reduce-scatter.17.cloned.1.call-done = f32[256,2048]{1,0:T(8,128)} async-done(((f32[8192,2048]{1,0:T(8,128)}), f32[256,2048]{1,0:T(8,128)}) %reduce-scatter.17.cloned.1.call-update) | async-done | bytes 2097168 | tf_op jit(solution)/shard_map/reduce_scatter | solution.py:215
  2296.2 713.3 %reduce-scatter.15.cloned.1.call-done = f32[64,8192]{1,0:T(8,128)} async-done(((f32[2048,8192]{1,0:T(8,128)}), f32[64,8192]{1,0:T(8,128)}) %reduce-scatter.15.cloned.1.call-update) | async-done | bytes 2097168 | tf_op jit(solution)/shard_map/reduce_scatter | solution.py:213
  (177 shorter events, 48.7 us)
Async XLA Ops:
  7.2 160.0 %all-gather.8.cloned.1.call-start = ((), (), s32[]{:S(2)}) async-start(), calls=%async_computation.6 | async-start | bytes 25952256 | tf_op jit(solution)/shard_map/all_gather | solution.py:93
  7.9 238.2 %all-gather.14.cloned.1.call-start = ((), (), s32[]{:S(2)}) async-start(), calls=%async_computation.9 | async-start | bytes 8650752 | tf_op jit(solution)/shard_map/all_gather | solution.py:95
  8.7 261.3 %all-gather.12.cloned.1.call-start = ((), (), s32[]{:S(2)}) async-start(), calls=%async_computation.8 | async-start | bytes 2621440 | tf_op jit(solution)/shard_map/all_gather | solution.py:142
  58.1 119.3 %copy-start.21 = (f32[128]{0:T(128)}, f32[128]{0:T(128)S(1)}, u32[]{:S(2)}) copy-start(f32[128]{0:T(128)S(1)} %broadcast_multiply_fusion.4) | copy-start | bytes 1540
  59.5 118.0 %copy-start.23 = (f32[128]{0:T(128)}, f32[128]{0:T(128)S(1)}, u32[]{:S(2)}) copy-start(f32[128]{0:T(128)S(1)} %add_rsqrt_fusion) | copy-start | bytes 1540
  59.8 119.3 %copy-start.16 = (f32[128,32]{1,0:T(8,128)}, f32[128,32]{1,0:T(8,128)S(1)}, u32[]{:S(2)}) copy-start(f32[128,32]{1,0:T(8,128)S(1)} %get-tuple-element.61) | copy-start | bytes 49156
  181.5 113.3 %all-gather.10.cloned.1.call-start = ((), (), s32[]{:S(2)}) async-start(), calls=%async_computation.7 | async-start | bytes 2621440 | tf_op jit(solution)/shard_map/all_gather | solution.py:143
  184.5 161.8 %reduce-scatter.7.cloned.1.call-start = ((), (), s32[]{:S(2)}) async-start(), calls=%async_computation.12 | async-start | bytes 5242880 | tf_op jit(solution)/shard_map/reduce_scatter | solution.py:248
  185.4 67.2 %copy-start.31 = (pred[128]{0:T(512)(128)(4,1)}, pred[128]{0:T(512)(128)(4,1)S(1)}, u32[]{:S(2)}) copy-start(pred[128]{0:T(512)(128)(4,1)S(1)} %broadcast_compare_fusion) | copy-start | bytes 388
  185.6 67.3 %copy-start.4 = (f32[16,8,8,256]{3,2,1,0:T(8,128)S(1)}, f32[16,8,8,256]{3,2,1,0:T(8,128)}, u32[]{:S(2)}) copy-start(f32[16,8,8,256]{3,2,1,0:T(8,128)} %copy-done.3) | copy-start | bytes 3145732
  252.9 41.9 %copy-start.10 = (bf16[128,2048]{0,1:T(8,128)(2,1)}, bf16[128,2048]{0,1:T(8,128)(2,1)S(1)}, u32[]{:S(2)}) copy-start(bf16[128,2048]{0,1:T(8,128)(2,1)S(1)} %copy.81) | copy-start | bytes 1572868
  253.3 44.1 %copy-start.7 = (bf16[128,8,192]{2,0,1:T(8,128)(2,1)}, bf16[128,8,192]{2,0,1:T(8,128)(2,1)S(1)}, u32[]{:S(2)}) copy-start(bf16[128,8,192]{2,0,1:T(8,128)(2,1)S(1)} %copy.103) | copy-start | bytes 1179652
  301.5 91.9 %reduce-scatter.9.cloned.1.call-start = ((), (), s32[]{:S(2)}) async-start(), calls=%async_computation.13 | async-start | bytes 5242880 | tf_op jit(solution)/shard_map/reduce_scatter | solution.py:249
  306.0 38.5 %copy-start.28 = (f32[8,128]{1,0:T(8,128)S(1)}, f32[8,128]{1,0:T(8,128)}, u32[]{:S(2)}) copy-start(f32[8,128]{1,0:T(8,128)} %copy-done.27) | copy-start | bytes 12292
  306.0 38.5 %copy-start.30 = (f32[8,128]{1,0:T(8,128)S(1)}, f32[8,128]{1,0:T(8,128)}, u32[]{:S(2)}) copy-start(f32[8,128]{1,0:T(8,128)} %copy-done.29) | copy-start | bytes 12292
  306.1 284.1 %all-gather.16.cloned.1.call-start = ((), (), s32[]{:S(2)}) async-start(), calls=%async_computation.10 | async-start | bytes 34603008 | tf_op jit(solution)/shard_map/all_gather | solution.py:97
  306.8 479.2 %all-gather.18.cloned.1.call-start = ((), (), s32[]{:S(2)}) async-start(), calls=%async_computation.11 | async-start | bytes 34603008 | tf_op jit(solution)/shard_map/all_gather | solution.py:99
  307.6 656.8 %all-reduce.18.cloned.1.call-start = ((), (), s32[]{:S(2)}) async-start(), calls=%async_computation.18 | async-start | bytes 196608
  350.1 240.0 %copy-start = (bf16[128,2048]{1,0:T(8,128)(2,1)S(1)}, bf16[128,2048]{1,0:T(8,128)(2,1)}, u32[]{:S(2)}) copy-start(bf16[128,2048]{1,0:T(8,128)(2,1)} %param.15) | copy-start | bytes 1572868
  350.1 240.0 %copy-start.18 = (f32[2048]{0:T(1024)S(1)}, f32[2048]{0:T(1024)}, u32[]{:S(2)}) copy-start(f32[2048]{0:T(1024)} %convert_element_type.103) | copy-start | bytes 24580
  350.1 240.0 %copy-start.19 = (f32[2048]{0:T(1024)S(1)}, f32[2048]{0:T(1024)}, u32[]{:S(2)}) copy-start(f32[2048]{0:T(1024)} %convert_element_type.104) | copy-start | bytes 24580
  350.1 240.0 %copy-start.20 = (f32[32,1,256]{2,1,0:T(1,128)S(1)}, f32[32,1,256]{2,1,0:T(1,128)}, u32[]{:S(2)}) copy-start(f32[32,1,256]{2,1,0:T(1,128)} %convert_element_type.118) | copy-start | bytes 98308
  350.1 240.0 %copy-start.22 = (f32[128]{0:T(128)S(1)}, f32[128]{0:T(128)}, u32[]{:S(2)}) copy-start(f32[128]{0:T(128)} %copy-done.21) | copy-start | bytes 1540
  350.2 240.0 %copy-start.24 = (f32[128]{0:T(128)S(1)}, f32[128]{0:T(128)}, u32[]{:S(2)}) copy-start(f32[128]{0:T(128)} %copy-done.23) | copy-start | bytes 1540
  350.9 256.7 %copy-start.5 = (bf16[128,8,256]{0,2,1:T(8,128)(2,1)}, bf16[128,8,256]{0,2,1:T(8,128)(2,1)S(1)}, u32[]{:S(2)}) copy-start(bf16[128,8,256]{0,2,1:T(8,128)(2,1)S(1)} %copy.73) | copy-start | bytes 1572868
  352.8 254.8 %copy-start.6 = (bf16[128,8,256]{0,2,1:T(8,128)(2,1)}, bf16[128,8,256]{0,2,1:T(8,128)(2,1)S(1)}, u32[]{:S(2)}) copy-start(bf16[128,8,256]{0,2,1:T(8,128)(2,1)S(1)} %copy.70) | copy-start | bytes 1572868
  590.2 195.8 %copy-start.32 = (pred[128]{0:T(512)(128)(4,1)S(1)}, pred[128]{0:T(512)(128)(4,1)}, u32[]{:S(2)}) copy-start(pred[128]{0:T(512)(128)(4,1)} %copy-done.31) | copy-start | bytes 388
  840.1 307.9 %reduce-scatter.13.cloned.1.call-start = ((), (), s32[]{:S(2)}) async-start(), calls=%async_computation.15 | async-start | bytes 17301504 | tf_op jit(solution)/shard_map/reduce_scatter | solution.py:268
  849.6 740.7 %reduce-scatter.11.cloned.1.call-start = ((), (), s32[]{:S(2)}) async-start(), calls=%async_computation.14 | async-start | bytes 51904512 | tf_op jit(solution)/shard_map/reduce_scatter | solution.py:266
  870.8 1425.3 %reduce-scatter.17.cloned.1.call-start = ((), (), s32[]{:S(2)}) async-start(), calls=%async_computation.17 | async-start | bytes 69206016 | tf_op jit(solution)/shard_map/reduce_scatter | solution.py:215
  900.6 2108.8 %reduce-scatter.15.cloned.1.call-start = ((), (), s32[]{:S(2)}) async-start(), calls=%async_computation.16 | async-start | bytes 69206016 | tf_op jit(solution)/shard_map/reduce_scatter | solution.py:213
  965.1 2044.9 %copy-start.38 = (f32[64]{0:T(128)}, f32[64]{0:T(128)S(1)}, u32[]{:S(2)}) copy-start(f32[64]{0:T(128)S(1)} %dynamic-slice.1) | copy-start | bytes 772
  (20 other events, 70.4 us)
Sparse Core Ops, SparseCore 0:
  10.9 156.2 all-gather.7
  170.0 76.0 all-gather.13
  248.3 21.6 all-gather.11
  272.0 22.8 all-gather.9
  301.6 44.6 reduce-scatter.6
  348.8 44.5 reduce-scatter.8
  396.3 193.8 all-gather.15
  593.0 192.9 all-gather.17
  840.2 124.0 all-reduce.17
  967.2 180.7 reduce-scatter.12
  1156.1 434.1 reduce-scatter.10
  1593.2 702.8 reduce-scatter.16
  2299.2 710.2 reduce-scatter.14
where the time goes:
time: 3030 us; the launch traced here: 3020 us
  waiting for transfers between devices  2670 us (88%)
  matrix products  206 us (7%)
  blocking collectives  73.2 us (2%)
    reduce_scatter x1, waiting for transfers between devices, local(): lax.psum_scatter(up_grad, ('dp', 'ctx'), scatter_dimension=0, tiled=True)  713 us
    reduce_scatter x1, waiting for transfers between devices, local(): lax.psum_scatter(down_grad, ('dp', 'ctx'), scatter_dimension=0, tiled=True)  706 us
    reduce_scatter x1, waiting for transfers between devices, local(): lax.psum_scatter(qkv_grad, ('dp', 'ctx'), scatter_dimension=0, tiled=True)  442 us
    all_gather x1, waiting for transfers between devices, local(): lax.all_gather(up_weight, ('dp', 'ctx'), axis=0, tiled=True)  194 us
    all_gather x1, waiting for transfers between devices, local(): lax.all_gather(down_weight, ('dp', 'ctx'), axis=0, tiled=True)  178 us
    reduce_scatter x1, waiting for transfers between devices, local(): lax.psum_scatter(out_grad, ('dp', 'ctx'), scatter_dimension=0, tiled=True)  175 us
    all_gather x1, waiting for transfers between devices, local(): lax.all_gather(qkv_weight, ('dp', 'ctx'), axis=0, tiled=True)  107 us
  transfers between devices with their start and end apart: 13, of which 12 were waited for; matrix products, arithmetic and copies ran while one was open for 6% of the time, Pallas kernels for 0%

commit v1 on v0

v1 whole, which is shorter than its diff:
```python
import functools
import math

import jax
import jax.numpy as jnp
from jax import lax
from jax.experimental import pallas as pl
from jax.experimental.pallas import tpu as pltpu
from jax.sharding import PartitionSpec as P

HEADS = 8
HEAD_DIM = 256
ROT = 64
EPS = 1e-05
MESH = pl.DeviceIdType.MESH
BF = jnp.bfloat16
F32 = jnp.float32
VEC = 1024


class Plan:
    def __init__(self, dp, ctx, tok, d, ff):
        self.C = ctx
        self.X = ctx // 2
        self.A = HEADS // self.X
        self.S = dp // self.A
        self.n = dp * ctx
        self.tok = tok
        self.d = d
        self.ff = ff
        self.r = d // self.n
        self.R = ff // self.n
        self.ffl = self.S * self.R
        self.W = max(self.R, 128)
        self.P = self.W // self.R
        self.hc = 3 * HEAD_DIM
        self.m = HEAD_DIM // self.r // 2
        self.rows = self.A * self.C * tok


def remote(src, dst, send, recv, dev):
    return pltpu.make_async_remote_copy(
        src_ref=src, dst_ref=dst, send_sem=send, recv_sem=recv, device_id=dev, device_id_type=MESH
    )


def drain(ref, sem):
    pltpu.make_async_copy(ref, ref, sem).wait()


def unit_run(p, aa, cc, j):
    if p.P == 1:
        return p.R * ((aa * p.S + j) * p.C + cc)
    return p.R * ((aa * p.S + 2 * j + lax.rem(cc, 2)) * p.C + lax.div(cc, 2) * 2)


def unit_home(p, b, xh, core):
    if p.P == 1:
        return xh * 2 + core, b * p.R
    return xh * 2 + lax.rem(b, 2), (lax.div(b, 2) * 2 + core) * p.R


def place(p):
    dp = lax.axis_index("dp")
    c = lax.axis_index("ctx")
    a = lax.div(dp, p.S)
    b = lax.rem(dp, p.S)
    xh = lax.div(c, 2)
    core = lax.rem(c, 2)
    return dp, c, a, b, xh, core


def greet_all(p, me):
    barrier = pltpu.get_barrier_semaphore()

    def greet(k, carry):
        other = lax.rem(me + k, p.n)
        pl.semaphore_signal(
            barrier,
            inc=1,
            device_id=(lax.div(other, p.C), lax.rem(other, p.C)),
            device_id_type=MESH,
        )
        return carry

    lax.fori_loop(1, p.n, greet, 0)
    pl.semaphore_wait(barrier, p.n - 1)


def spread_kernel(
    p,
    x,
    g,
    qkv,
    outw,
    up,
    down,
    small,
    xa,
    ga,
    qw,
    dw,
    uw,
    sm,
    loc,
    s_sm,
    r_sm,
    s_up,
    r_up,
    s_upb,
    r_upb,
    s_q,
    r_q,
    s_qb,
    r_qb,
    s_qc,
    r_qc,
    s_o,
    r_o,
    s_oc,
    r_oc,
    s_d,
    r_d,
    s_r,
    r_r,
    s_l,
    r_l,
    s_x,
    r_x,
    s_s,
    r_s,
):
    A, S, C, r, R = p.A, p.S, p.C, p.r, p.R
    dp, c, a, b, xh, core = place(p)
    me = dp * C + c
    t = a * C + c
    head = a * p.X + xh
    sib = (dp, xh * 2 + 1 - core)
    xnb = (dp, (1 - xh) * 2 + core)
    right = (dp + S, c)
    left = (dp - S, c)
    greet_all(p, me)

    own_small = pltpu.make_async_copy(small, sm.at[me], loc.at[0])
    own_small.start()
    own_x = pltpu.make_async_copy(x, xa.at[a, c], loc.at[1])
    own_x.start()
    own_g = pltpu.make_async_copy(g, ga.at[a, c], loc.at[2])
    own_g.start()

    def up_piece(aa, cc, j):
        col = pl.multiple_of(unit_run(p, aa, cc, j), 128)
        return up.at[:, pl.ds(col, p.W)], uw.at[a, b, c, :, pl.ds(j * p.W, p.W)]

    def up_send(k, carry):
        tt = lax.rem(t + k, A * C)
        aa, cc = lax.div(tt, C), lax.rem(tt, C)
        for j in range(p.ffl // p.W):
            src, dst = up_piece(aa, cc, j)
            remote(src, dst, s_up, r_up, (aa * S + b, cc)).start()
        return carry

    lax.fori_loop(1, A * C, up_send, 0)
    for j in range(p.ffl // p.W):
        src, dst = up_piece(a, c, j)
        pltpu.make_async_copy(src, dst, r_up).start()

    def q_piece(hh, j):
        col = pl.multiple_of(j * p.d + hh * HEAD_DIM, HEAD_DIM)
        return (
            qkv.at[:, pl.ds(col, HEAD_DIM)],
            qw.at[a, b, xh, core, :, pl.ds(j * HEAD_DIM, HEAD_DIM)],
        )

    def q_send(k, carry):
        hh = lax.rem(head + k, HEADS)
        for j in range(3):
            src, dst = q_piece(hh, j)
            dev = (lax.div(hh, p.X) * S + b, lax.rem(hh, p.X) * 2 + core)
            remote(src, dst, s_q, r_q, dev).start()
        return carry

    lax.fori_loop(1, HEADS, q_send, 0)
    for j in range(3):
        src, dst = q_piece(head, j)
        pltpu.make_async_copy(src, dst, r_q).start()

    row_head = lax.div(me * r, HEAD_DIM)
    row_part = lax.div(lax.rem(me * r, HEAD_DIM), 2 * r)
    o_dst = dw.at[pl.ds(pl.multiple_of(p.ffl + (row_part * 2 + core) * r, r), r)]

    def o_dev(bb):
        return lax.div(row_head, p.X) * S + bb, lax.rem(row_head, p.X) * 2 + core

    for bb in range(S):
        od, oc = o_dev(bb)
        here = (od == dp) & (oc == c)

        @pl.when(jnp.logical_not(here))
        def _():
            remote(outw, o_dst, s_o.at[bb], r_o, (od, oc)).start()

        @pl.when(here)
        def _():
            pltpu.make_async_copy(outw, o_dst, r_o).start()

    d_ctx, d_row = unit_home(p, b, xh, core)
    d_dst = dw.at[pl.ds(pl.multiple_of(d_row, R), R)]
    for bb in range(S):
        here = (bb == b) & (d_ctx == c)

        @pl.when(jnp.logical_not(here))
        def _():
            remote(down, d_dst, s_d.at[bb], r_d, (a * S + bb, d_ctx)).start()

        @pl.when(here)
        def _():
            pltpu.make_async_copy(down, d_dst, r_d).start()

    streams = ((x, xa), (g, ga))

    for j, (own, full) in enumerate(streams):
        slot = full.at[a, c]

        @pl.when(a < A - 1)
        def _():
            remote(own, slot, s_r.at[j, 0], r_r.at[j, 0], right).start()

        @pl.when(a > 0)
        def _():
            remote(own, slot, s_l.at[j, 0], r_l.at[j, 0], left).start()

        remote(own, slot, s_x.at[j, a], r_x.at[j, a], xnb).start()
        remote(own, slot, s_s.at[j], r_s.at[j], sib).start()

    def small_send(k, carry):
        other = lax.rem(me + k, p.n)
        dev = (lax.div(other, C), lax.rem(other, C))
        remote(small, sm.at[me], s_sm, r_sm, dev).start()
        return carry

    lax.fori_loop(1, p.n, small_send, 0)

    drain(uw.at[:, b], r_up)

    def up_cross(k, carry):
        bb = lax.rem(b + k, S)
        remote(uw.at[:, b], uw.at[:, b], s_upb, r_upb, (a * S + bb, c)).start()
        return carry

    lax.fori_loop(1, S, up_cross, 0)
    drain(qw.at[:, b, :, core], r_q)

    def q_cross(k, carry):
        bb = lax.rem(b + k, S)
        part = qw.at[:, b, :, core]
        remote(part, part, s_qb, r_qb, (a * S + bb, c)).start()
        return carry

    lax.fori_loop(1, S, q_cross, 0)
    drain(dw.at[pl.ds(p.ffl, p.m * r)], r_o)
    for k in range(p.m):
        rows = dw.at[pl.ds(pl.multiple_of(p.ffl + (2 * k + core) * r, r), r)]
        remote(rows, rows, s_oc.at[k], r_oc.at[k], sib).start()

    for s in range(A - 1):
        for j, (own, full) in enumerate(streams):

            @pl.when(a - 1 - s >= 0)
            def _():
                blk = full.at[a - 1 - s, c]
                remote(blk, blk, s_r.at[j, s], r_r.at[j, s], left).wait_recv()
                if s + 1 < A - 1:

                    @pl.when(a < A - 1)
                    def _():
                        remote(blk, blk, s_r.at[j, s + 1], r_r.at[j, s + 1], right).start()

                remote(blk, blk, s_x.at[j, a - 1 - s], r_x.at[j, a - 1 - s], xnb).start()
                remote(blk, blk, s_s.at[j], r_s.at[j], sib).start()

            @pl.when(a + 1 + s <= A - 1)
            def _():
                blk = full.at[a + 1 + s, c]
                remote(blk, blk, s_l.at[j, s], r_l.at[j, s], right).wait_recv()
                if s + 1 < A - 1:

                    @pl.when(a > 0)
                    def _():
                        remote(blk, blk, s_l.at[j, s + 1], r_l.at[j, s + 1], left).start()

                remote(blk, blk, s_x.at[j, a + 1 + s], r_x.at[j, a + 1 + s], xnb).start()
                remote(blk, blk, s_s.at[j], r_s.at[j], sib).start()

        if s == 0:
            for _ in range(S - 1):
                drain(qw.at[:, b, :, core], r_qb)
            half = qw.at[:, :, :, core]
            remote(half, half, s_qc, r_qc, sib).start()

    xc = (1 - xh) * 2 + core
    for j, (own, full) in enumerate(streams):

        def cross(k):
            blk = full.at[k, xc]
            remote(blk, blk, s_x.at[j, k], r_x.at[j, k], xnb).wait_recv()
            remote(blk, blk, s_s.at[j], r_s.at[j], sib).start()

        cross(a)
        for s in range(A - 1):

            @pl.when(a - 1 - s >= 0)
            def _():
                cross(a - 1 - s)

            @pl.when(a + 1 + s <= A - 1)
            def _():
                cross(a + 1 + s)

    other_half = qw.at[:, :, :, 1 - core]
    drain(other_half, r_qc)
    for _ in range(S - 1):
        drain(uw.at[:, b], r_upb)
    drain(dw.at[pl.ds(0, p.ffl)], r_d)
    for k in range(p.m):
        drain(dw.at[pl.ds(0, r)], r_oc.at[k])
    drain(sm.at[pl.ds(0, p.n - 1)], r_sm)
    for j, (own, full) in enumerate(streams):
        drain(full.at[:, pl.ds(0, p.X)], r_s.at[j])

    own_small.wait()
    own_x.wait()
    own_g.wait()
    drain(sm.at[pl.ds(0, p.n - 1)], s_sm)
    for _ in range(A * C - 1):
        drain(uw.at[a, b, c], s_up)
    for _ in range(HEADS - 1):
        drain(qw.at[a, b, xh, core], s_q)
    for bb in range(S):
        od, oc = o_dev(bb)

        @pl.when(jnp.logical_not((od == dp) & (oc == c)))
        def _():
            drain(outw, s_o.at[bb])

        @pl.when(jnp.logical_not((bb == b) & (d_ctx == c)))
        def _():
            drain(down, s_d.at[bb])

    for k in range(p.m):
        drain(dw.at[pl.ds(0, r)], s_oc.at[k])
    for _ in range(S - 1):
        drain(uw.at[:, b], s_upb)
        drain(qw.at[:, b, :, core], s_qb)
    drain(other_half, s_qc)
    for j, (own, full) in enumerate(streams):
        for s in range(A - 1):

            @pl.when((a < A - 1) & (a - s >= 0))
            def _():
                drain(own, s_r.at[j, s])

            @pl.when((a > 0) & (a + s <= A - 1))
            def _():
                drain(own, s_l.at[j, s])

        for k in range(A):
            drain(own, s_x.at[j, k])
        drain(full.at[:, pl.ds(0, p.X)], s_s.at[j])


def spread(p, x, g, qkv, outw, up, down, small):
    dma = pltpu.SemaphoreType.DMA
    A, S, C, r = p.A, p.S, p.C, p.r
    return pl.pallas_call(
        functools.partial(spread_kernel, p),
        out_shape=(
            jax.ShapeDtypeStruct((A, C, p.tok, p.d), BF),
            jax.ShapeDtypeStruct((A, C, p.tok, p.d), BF),
            jax.ShapeDtypeStruct((A, S, p.X, 2, r, p.hc), BF),
            jax.ShapeDtypeStruct((p.ffl + HEAD_DIM, p.d), BF),
            jax.ShapeDtypeStruct((A, S, C, r, p.ffl), BF),
            jax.ShapeDtypeStruct((p.n, 8, VEC // 8), F32),
        ),
        in_specs=[pl.BlockSpec(memory_space=pltpu.VMEM)] * 7,
        out_specs=[pl.BlockSpec(memory_space=pl.ANY)] * 6,
        scratch_shapes=[
            dma((3,)),
            dma,
            dma,
            dma,
            dma,
            dma,
            dma,
            dma,
            dma,
            dma,
            dma,
            dma,
            dma,
            dma((S,)),
            dma,
            dma((p.m,)),
            dma((p.m,)),
            dma((S,)),
            dma,
            dma((2, A - 1)),
            dma((2, A - 1)),
            dma((2, A - 1)),
            dma((2, A - 1)),
            dma((2, A)),
            dma((2, A)),
            dma((2,)),
            dma((2,)),
        ],
        compiler_params=pltpu.CompilerParams(collective_id=0, has_side_effects=True),
        name="spread",
    )(x, g, qkv, outw, up, down, small)


def add_rows(dst, parts, rows):
    step = 16

    def body(k, carry):
        at = pl.ds(pl.multiple_of(k * step, step), step)
        total = parts[0][at, :].astype(F32)
        for part in parts[1:]:
            total = total + part[at, :].astype(F32)
        dst[at, :] = total.astype(dst.dtype)
        return carry

    lax.fori_loop(0, rows // step, body, 0)


def collect_kernel(
    p,
    op,
    ep,
    qg,
    og,
    ug,
    dg,
    vec,
    o_sum,
    e_sum,
    q_out,
    o_out,
    u_out,
    d_out,
    v_all,
    mine,
    from_sib,
    from_x,
    from_l,
    from_r,
    to_x,
    line,
    q_mine,
    q_sib,
    q_group,
    q_fin,
    o_mine,
    o_sib,
    o_parts,
    u_mine,
    u_parts,
    u_fin,
    d_mine,
    d_parts,
    loc,
    s_v,
    r_v,
    s_s,
    r_s,
    s_x,
    r_x,
    s_r,
    r_r,
    s_l,
    r_l,
    s_q,
    r_q,
    s_qb,
    r_qb,
    s_qa,
    r_qa,
    s_o,
    r_o,
    s_oa,
    r_oa,
    s_u,
    r_u,
    s_ua,
    r_ua,
    s_d,
    r_d,
):
    A, S, C, X, r, R = p.A, p.S, p.C, p.X, p.r, p.R
    dp, c, a, b, xh, core = place(p)
    me = dp * C + c
    t = a * C + c
    head = a * X + xh
    sib = (dp, xh * 2 + 1 - core)
    xnb = (dp, (1 - xh) * 2 + core)
    right = (dp + S, c)
    left = (dp - S, c)
    far = 1 - xh
    greet_all(p, me)

    parts = (op, ep)
    remote(qg.at[:, :, :, 1 - core], q_sib, s_q, r_q, sib).start()
    for j in range(2):
        for k in range(2):
            side = far if k == 0 else xh
            remote(
                parts[j].at[:, side, 1 - core],
                from_sib.at[j, :, side],
                s_s.at[j, k],
                r_s.at[j, k],
                sib,
            ).start()
            pltpu.make_async_copy(
                parts[j].at[:, side, core], mine.at[j, :, side], loc.at[2 * j + k]
            ).start()
    remote(og.at[:, 1 - core], o_sib, s_o, r_o, sib).start()
    own_q = pltpu.make_async_copy(qg.at[:, :, :, core], q_mine, loc.at[4])
    own_q.start()
    own_o = pltpu.make_async_copy(og.at[:, core], o_mine, loc.at[5])
    own_o.start()
    own_u = pltpu.make_async_copy(ug.at[:, b], u_mine, loc.at[6])
    own_u.start()
    own_v = pltpu.make_async_copy(vec, v_all.at[me], loc.at[7])
    own_v.start()

    def u_send(k, carry):
        bb = lax.rem(b + k, S)
        remote(ug.at[:, bb], u_parts.at[b], s_u, r_u, (a * S + bb, c)).start()
        return carry

    lax.fori_loop(1, S, u_send, 0)

    d_ctx, _ = unit_home(p, b, xh, core)
    for j in range(S):
        if p.P == 1:
            own_b, own_c = j, c
        else:
            own_b, own_c = 2 * (j // 2) + core, xh * 2 + j % 2
        src = dg.at[pl.ds(j * R, R)]
        here = (own_b == b) & (own_c == c)

        @pl.when(jnp.logical_not(here))
        def _():
            remote(src, d_parts.at[b], s_d.at[j], r_d, (a * S + own_b, own_c)).start()

        @pl.when(here)
        def _():
            pltpu.make_async_copy(src, d_parts.at[b], r_d).start()

    def v_send(k, carry):
        other = lax.rem(me + k, p.n)
        dev = (lax.div(other, C), lax.rem(other, C))
        remote(vec, v_all.at[me], s_v, r_v, dev).start()
        return carry

    lax.fori_loop(1, p.n, v_send, 0)

    def far_first(step):
        for s in range(A - 1, 0, -1):

            @pl.when(a + s <= A - 1)
            def _():
                step(a + s)

            @pl.when(a - s >= 0)
            def _():
                step(a - s)

        step(a)

    def halves(j):
        drain(mine.at[j, :, far], loc.at[2 * j])
        drain(from_sib.at[j, :, far], r_s.at[j, 0])

        def send_x(k):
            add_rows(to_x.at[j, k], (mine.at[j, k, far], from_sib.at[j, k, far]), p.tok)
            remote(to_x.at[j, k], from_x.at[j, k], s_x.at[j, k], r_x.at[j, k], xnb).start()

        far_first(send_x)

    halves(0)
    own_q.wait()
    drain(q_sib, r_q)
    for aa in range(A):
        for bb in range(S):
            for xx in range(X):
                add_rows(
                    q_mine.at[aa, bb, xx], (q_mine.at[aa, bb, xx], q_sib.at[aa, bb, xx]), r
                )

    def q_cross(k, carry):
        bb = lax.rem(b + k, S)
        remote(q_mine.at[:, bb], q_group.at[b], s_qb, r_qb, (a * S + bb, c)).start()
        return carry

    lax.fori_loop(1, S, q_cross, 0)
    own_o.wait()
    drain(o_sib, r_o)
    for k in range(p.m):
        add_rows(o_mine.at[k], (o_mine.at[k], o_sib.at[k]), r)
        owner = lax.div(head * HEAD_DIM, r) + 2 * k + core
        od, oc = lax.div(owner, C), lax.rem(owner, C)
        here = owner == me

        @pl.when(jnp.logical_not(here))
        def _():
            remote(o_mine.at[k], o_parts.at[b], s_oa.at[k], r_oa, (od, oc)).start()

        @pl.when(here)
        def _():
            pltpu.make_async_copy(o_mine.at[k], o_parts.at[b], r_oa).start()

    halves(1)

    own_u.wait()
    for _ in range(S - 1):
        drain(u_mine, r_u)
    for aa in range(A):
        for cc in range(C):
            if S == 2:
                add_rows(
                    u_fin.at[aa, cc], (u_mine.at[aa, cc], u_parts.at[1 - b, aa, cc]), r
                )
            else:
                for k in range(1, S):
                    add_rows(
                        u_mine.at[aa, cc],
                        (u_mine.at[aa, cc], u_parts.at[lax.rem(b + k, S), aa, cc]),
                        r,
                    )
                add_rows(u_fin.at[aa, cc], (u_mine.at[aa, cc],), r)

    def u_piece(tt, j):
        col = pl.multiple_of(unit_run(p, a, c, j), 128)
        aa, cc = lax.div(tt, C), lax.rem(tt, C)
        return u_fin.at[aa, cc, :, pl.ds(j * p.W, p.W)], u_out.at[:, pl.ds(col, p.W)]

    def u_back(k, carry):
        tt = lax.rem(t + k, A * C)
        for j in range(p.ffl // p.W):
            src, dst = u_piece(tt, j)
            remote(src, dst, s_ua, r_ua, (lax.div(tt, C) * S + b, lax.rem(tt, C))).start()
        return carry

    lax.fori_loop(1, A * C, u_back, 0)
    for j in range(p.ffl // p.W):
        src, dst = u_piece(t, j)
        pltpu.make_async_copy(src, dst, r_ua).start()

    for _ in range(S - 1):
        drain(q_group.at[0], r_qb)
    for aa in range(A):
        for xx in range(X):
            if S == 2:
                add_rows(
                    q_fin.at[aa, xx], (q_mine.at[aa, b, xx], q_group.at[1 - b, aa, xx]), r
                )
            else:
                for k in range(1, S):
                    add_rows(
                        q_mine.at[aa, b, xx],
                        (q_mine.at[aa, b, xx], q_group.at[lax.rem(b + k, S), aa, xx]),
                        r,
                    )
                add_rows(q_fin.at[aa, xx], (q_mine.at[aa, b, xx],), r)

    def q_piece(hh, j):
        col = pl.multiple_of(j * p.d + head * HEAD_DIM, HEAD_DIM)
        return (
            q_fin.at[lax.div(hh, X), lax.rem(hh, X), :, pl.ds(j * HEAD_DIM, HEAD_DIM)],
            q_out.at[:, pl.ds(col, HEAD_DIM)],
        )

    def q_back(k, carry):
        hh = lax.rem(head + k, HEADS)
        dev = (lax.div(hh, X) * S + b, lax.rem(hh, X) * 2 + core)
        for j in range(3):
            src, dst = q_piece(hh, j)
            remote(src, dst, s_qa, r_qa, dev).start()
        return carry

    lax.fori_loop(1, HEADS, q_back, 0)
    for j in range(3):
        src, dst = q_piece(head, j)
        pltpu.make_async_copy(src, dst, r_qa).start()

    def column(j, total):
        drain(mine.at[j, :, xh], loc.at[2 * j + 1])
        drain(from_sib.at[j, :, xh], r_s.at[j, 1])

        def hop(k, first, came, s_, r_, dev, whence):
            got = (mine.at[j, k, xh], from_sib.at[j, k, xh], from_x.at[j, k])

            @pl.when(first)
            def _():
                add_rows(line.at[j, k], got, p.tok)

            @pl.when(jnp.logical_not(first))
            def _():
                remote(came.at[j, k], came.at[j, k], s_.at[j, k], r_.at[j, k], whence).wait_recv()
                add_rows(line.at[j, k], got + (came.at[j, k],), p.tok)

            remote(line.at[j, k], came.at[j, k], s_.at[j, k], r_.at[j, k], dev).start()

        for s in range(A - 1, 0, -1):

            @pl.when(a + s <= A - 1)
            def _():
                k = a + s
                remote(to_x.at[j, k], from_x.at[j, k], s_x.at[j, k], r_x.at[j, k], xnb).wait_recv()
                hop(k, a == 0, from_l, s_r, r_r, right, left)

            @pl.when(a - s >= 0)
            def _():
                k = a - s
                remote(to_x.at[j, k], from_x.at[j, k], s_x.at[j, k], r_x.at[j, k], xnb).wait_recv()
                hop(k, a == A - 1, from_r, s_l, r_l, left, right)

        remote(to_x.at[j, a], from_x.at[j, a], s_x.at[j, a], r_x.at[j, a], xnb).wait_recv()
        add_rows(
            line.at[j, a], (mine.at[j, a, xh], from_sib.at[j, a, xh], from_x.at[j, a]), p.tok
        )

    column(0, o_sum)
    column(1, e_sum)
    for j, total in enumerate((o_sum, e_sum)):

        @pl.when(a == 0)
        def _():
            remote(from_r.at[j, a], from_r.at[j, a], s_l.at[j, a], r_l.at[j, a], right).wait_recv()
            add_rows(total, (line.at[j, a], from_r.at[j, a]), p.tok)

        @pl.when(a == A - 1)
        def _():
            remote(from_l.at[j, a], from_l.at[j, a], s_r.at[j, a], r_r.at[j, a], left).wait_recv()
            add_rows(total, (line.at[j, a], from_l.at[j, a]), p.tok)

        @pl.when((a > 0) & (a < A - 1))
        def _():
            remote(from_r.at[j, a], from_r.at[j, a], s_l.at[j, a], r_l.at[j, a], right).wait_recv()
            remote(from_l.at[j, a], from_l.at[j, a], s_r.at[j, a], r_r.at[j, a], left).wait_recv()
            add_rows(total, (line.at[j, a], from_l.at[j, a], from_r.at[j, a]), p.tok)

    drain(d_parts, r_d)
    add_rows(d_out, tuple(d_parts.at[k] for k in range(S)), R)
    drain(o_parts, r_oa)
    add_rows(o_out, tuple(o_parts.at[k] for k in range(S)), r)

    drain(u_out, r_ua)
    drain(q_out, r_qa)
    drain(v_all.at[pl.ds(0, p.n - 1)], r_v)

    own_v.wait()
    drain(v_all.at[pl.ds(0, p.n - 1)], s_v)
    drain(q_sib, s_q)
    drain(o_sib, s_o)
    for _ in range(S - 1):
        drain(u_mine, s_u)
        drain(q_group.at[0], s_qb)
    for _ in range(A * C - 1):
        drain(u_fin.at[0, 0], s_ua)
    for _ in range(HEADS - 1):
        drain(q_fin.at[0, 0], s_qa)
    for k in range(p.m):

        @pl.when(lax.div(head * HEAD_DIM, r) + 2 * k + core != me)
        def _():
            drain(o_mine.at[k], s_oa.at[k])

    for j in range(S):
        if p.P == 1:
            own_b, own_c = j, c
        else:
            own_b, own_c = 2 * (j // 2) + core, xh * 2 + j % 2

        @pl.when(jnp.logical_not((own_b == b) & (own_c == c)))
        def _():
            drain(d_parts.at[0], s_d.at[j])

    for j in range(2):
        for k in range(2):
            drain(from_sib.at[j, :, 0], s_s.at[j, k])
        for k in range(A):
            drain(to_x.at[j, k], s_x.at[j, k])

            @pl.when(k > a)
            def _():
                drain(line.at[j, k], s_r.at[j, k])

            @pl.when(k < a)
            def _():
                drain(line.at[j, k], s_l.at[j, k])


def collect(p, op, ep, qg, og, ug, dg, vec):
    dma = pltpu.SemaphoreType.DMA
    A, S, C, X, r, R = p.A, p.S, p.C, p.X, p.r, p.R
    vm = pltpu.VMEM
    return pl.pallas_call(
        functools.partial(collect_kernel, p),
        out_shape=(
            jax.ShapeDtypeStruct((p.tok, p.d), F32),
            jax.ShapeDtypeStruct((p.tok, p.d), F32),
            jax.ShapeDtypeStruct((r, 3 * p.d), BF),
            jax.ShapeDtypeStruct((r, p.d), F32),
            jax.ShapeDtypeStruct((r, p.ff), BF),
            jax.ShapeDtypeStruct((R, p.d), F32),
            jax.ShapeDtypeStruct((p.n, 16, 128), F32),
        ),
        in_specs=[pl.BlockSpec(memory_space=pl.ANY)] * 6 + [pl.BlockSpec(memory_space=pltpu.VMEM)],
        out_specs=[pl.BlockSpec(memory_space=pltpu.VMEM)] * 7,
        scratch_shapes=[
            vm((2, A, X, p.tok, p.d), BF),
            vm((2, A, X, p.tok, p.d), BF),
            vm((2, A, p.tok, p.d), BF),
            vm((2, A, p.tok, p.d), BF),
            vm((2, A, p.tok, p.d), BF),
            vm((2, A, p.tok, p.d), BF),
            vm((2, A, p.tok, p.d), BF),
            vm((A, S, X, r, p.hc), BF),
            vm((A, S, X, r, p.hc), BF),
            vm((S, A, X, r, p.hc), BF),
            vm((A, X, r, p.hc), BF),
            vm((p.m, r, p.d), BF),
            vm((p.m, r, p.d), BF),
            vm((S, r, p.d), BF),
            vm((A, C, r, p.ffl), BF),
            vm((S, A, C, r, p.ffl), BF),
            vm((A, C, r, p.ffl), BF),
            vm((1, 8, 128), BF),
            vm((S, R, p.d), BF),
            dma((8,)),
            dma,
            dma,
            dma((2, 2)),
            dma((2, 2)),
            dma((2, A)),
            dma((2, A)),
            dma((2, A)),
            dma((2, A)),
            dma((2, A)),
            dma((2, A)),
            dma,
            dma,
            dma,
            dma,
            dma,
            dma,
            dma,
            dma,
            dma((p.m,)),
            dma,
            dma,
            dma,
            dma,
            dma,
            dma((S,)),
            dma,
        ],
        compiler_params=pltpu.CompilerParams(
            collective_id=1, has_side_effects=True, vmem_limit_bytes=60 * 1024 * 1024
        ),
        name="collect",
    )(op, ep, qg, og, ug, dg, vec)


def norm_stats(values):
    center = jnp.mean(values, axis=-1, keepdims=True)
    spread = jnp.mean(jnp.square(values - center), axis=-1, keepdims=True)
    inv_std = lax.rsqrt(spread + EPS)
    return (values - center) * inv_std, inv_std


def tables(length):
    half = ROT // 2
    frequency = 10000.0 ** (-2.0 * jnp.arange(half, dtype=F32) / ROT)
    angles = jnp.arange(length, dtype=F32)[:, None] * frequency[None, :]
    return jnp.cos(angles), jnp.sin(angles)


def rotate(v, cos, sin):
    half = ROT // 2
    lo, hi = v[..., :half], v[..., half:ROT]
    return jnp.concatenate([lo * cos - hi * sin, hi * cos + lo * sin, v[..., ROT:]], axis=-1)


def dot(x, y):
    return jnp.dot(x, y, preferred_element_type=F32)


def dot_t(x, y):
    return lax.dot_general(x, y, (((1,), (1,)), ((), ())), preferred_element_type=F32)


def t_dot(x, y):
    return lax.dot_general(x, y, (((0,), (0,)), ((), ())), preferred_element_type=F32)


def attention(joint, d_heads, length, scale):
    cos, sin = tables(length)
    joint = joint.reshape(-1, length, 3 * HEAD_DIM)
    q = rotate(joint[..., :HEAD_DIM], cos, sin).astype(BF)
    k = rotate(joint[..., HEAD_DIM : 2 * HEAD_DIM], cos, sin).astype(BF)
    v = joint[..., 2 * HEAD_DIM :].astype(BF)
    pos = jnp.arange(length, dtype=jnp.int32)
    allowed = (pos[None, :] <= pos[:, None])[None]
    scores = jnp.einsum("sqd,skd->sqk", q, k, preferred_element_type=F32) * scale
    scores = jnp.where(allowed, scores, -1e30)
    expo = jnp.exp(scores - jnp.max(scores, axis=-1, keepdims=True))
    probs = expo / jnp.sum(expo, axis=-1, keepdims=True)
    low = probs.astype(BF)
    head_out = jnp.einsum("sqk,skd->sqd", low, v, preferred_element_type=F32).astype(BF)
    d_heads = d_heads.reshape(head_out.shape)
    dv = jnp.einsum("sqk,sqd->skd", low, d_heads, preferred_element_type=F32)
    dp = jnp.einsum("sqd,skd->sqk", d_heads, v, preferred_element_type=F32)
    delta = jnp.sum(probs * dp, axis=-1, keepdims=True)
    ds = (probs * (dp - delta)).astype(BF)
    dq = jnp.einsum("sqk,skd->sqd", ds, k, preferred_element_type=F32) * scale
    dk = jnp.einsum("sqk,sqd->skd", ds, q, preferred_element_type=F32) * scale
    d_joint = jnp.concatenate([rotate(dq, cos, -sin), rotate(dk, cos, -sin), dv], axis=-1)
    return head_out.reshape(-1, HEAD_DIM), d_joint.reshape(-1, 3 * HEAD_DIM).astype(BF)


def gelu_and_slope(v):
    phi = 0.5 * (1.0 + lax.erf(v * (1.0 / math.sqrt(2.0))))
    density = jnp.exp(-0.5 * v * v) * (1.0 / math.sqrt(2.0 * math.pi))
    return v * phi, phi + v * density


def local(
    dp_size,
    ctx_size,
    layer_input,
    lengths,
    cotangent,
    qkv_weight,
    qkv_bias,
    out_weight,
    out_bias,
    up_weight,
    up_bias,
    down_weight,
    down_bias,
    first_gain,
    first_bias,
    second_gain,
    second_bias,
):
    tok, d = layer_input.shape
    ff = up_weight.shape[1]
    p = Plan(dp_size, ctx_size, tok, d, ff)
    A, S, C, X, r, R = p.A, p.S, p.C, p.X, p.r, p.R
    dp, c, a, b, xh, core = place(p)
    me = dp * C + c
    t = a * C + c
    length = C * tok

    valid = (c * tok + jnp.arange(tok, dtype=jnp.int32) < lengths[0])[:, None]
    grad_out = jnp.where(valid, cotangent, jnp.zeros_like(cotangent))
    smalls = (
        qkv_bias,
        out_bias,
        up_bias,
        down_bias,
        first_gain,
        first_bias,
        second_gain,
        second_bias,
    )
    small = jnp.concatenate([v.astype(F32) for v in smalls])
    small = jnp.pad(small, (0, VEC - small.shape[0])).reshape(8, VEC // 8)
    x_all, g_all, qw, dw, uw, sm = spread(
        p, layer_input, grad_out, qkv_weight, out_weight, up_weight, down_weight, small
    )
    sm = sm.reshape(p.n, VEC)
    full, at = [], 0
    for v in smalls:
        full.append(sm[:, at : at + v.shape[0]].reshape(-1))
        at += v.shape[0]
    qkvb, outb, upb, downb, gain1, bias1, gain2, bias2 = full
    rows = p.rows
    mine = rows // 2
    head = a * X + xh
    x_all = x_all.reshape(rows, d)
    g_all = g_all.reshape(rows, d)
    qw = qw.reshape(d, p.hc)
    uw = uw.reshape(d, p.ffl)
    qb = lax.dynamic_index_in_dim(qkvb.reshape(3, HEADS, HEAD_DIM), head, 1, False).reshape(-1)
    if p.P == 1:
        ub = lax.dynamic_slice(upb.reshape(A, S, C, R), (a, 0, c, 0), (1, S, 1, R))
    else:
        ub = lax.dynamic_slice(
            upb.reshape(A, S // 2, 2, X, p.W), (a, 0, core, xh, 0), (1, S // 2, 1, 1, p.W)
        )
    ub = ub.reshape(-1)

    xs = lax.dynamic_slice(x_all, (core * mine, 0), (mine, d)).astype(F32)
    gs = lax.dynamic_slice(g_all, (core * mine, 0), (mine, d))
    xhat_s, _ = norm_stats(xs)
    n1 = (xhat_s * gain1 + bias1).astype(BF)
    joint = dot(n1, qw) + qb
    ow = dw[p.ffl :]
    d_heads = dot_t(gs, ow).astype(BF)
    head_out, d_joint = attention(joint, d_heads, length, 1.0 / math.sqrt(HEAD_DIM))
    out_grad = t_dot(head_out, gs).astype(BF)
    qkv_grad = t_dot(n1, d_joint).astype(BF)
    e1 = (dot_t(d_joint, qw) * gain1).astype(BF)
    qkv_bias_part = jnp.sum(d_joint.astype(F32), axis=0)

    xhat, _ = norm_stats(x_all.astype(F32))
    n2 = (xhat * gain2 + bias2).astype(BF)
    pre = dot(n2, uw) + ub
    act, slope = gelu_and_slope(pre)
    hidden = act.astype(BF)
    wide = jnp.zeros((rows, HEAD_DIM), BF)
    wide = lax.dynamic_update_slice(wide, head_out, (core * mine, 0))
    out_part = dot(jnp.concatenate([hidden, wide], axis=1), dw).astype(BF)
    down_grad = t_dot(hidden, g_all).astype(BF)
    d_pre = (dot_t(g_all, dw[: p.ffl]) * slope).astype(BF)
    up_grad = t_dot(n2, d_pre).astype(BF)
    up_bias_part = jnp.sum(d_pre.astype(F32), axis=0)
    e_part = dot_t(d_pre, uw) * gain2
    e_wide = jnp.zeros((rows, d), BF)
    e_wide = lax.dynamic_update_slice(e_wide, e1, (core * mine, 0))
    e_part = (e_part + e_wide.astype(F32)).astype(BF)

    g_cols = d // (A * C)
    g_part = lax.dynamic_slice(g_all, (0, t * g_cols), (rows, g_cols))
    g_part = jnp.sum(g_part.astype(F32), axis=0)
    vec = jnp.concatenate([qkv_bias_part, up_bias_part, g_part])
    vec = jnp.pad(vec, (0, 2048 - vec.shape[0])).reshape(16, 128)

    o_sum, e_sum, q_out, o_out, u_out, d_out, v_all = collect(
        p,
        out_part.reshape(A, X, 2, tok, d),
        e_part.reshape(A, X, 2, tok, d),
        qkv_grad.reshape(A, S, X, 2, r, p.hc),
        out_grad.reshape(p.m, 2, r, d),
        up_grad.reshape(A, S, C, r, p.ffl),
        down_grad,
        vec,
    )

    xf = layer_input.astype(F32)
    output = jnp.where(valid, xf + o_sum + (outb + downb), 0.0).astype(BF)
    xhat_o, inv = norm_stats(xf)
    dx = inv * (
        e_sum
        - jnp.mean(e_sum, axis=-1, keepdims=True)
        - xhat_o * jnp.mean(e_sum * xhat_o, axis=-1, keepdims=True)
    )
    input_grad = (grad_out.astype(F32) + dx).astype(BF)

    v_all = v_all.reshape(A, S, C, 2048)
    v_sum = jnp.sum(v_all, axis=1)
    q_bias = v_sum[..., : p.hc].reshape(A, X, 2, 3, HEAD_DIM).sum(axis=2)
    q_bias = q_bias.reshape(HEADS, 3, HEAD_DIM).transpose(1, 0, 2).reshape(-1)
    u_bias = v_sum[..., p.hc : p.hc + p.ffl]
    if p.P == 1:
        u_bias = u_bias.reshape(A, C, S, R).transpose(0, 2, 1, 3).reshape(-1)
    else:
        u_bias = u_bias.reshape(A, X, 2, S // 2, p.W).transpose(0, 3, 2, 1, 4).reshape(-1)
    g_bias = v_sum[..., p.hc + p.ffl : p.hc + p.ffl + g_cols].reshape(-1)

    def own(vector):
        size = vector.shape[0] // p.n
        return lax.dynamic_slice(vector, (me * size,), (size,))

    def norm_grads(weight, grad, bias_grad, gain, shift):
        weight = weight.astype(F32)
        shift_grad = jnp.sum(weight * bias_grad, axis=1)
        gain_grad = (jnp.sum(weight * grad, axis=1) - shift.astype(F32) * shift_grad) / gain.astype(
            F32
        )
        return gain_grad, shift_grad

    q_grad = q_out.astype(F32)
    u_grad = u_out.astype(F32)
    gain1_grad, bias1_grad = norm_grads(qkv_weight, q_grad, q_bias, first_gain, first_bias)
    gain2_grad, bias2_grad = norm_grads(up_weight, u_grad, u_bias, second_gain, second_bias)
    g_own = own(g_bias)
    return (
        output,
        input_grad,
        q_grad,
        own(q_bias),
        o_out,
        g_own,
        u_grad,
        own(u_bias),
        d_out,
        g_own,
        gain1_grad,
        bias1_grad,
        gain2_grad,
        bias2_grad,
    )


def solution(mesh):
    rows = P(("dp", "ctx"), None)
    vector = P(("dp", "ctx"))
    return jax.shard_map(
        functools.partial(local, mesh.shape["dp"], mesh.shape["ctx"]),
        mesh=mesh,
        in_specs=(
            rows,
            P("dp"),
            rows,
            rows,
            vector,
            rows,
            vector,
            rows,
            vector,
            rows,
            vector,
            vector,
            vector,
            vector,
            vector,
        ),
        out_specs=(
            rows,
            rows,
            rows,
            vector,
            rows,
            vector,
            rows,
            vector,
            rows,
            vector,
            vector,
            vector,
            vector,
            vector,
        ),
        check_vma=False,
    )
```

time: 3030 us -> 466 us (0.15)
  the two profiles are of different devices: /device:TPU:16 before, /device:TPU:2 now
where the time goes in v1:
time: 466 us; the launch traced here: 461 us
  Pallas kernels  298 us (64%)
  matrix products  90.3 us (19%)
  other arithmetic  45.3 us (10%)
  local copies, waits for them, and re-layouts  25.4 us (5%)
    pallas_call x1, Pallas kernels, collect(): pl.pallas_call(functools.partial(collect_kernel, p), out_shape=(jax.Shape...  168 us
    pallas_call x1, Pallas kernels, spread(): pl.pallas_call(functools.partial(spread_kernel, p), out_shape=(jax.ShapeD...  130 us
    dot_general x4, matrix products, t_dot(): lax.dot_general(x, y, (((0,), (0,)), ((), ())), preferred_element_type=F32)  33 us
    dot_general x4, matrix products, dot_t(): lax.dot_general(x, y, (((1,), (1,)), ((), ())), preferred_element_type=F32)  26.1 us
    dot_general x3, matrix products, dot(): return jnp.dot(x, y, preferred_element_type=F32)  21.8 us
    reduce_sum x3, other arithmetic, norm_stats(): spread = jnp.mean(jnp.square(values - center), axis=-1, keepdims=True)  9.44 us

profile of v1, /device:TPU:2, one launch (start us, length us, event | category | flops | bytes accessed | tf_op | source)
XLA Modules:
  0.0 461.4 jit_solution(11893389997867018984)
XLA Ops:
  1.8 1.9 broadcast_select_fusion.g
  3.8 5.4 %concatenate.38 = f32[832]{0:T(1024)S(1)} concatenate(bf16[192]{0:T(256)(128)(2,1)} %param.19, bf16[64]{0:T(256)(128)(2,1)} %param.21, bf16[256]{0:T(256)(128)(2,1)} %param.23, bf16[64]{0:T(256)(128)(2,1)} %param.25, bf16[64]{0:T(256)(128)(2,1)} %param.26, bf16[64]{0:T(256)(128)(2,1)} %param.27, bf16[64]{0:T(256)(128)(2,1)} %param.28, bf16[64]{0:T(256)(128)(2,1)} %param.29), dimensions={0} | concatenate | bytes 4992 | tf_op jit(solution)/shard_map/concatenate | solution.py:979
  9.8 130.3 %spread.1 = (bf16[4,4,128,2048]{3,2,1,0:T(8,128)(2,1)}, bf16[4,4,128,2048]{3,2,1,0:T(8,128)(2,1)}, bf16[4,2,2,2,64,768]{5,4,3,2,1,0:T(8,128)(2,1)}, bf16[768,204...) custom-call(bf16[128,2048]{1,0:T(8,128)(2,1)} %x.5, ...), custom_call_target="tpu_custom_call" | custom-call | tf_op jit(solution)/shard_map/spread/pallas_call | solution.py:375
  140.1 3.0 convert_reduce_fusion.1
  143.1 3.4 fusion.9
  147.5 6.4 %convolution_add_fusion = f32[1024,768]{1,0:T(8,128)S(1)} fusion(bf16[2048,768]{1,0:T(8,128)(2,1)S(1)} %bitcast.110, f32[768]{0:T(1024)S(1)} %add.201, f32[2048]{0:T(1024)S(1)} %add.196, f32[2048]{0:T(1024)S(1)} %mul.453, f32[1024]{0:T(1024)S(1)} %add_rsqrt_fusion.1, f32[1024]{0:T(1024)S(1)} %broadcast_multiply_fusion.1, bf16[2048,2048]{1,0:T(8,128)(2,1)} %bitcast.67, ...), kind=kOutput, calls=%fused_computation.61 | convolution fusion | flops 3234594816 | bytes 10513412 | tf_op jit(solution)/shard_map/dot_general | solution.py:897
  156.3 1.3 fusion.82
  158.4 4.6 fusion.85
  163.0 3.9 fusion.42
  172.4 2.8 concatenate.50
  177.5 4.5 convert_reduce_fusion
  182.1 5.7 %fusion.3 = f32[4,4,128]{2,1,0:T(4,128)S(1)} fusion(bf16[4,4,128,2048]{3,2,1,0:T(8,128)(2,1)} %get-tuple-element.27, f32[4,4,128]{2,1,0:T(4,128)S(1)} %broadcast_multiply_fusion), kind=kLoop, calls=%fused_computation.5 | loop fusion | flops 16775168 | bytes 8404992 | tf_op jit(solution)/shard_map/reduce_sum | solution.py:878
  188.0 6.4 %fusion.6 = bf16[4,4,128,2048]{3,2,1,0:T(8,128)(2,1)S(1)} fusion(bf16[4,4,128,2048]{3,2,1,0:T(8,128)(2,1)} %get-tuple-element.27, f32[2048]{0:T(1024)S(1)} %add.183, f32[2048]{0:T(1024)S(1)} %mul.442, f32[4,4,128]{2,1,0:T(4,128)S(1)} %add_rsqrt_fusion, f32[4,4,128]{2,1,0:T(4,128)S(1)} %broadcast_multiply_fusion), kind=kLoop, calls=%fused_computation.8 | loop fusion | flops 25165824 | bytes 16809984 | tf_op jit(solution)/shard_map/convert_element_type | solution.py:1020
  194.4 6.5 %multiply_convert_fusion.1 = (bf16[2048,512]{1,0:T(8,128)(2,1)}, f32[2048,512]{1,0:T(8,128)S(1)}) fusion(f32[512]{0:T(512)S(1)} %bitcast.108, bf16[2048,2048]{1,0:T(8,128)(2,1)S(1)} %bitcast.73, bf16[2048,512]{1,0:T(8,128)(2,1)S(1)} %bitcast.113), kind=kOutput, calls=%fused_computation.34 | convolution fusion | flops 4301258752 | bytes 16779264 | tf_op jit(solution)/shard_map/dot_general | solution.py:897
  200.9 8.0 %convert_reduce_fusion.2 = (f32[512]{0:T(512)S(1)}, bf16[2048,512]{1,0:T(8,128)(2,1)}) fusion(f32[2048,512]{1,0:T(8,128)S(1)} %get-tuple-element.77, f32[512]{0:T(512)S(1)} %bitcast.109, bf16[2048,2048]{1,0:T(8,128)(2,1)S(1)} %bitcast.106, bf16[768,2048]{1,0:T(8,128)(2,1)S(1)} %copy-done.30), kind=kOutput, calls=%fused_computation.33 | convolution fusion | flops 4308598272 | bytes 16781312 | tf_op jit(solution)/shard_map/dot_general | solution.py:901
  209.0 1.3 convert_reduce_fusion.5
  210.9 11.0 %fusion.32 = bf16[2048,512]{1,0:T(8,128)(2,1)} fusion(bf16[2048,512]{1,0:T(8,128)(2,1)} %get-tuple-element.81, bf16[2048,2048]{1,0:T(8,128)(2,1)} %bitcast.68, f32[2048]{0:T(1024)S(1)} %add.183, f32[2048]{0:T(1024)S(1)} %bitcast.99, f32[2048]{0:T(1024)S(1)} %bitcast.98, f32[2048]{0:T(1024)S(1)} %mul.442), kind=kOutput, calls=%fused_computation.46 | convolution fusion | flops 4321181696 | bytes 12615680 | tf_op jit(solution)/shard_map/dot_general | solution.py:905
  222.0 8.1 %convolution_convert_fusion.1 = bf16[2048,768]{1,0:T(8,128)(2,1)} fusion(bf16[1024,768]{1,0:T(8,128)(2,1)S(1)} %bitcast.74, f32[2048]{0:T(1024)S(1)} %copy-done.21, f32[2048]{0:T(1024)S(1)} %copy-done.19, f32[1024]{0:T(1024)S(1)} %copy-done.25, f32[1024]{0:T(1024)S(1)} %copy-done.17, bf16[2048,2048]{1,0:T(8,128)(2,1)} %bitcast.69, s32[]{:T(128)S(6)} %select_n.43), kind=kOutput, calls=%fused_computation.41 | convolution fusion | flops 3235381248 | bytes 8937476 | tf_op jit(solution)/shard_map/dot_general | solution.py:905
  230.1 2.6 concatenate.49
  234.6 3.8 fusion.24
  238.5 10.3 %add_convert_fusion.1 = bf16[2048,2048]{1,0:T(8,128)(2,1)} fusion(bf16[2048,2048]{1,0:T(8,128)(2,1)S(1)} %fusion.24, bf16[2048,512]{1,0:T(8,128)(2,1)} %get-tuple-element.81, bf16[2048,512]{1,0:T(8,128)(2,1)} %bitcast.112, f32[2048]{0:T(1024)S(1)} %mul.442), kind=kOutput, calls=%fused_computation.10 | convolution fusion | flops 4311744512 | bytes 20979712 | tf_op jit(solution)/shard_map/dot_general | solution.py:901
  248.8 9.3 %convolution_convert_fusion.2.dg = bf16[512,2048]{1,0:T(8,128)(2,1)} fusion(bf16[2048,512]{1,0:T(8,128)(2,1)S(1)} %copy-done.36, bf16[2048,2048]{1,0:T(8,128)(2,1)} %bitcast.102), kind=kOutput, calls=%fused_computation.47 | convolution fusion | flops 4296015872 | bytes 12582912 | tf_op jit(solution)/shard_map/dot_general | solution.py:905
  258.0 1.6 convolution_convert_fusion.3
  259.6 4.6 fusion.33
  264.4 8.8 %convolution_convert_fusion = bf16[2048,2048]{1,0:T(8,128)(2,1)} fusion(bf16[768,2048]{1,0:T(8,128)(2,1)S(1)} %copy-done.31, bf16[2048,256]{1,0:T(8,128)(2,1)S(1)} %constant_dynamic-update-slice_fusion, bf16[2048,512]{1,0:T(8,128)(2,1)S(1)} %copy-done.36), kind=kOutput, calls=%fused_computation.25 | convolution fusion | flops 6452936704 | bytes 14680064 | tf_op jit(solution)/shard_map/dot_general | solution.py:897
  273.2 167.9 %collect.1 = (f32[128,2048]{1,0:T(8,128)}, f32[128,2048]{1,0:T(8,128)}, bf16[64,6144]{1,0:T(8,128)(2,1)}, f32[64,2048]{1,0:T(8,128)}, bf16[64,8192]{1,0:T(8,128)...) custom-call(bf16[4,2,2,128,2048]{4,3,2,1,0:T(8,128)(2,1)} %bitcast.72, bf16[4,2,2,128,2048]{4,3,2,1,0:T(8,128)(2,1)} %bitcast.71, ...), custom_call_target="tpu_custom_call" | custom-call | tf_op jit(solution)/shard_map/collect/pallas_call | solution.py:808
  442.4 3.1 fusion.37
  447.0 2.7 fusion.41
  449.7 1.3 subtract_divide_fusion.1
  451.8 2.9 fusion.53
  455.3 1.3 dynamic_slice.32
  458.0 3.1 copy.73
  (138 shorter events, 21.2 us)
Async XLA Ops:
  140.1 6.5 %copy-start.12 = (f32[32,8,128]{2,1,0:T(8,128)S(1)}, f32[32,8,128]{2,1,0:T(8,128)}, u32[]{:S(2)}) copy-start(f32[32,8,128]{2,1,0:T(8,128)} %get-tuple-element.28) | copy-start | bytes 393220
  140.1 7.4 %copy-start.32 = (bf16[4,2,2,2,64,768]{5,4,3,2,1,0:T(8,128)(2,1)S(1)}, bf16[4,2,2,2,64,768]{5,4,3,2,1,0:T(8,128)(2,1)}, u32[]{:S(2)}) copy-start(bf16[4,2,2,2,64,768]{5,4,3,2,1,0:T(8,128)(2,1)} %get-tuple-element.30) | copy-start | bytes 9437188
  143.0 10.9 %copy-start.16 = (f32[1024]{0:T(1024)}, f32[1024]{0:T(1024)S(1)}, u32[]{:S(2)}) copy-start(f32[1024]{0:T(1024)S(1)} %broadcast_multiply_fusion.1) | copy-start | bytes 12292
  146.5 7.5 %copy-start.24 = (f32[1024]{0:T(1024)}, f32[1024]{0:T(1024)S(1)}, u32[]{:S(2)}) copy-start(f32[1024]{0:T(1024)S(1)} %add_rsqrt_fusion.1) | copy-start | bytes 12292
  147.4 6.6 %copy-start.18 = (f32[2048]{0:T(1024)}, f32[2048]{0:T(1024)S(1)}, u32[]{:S(2)}) copy-start(f32[2048]{0:T(1024)S(1)} %mul.453) | copy-start | bytes 24580
  147.5 6.5 %copy-start.20 = (f32[2048]{0:T(1024)}, f32[2048]{0:T(1024)S(1)}, u32[]{:S(2)}) copy-start(f32[2048]{0:T(1024)S(1)} %add.196) | copy-start | bytes 24580
  156.3 11.9 %copy-start.1 = (bf16[2,512,768]{2,1,0:T(8,128)(2,1)}, bf16[2,512,768]{2,1,0:T(8,128)(2,1)S(1)}, u32[]{:S(2)}) copy-start(bf16[2,512,768]{2,1,0:T(8,128)(2,1)S(1)} %bitcast_convert_fusion) | copy-start | bytes 4718596
  182.1 5.8 %copy-start.14 = (f32[32,64]{1,0:T(8,128)S(1)}, f32[32,64]{1,0:T(8,128)}, u32[]{:S(2)}) copy-start(f32[32,64]{1,0:T(8,128)} %get-tuple-element.70) | copy-start | bytes 24580
  182.1 5.8 %copy-start.13 = (f32[32,64]{1,0:T(8,128)S(1)}, f32[32,64]{1,0:T(8,128)}, u32[]{:S(2)}) copy-start(f32[32,64]{1,0:T(8,128)} %get-tuple-element.69) | copy-start | bytes 24580
  188.0 6.4 %copy-start.34 = (bf16[4,2,4,64,512]{4,3,2,1,0:T(8,128)(2,1)S(1)}, bf16[4,2,4,64,512]{4,3,2,1,0:T(8,128)(2,1)}, u32[]{:S(2)}) copy-start(bf16[4,2,4,64,512]{4,3,2,1,0:T(8,128)(2,1)} %get-tuple-element.29) | copy-start | bytes 6291460
  188.0 12.9 %slice-start = ((s8[8388608]{0:T(1024)(128)(4,1)}), s8[4194304]{0:T(1024)(128)(4,1)S(1)}, s32[]{:S(2)}) async-start(s8[8388608]{0:T(1024)(128)(4,1)} %bitcast.104), calls=%async_computation | async-start | bytes 8388608
  194.4 6.5 %slice-start.1 = ((s8[8388608]{0:T(1024)(128)(4,1)}), s8[4194304]{0:T(1024)(128)(4,1)S(1)}, s32[]{:S(2)}) async-start(s8[8388608]{0:T(1024)(128)(4,1)} %bitcast.104), calls=%async_computation.1 | async-start | bytes 8388608
  194.4 6.5 %copy-start.30 = (bf16[768,2048]{1,0:T(8,128)(2,1)S(1)}, bf16[768,2048]{1,0:T(8,128)(2,1)}, u32[]{:S(2)}) copy-start(bf16[768,2048]{1,0:T(8,128)(2,1)} %get-tuple-element.31) | copy-start | bytes 9437188
  200.9 9.4 %copy-start.15 = (f32[768]{0:T(1024)S(1)}, f32[768]{0:T(1024)}, u32[]{:S(2)}) copy-start(f32[768]{0:T(1024)} %convert_reduce_fusion.3) | copy-start | bytes 9220
  210.9 11.1 %copy-start.17 = (f32[1024]{0:T(1024)S(1)}, f32[1024]{0:T(1024)}, u32[]{:S(2)}) copy-start(f32[1024]{0:T(1024)} %copy-done.16) | copy-start | bytes 12292
  210.9 11.1 %copy-start.19 = (f32[2048]{0:T(1024)S(1)}, f32[2048]{0:T(1024)}, u32[]{:S(2)}) copy-start(f32[2048]{0:T(1024)} %copy-done.18) | copy-start | bytes 24580
  210.9 11.1 %copy-start.21 = (f32[2048]{0:T(1024)S(1)}, f32[2048]{0:T(1024)}, u32[]{:S(2)}) copy-start(f32[2048]{0:T(1024)} %copy-done.20) | copy-start | bytes 24580
  210.9 11.1 %copy-start.25 = (f32[1024]{0:T(1024)S(1)}, f32[1024]{0:T(1024)}, u32[]{:S(2)}) copy-start(f32[1024]{0:T(1024)} %copy-done.24) | copy-start | bytes 12292
  238.5 10.3 %copy-start.36 = (bf16[2048,512]{1,0:T(8,128)(2,1)S(1)}, bf16[2048,512]{1,0:T(8,128)(2,1)}, u32[]{:S(2)}) copy-start(bf16[2048,512]{1,0:T(8,128)(2,1)} %get-tuple-element.76) | copy-start | bytes 6291460
  248.8 9.3 %copy-start.6 = (f32[2,512,512]{1,2,0:T(8,128)S(1)}, f32[2,512,512]{1,2,0:T(8,128)}, u32[]{:S(2)}) copy-start(f32[2,512,512]{1,2,0:T(8,128)} %get-tuple-element.75) | copy-start | bytes 6291460
  248.8 9.3 %copy-start.23 = (f32[2,512]{1,0:T(2,128)S(1)}, f32[2,512]{1,0:T(2,128)}, u32[]{:S(2)}) copy-start(f32[2,512]{1,0:T(2,128)} %get-tuple-element.74) | copy-start | bytes 12292
  259.6 4.7 %copy-start.31 = (bf16[768,2048]{1,0:T(8,128)(2,1)S(1)}, bf16[768,2048]{1,0:T(8,128)(2,1)}, u32[]{:S(2)}) copy-start(bf16[768,2048]{1,0:T(8,128)(2,1)} %get-tuple-element.31) | copy-start | bytes 9437188
  273.2 169.2 %copy-start.2 = (bf16[64,8192]{1,0:T(8,128)(2,1)S(1)}, bf16[64,8192]{1,0:T(8,128)(2,1)}, u32[]{:S(2)}) copy-start(bf16[64,8192]{1,0:T(8,128)(2,1)} %up.1) | copy-start | bytes 3145732
  441.1 5.8 %copy-start.4 = (bf16[64,6144]{1,0:T(8,128)(2,1)S(1)}, bf16[64,6144]{1,0:T(8,128)(2,1)}, u32[]{:S(2)}) copy-start(bf16[64,6144]{1,0:T(8,128)(2,1)} %qkv.1) | copy-start | bytes 2359300
  442.2 8.7 %copy-start = (bf16[128,2048]{1,0:T(8,128)(2,1)S(1)}, bf16[128,2048]{1,0:T(8,128)(2,1)}, u32[]{:S(2)}) copy-start(bf16[128,2048]{1,0:T(8,128)(2,1)} %x.5) | copy-start | bytes 1572868
  442.4 4.5 copy-start.11
  442.4 9.0 %copy-start.3 = (f32[128,2048]{1,0:T(8,128)S(1)}, f32[128,2048]{1,0:T(8,128)}, u32[]{:S(2)}) copy-start(f32[128,2048]{1,0:T(8,128)} %get-tuple-element.34) | copy-start | bytes 3145732
  445.6 6.3 %copy-start.7 = (bf16[128,2048]{1,0:T(8,128)(2,1)S(1)}, bf16[128,2048]{1,0:T(8,128)(2,1)}, u32[]{:S(2)}) copy-start(bf16[128,2048]{1,0:T(8,128)(2,1)} %param.17) | copy-start | bytes 1572868
  445.6 6.2 %copy-start.27 = (pred[128]{0:T(512)(128)(4,1)S(1)}, pred[128]{0:T(512)(128)(4,1)}, u32[]{:S(2)}) copy-start(pred[128]{0:T(512)(128)(4,1)} %copy-done.26) | copy-start | bytes 388
  449.7 11.5 %copy-start.29 = (f32[64]{0:T(128)}, f32[64]{0:T(128)S(1)}, u32[]{:S(2)}) copy-start(f32[64]{0:T(128)S(1)} %get-tuple-element.137) | copy-start | bytes 772
  449.7 7.6 %copy-start.8 = (f32[64,2048]{1,0:T(8,128)S(1)}, f32[64,2048]{1,0:T(8,128)}, u32[]{:S(2)}) copy-start(f32[64,2048]{1,0:T(8,128)} %get-tuple-element.130) | copy-start | bytes 1572868
  456.7 4.5 copy-start.35
  (7 other events, 14.6 us)

commit v2 on v1

v2 whole, which is shorter than its diff:
```python
import functools
import math

import jax
import jax.numpy as jnp
from jax import lax
from jax.experimental import pallas as pl
from jax.experimental.pallas import tpu as pltpu
from jax.sharding import PartitionSpec as P

HEADS = 8
HEAD_DIM = 256
ROT = 64
EPS = 1e-05
SCALE = 1.0 / math.sqrt(HEAD_DIM)
MESH = pl.DeviceIdType.MESH
BF = jnp.bfloat16
F32 = jnp.float32
TILE = 256
LANES = 128


class Plan:
    def __init__(self, dp, ctx, tok, d, ff):
        self.C = ctx
        self.X = ctx // 2
        self.A = HEADS // self.X
        self.S = dp // self.A
        self.n = dp * ctx
        self.tok = tok
        self.d = d
        self.ff = ff
        self.r = d // self.n
        self.R = ff // self.n
        self.ffl = self.S * self.R
        self.W = max(self.R, 128)
        self.P = self.W // self.R
        self.hc = 3 * HEAD_DIM
        self.m = HEAD_DIM // self.r // 2
        self.rows = self.A * self.C * tok


def remote(src, dst, send, recv, dev):
    return pltpu.make_async_remote_copy(
        src_ref=src, dst_ref=dst, send_sem=send, recv_sem=recv, device_id=dev, device_id_type=MESH
    )


def drain(ref, sem):
    pltpu.make_async_copy(ref, ref, sem).wait()


def unit_run(p, aa, cc, j):
    if p.P == 1:
        return p.R * ((aa * p.S + j) * p.C + cc)
    return p.R * ((aa * p.S + 2 * j + lax.rem(cc, 2)) * p.C + lax.div(cc, 2) * 2)


def unit_home(p, b, xh, core):
    if p.P == 1:
        return xh * 2 + core, b * p.R
    return xh * 2 + lax.rem(b, 2), (lax.div(b, 2) * 2 + core) * p.R


def place(p):
    dp = lax.axis_index("dp")
    c = lax.axis_index("ctx")
    a = lax.div(dp, p.S)
    b = lax.rem(dp, p.S)
    xh = lax.div(c, 2)
    core = lax.rem(c, 2)
    return dp, c, a, b, xh, core


def greet_all(p, me):
    barrier = pltpu.get_barrier_semaphore()

    def greet(k, carry):
        other = lax.rem(me + k, p.n)
        pl.semaphore_signal(
            barrier,
            inc=1,
            device_id=(lax.div(other, p.C), lax.rem(other, p.C)),
            device_id_type=MESH,
        )
        return carry

    lax.fori_loop(1, p.n, greet, 0)
    pl.semaphore_wait(barrier, p.n - 1)


def dot(x, y):
    return jnp.dot(x, y, preferred_element_type=F32)


def dot_t(x, y):
    return lax.dot_general(x, y, (((1,), (1,)), ((), ())), preferred_element_type=F32)


def t_dot(x, y):
    return lax.dot_general(x, y, (((0,), (0,)), ((), ())), preferred_element_type=F32)


def tiles(count, body, size=TILE):
    def run(i, carry):
        body(pl.multiple_of(i * size, size))
        return carry

    lax.fori_loop(0, count // size, run, 0)


def pick(values, i):
    out = values[0]
    for k in range(1, len(values)):
        out = jnp.where(i == k, values[k], out)
    return out


def far_order(p, a):
    order = []
    lo, hi = 0, p.A - 1
    for _ in range(p.A):
        up_far = hi - a >= a - lo
        order.append(jnp.where(up_far, hi, lo))
        lo = jnp.where(up_far, lo, lo + 1)
        hi = jnp.where(up_far, hi - 1, hi)
    return order


def add_rows(dst, parts, rows):
    step = 16

    def body(k, carry):
        at = pl.ds(pl.multiple_of(k * step, step), step)
        total = parts[0][at, :].astype(F32)
        for part in parts[1:]:
            total = total + part[at, :].astype(F32)
        dst[at, :] = total.astype(dst.dtype)
        return carry

    lax.fori_loop(0, rows // step, body, 0)


def angle_tables(cos_v, sin_v):
    rows = cos_v.shape[0]
    half = ROT // 2

    def body(at):
        shape = (64, LANES)
        lane = lax.broadcasted_iota(jnp.int32, shape, 1)
        pos = (lax.broadcasted_iota(jnp.int32, shape, 0) + at).astype(F32)
        exponent = lax.rem(lane, half).astype(F32) * (-2.0 * math.log(10000.0) / ROT)
        angle = pos * jnp.exp(exponent)
        turned = lane < ROT
        sign = jnp.where(lane < half, -1.0, 1.0)
        cos_v[pl.ds(at, 64), :] = jnp.where(turned, jnp.cos(angle), 1.0)
        sin_v[pl.ds(at, 64), :] = jnp.where(turned, jnp.sin(angle) * sign, 0.0)

    tiles(rows, body, 64)


def turn(v, cos, sin):
    first = v[:, :LANES]
    half = ROT // 2
    lane = lax.broadcasted_iota(jnp.int32, first.shape, 1)
    partner = jnp.where(
        lane < half, pltpu.roll(first, LANES - half, 1), pltpu.roll(first, half, 1)
    )
    return jnp.concatenate([first * cos + partner * sin, v[:, LANES:]], axis=1)


def probabilities(q, k, row0, scale):
    scores = dot_t(q, k) * scale
    row = lax.broadcasted_iota(jnp.int32, scores.shape, 0) + row0
    col = lax.broadcasted_iota(jnp.int32, scores.shape, 1)
    scores = jnp.where(col <= row, scores, -1e30)
    expo = jnp.exp(scores - jnp.max(scores, axis=1, keepdims=True))
    return expo / jnp.sum(expo, axis=1, keepdims=True)


def front_kernel(
    p,
    x,
    g,
    qkv,
    outw,
    up,
    down,
    lens,
    qkv_b,
    out_b,
    up_b,
    down_b,
    gain1,
    bias1,
    gain2,
    bias2,
    xa,
    ga,
    qw,
    dw,
    uw,
    sm,
    n1,
    n2,
    hid,
    slope,
    heads,
    joint,
    rows_out,
    small,
    pads,
    gm,
    sm_v,
    vecs,
    ub,
    qb,
    cos_v,
    sin_v,
    uw_v,
    qw_v,
    xs,
    n1_v,
    n2_v,
    hid_v,
    slope_v,
    heads_v,
    joint_v,
    loc,
    s_sm,
    r_sm,
    s_up,
    r_up,
    s_upb,
    r_upb,
    s_q,
    r_q,
    s_qb,
    r_qb,
    s_qc,
    r_qc,
    s_o,
    r_o,
    s_oc,
    r_oc,
    s_d,
    r_d,
    s_r,
    r_r,
    s_l,
    r_l,
    s_x,
    r_x,
    s_s,
    r_s,
):
    A, S, C, r, R = p.A, p.S, p.C, p.r, p.R
    dp, c, a, b, xh, core = place(p)
    me = dp * C + c
    t = a * C + c
    head = a * p.X + xh
    sib = (dp, xh * 2 + 1 - core)
    xnb = (dp, (1 - xh) * 2 + core)
    right = (dp + S, c)
    left = (dp - S, c)
    L = C * p.tok
    half = A // 2

    length = lens[0]

    def mask(at):
        row = lax.broadcasted_iota(jnp.int32, (32, p.d), 0) + (at + c * p.tok)
        rows = g[pl.ds(at, 32), :].astype(F32)
        gm[pl.ds(at, 32), :] = jnp.where(row < length, rows, 0.0).astype(BF)

    tiles(p.tok, mask, 32)

    pads[...] = jnp.zeros_like(pads)
    vectors = (qkv_b, up_b, gain1, bias1, gain2, bias2, out_b)
    for k, v in enumerate(vectors):
        value = v[...].astype(F32)
        if k == len(vectors) - 1:
            value = value + down_b[...].astype(F32)
        pads[k : k + 1, 0 : v.shape[1]] = value
    for k, v in enumerate(vectors):
        placed = pltpu.roll(pads[k : k + 1, :], lax.rem(v.shape[1] * me, LANES), 1)
        small[2 * k : 2 * k + 1, :] = placed[:, :LANES]
        small[2 * k + 1 : 2 * k + 2, :] = placed[:, LANES:]
    small[2 * len(vectors) :, :] = jnp.zeros((2, LANES), F32)
    greet_all(p, me)

    own_small = pltpu.make_async_copy(small, sm.at[me], loc.at[0])
    own_small.start()
    own_x = pltpu.make_async_copy(x, xa.at[a, pl.ds(pl.multiple_of(c * p.tok, p.tok), p.tok)], loc.at[1])
    own_x.start()
    own_g = pltpu.make_async_copy(gm, ga.at[a, pl.ds(pl.multiple_of(c * p.tok, p.tok), p.tok)], loc.at[2])
    own_g.start()

    def small_send(k, carry):
        other = lax.rem(me + k, p.n)
        dev = (lax.div(other, C), lax.rem(other, C))
        remote(small, sm.at[me], s_sm, r_sm, dev).start()
        return carry

    lax.fori_loop(1, p.n, small_send, 0)

    def up_piece(aa, cc, j):
        col = pl.multiple_of(unit_run(p, aa, cc, j), 128)
        return up.at[:, pl.ds(col, p.W)], uw.at[a, b, c, :, pl.ds(j * p.W, p.W)]

    def up_send(k, carry):
        tt = lax.rem(t + k, A * C)
        aa, cc = lax.div(tt, C), lax.rem(tt, C)
        for j in range(p.ffl // p.W):
            src, dst = up_piece(aa, cc, j)
            remote(src, dst, s_up, r_up, (aa * S + b, cc)).start()
        return carry

    lax.fori_loop(1, A * C, up_send, 0)
    for j in range(p.ffl // p.W):
        src, dst = up_piece(a, c, j)
        pltpu.make_async_copy(src, dst, r_up).start()

    def q_piece(hh, j):
        col = pl.multiple_of(j * p.d + hh * HEAD_DIM, HEAD_DIM)
        return (
            qkv.at[:, pl.ds(col, HEAD_DIM)],
            qw.at[a, b, xh, core, :, pl.ds(j * HEAD_DIM, HEAD_DIM)],
        )

    def q_send(k, carry):
        hh = lax.rem(head + k, HEADS)
        for j in range(3):
            src, dst = q_piece(hh, j)
            dev = (lax.div(hh, p.X) * S + b, lax.rem(hh, p.X) * 2 + core)
            remote(src, dst, s_q, r_q, dev).start()
        return carry

    lax.fori_loop(1, HEADS, q_send, 0)
    for j in range(3):
        src, dst = q_piece(head, j)
        pltpu.make_async_copy(src, dst, r_q).start()

    row_head = lax.div(me * r, HEAD_DIM)
    row_part = lax.div(lax.rem(me * r, HEAD_DIM), 2 * r)
    o_dst = dw.at[pl.ds(pl.multiple_of(p.ffl + (row_part * 2 + core) * r, r), r)]

    def o_dev(bb):
        return lax.div(row_head, p.X) * S + bb, lax.rem(row_head, p.X) * 2 + core

    for bb in range(S):
        od, oc = o_dev(bb)
        here = (od == dp) & (oc == c)

        @pl.when(jnp.logical_not(here))
        def _():
            remote(outw, o_dst, s_o.at[bb], r_o, (od, oc)).start()

        @pl.when(here)
        def _():
            pltpu.make_async_copy(outw, o_dst, r_o).start()

    d_ctx, d_row = unit_home(p, b, xh, core)
    d_dst = dw.at[pl.ds(pl.multiple_of(d_row, R), R)]
    for bb in range(S):
        here = (bb == b) & (d_ctx == c)

        @pl.when(jnp.logical_not(here))
        def _():
            remote(down, d_dst, s_d.at[bb], r_d, (a * S + bb, d_ctx)).start()

        @pl.when(here)
        def _():
            pltpu.make_async_copy(down, d_dst, r_d).start()

    streams = ((x, xa), (gm, ga))

    def blk(j, k, cc):
        return streams[j][1].at[k, pl.ds(pl.multiple_of(cc * p.tok, p.tok), p.tok)]

    def send_own(j):
        own, slot = streams[j][0], blk(j, a, c)

        @pl.when(a < A - 1)
        def _():
            remote(own, slot, s_r.at[j, 0], r_r.at[j, 0], right).start()

        @pl.when(a > 0)
        def _():
            remote(own, slot, s_l.at[j, 0], r_l.at[j, 0], left).start()

        remote(own, slot, s_x.at[j, a], r_x.at[j, a], xnb).start()
        remote(own, slot, s_s.at[j, a], r_s.at[j, a], sib).start()

    def z_step(j, s):
        @pl.when(a - 1 - s >= 0)
        def _():
            k = a - 1 - s
            part = blk(j, k, c)
            drain(part, r_r.at[j, s])

            @pl.when((s + 1 < A - 1) & (a < A - 1))
            def _():
                nxt = jnp.minimum(s + 1, A - 2)
                remote(part, part, s_r.at[j, nxt], r_r.at[j, nxt], right).start()

            remote(part, part, s_x.at[j, k], r_x.at[j, k], xnb).start()
            remote(part, part, s_s.at[j, k], r_s.at[j, k], sib).start()

        @pl.when(a + 1 + s <= A - 1)
        def _():
            k = a + 1 + s
            part = blk(j, k, c)
            drain(part, r_l.at[j, s])

            @pl.when((s + 1 < A - 1) & (a > 0))
            def _():
                nxt = jnp.minimum(s + 1, A - 2)
                remote(part, part, s_l.at[j, nxt], r_l.at[j, nxt], left).start()

            remote(part, part, s_x.at[j, k], r_x.at[j, k], xnb).start()
            remote(part, part, s_s.at[j, k], r_s.at[j, k], sib).start()

    xc = (1 - xh) * 2 + core

    def cross(j, k):
        part = blk(j, k, xc)
        drain(part, r_x.at[j, k])
        remote(part, part, s_s.at[j, k], r_s.at[j, k], sib).start()

    send_own(0)
    angle_tables(cos_v, sin_v)

    own_small.wait()
    drain(sm.at[pl.ds(0, p.n - 1)], r_sm)
    get_small = pltpu.make_async_copy(sm, sm_v, loc.at[0])
    get_small.start()
    get_small.wait()

    def chunk(which, jj):
        size = vectors[which].shape[1]
        if size % LANES == 0:
            count = 1
        elif LANES % size == 0:
            count = LANES // size
        else:
            count = (LANES - 1) // size + 2
        total = jnp.zeros((1, LANES), F32)
        for o in range(count):
            i = lax.div(LANES * jj, size) + o
            row = jj - lax.div(i * size, LANES)
            good = ((row >= 0) & (row <= 1) & (i < p.n)).astype(F32)
            at = 2 * which + jnp.clip(row, 0, 1)
            total = total + good * sm_v[jnp.minimum(i, p.n - 1), pl.ds(at, 1), :]
        return total

    def fill(jj, carry):
        for k in range(5):
            vecs[k : k + 1, pl.ds(pl.multiple_of(jj * LANES, LANES), LANES)] = chunk(2 + k, jj)
        return carry

    lax.fori_loop(0, p.d // LANES, fill, 0)
    for j in range(p.ffl // LANES):
        run, rest = j * LANES // p.W, (j * LANES % p.W) // LANES
        first = lax.div(unit_run(p, a, c, run), LANES) + rest
        ub[:, j * LANES : (j + 1) * LANES] = chunk(1, first)
    for j in range(3):
        for k in range(HEAD_DIM // LANES):
            first = (j * p.d + head * HEAD_DIM) // LANES + k
            at = j * HEAD_DIM + k * LANES
            qb[:, at : at + LANES] = chunk(0, first)

    drain(uw.at[:, b], r_up)

    def up_cross(k, carry):
        bb = lax.rem(b + k, S)
        remote(uw.at[:, b], uw.at[:, b], s_upb, r_upb, (a * S + bb, c)).start()
        return carry

    lax.fori_loop(1, S, up_cross, 0)
    drain(qw.at[:, b, :, core], r_q)

    def q_cross(k, carry):
        bb = lax.rem(b + k, S)
        part = qw.at[:, b, :, core]
        remote(part, part, s_qb, r_qb, (a * S + bb, c)).start()
        return carry

    lax.fori_loop(1, S, q_cross, 0)
    drain(dw.at[pl.ds(p.ffl, p.m * r)], r_o)
    for k in range(p.m):
        rows = dw.at[pl.ds(pl.multiple_of(p.ffl + (2 * k + core) * r, r), r)]
        remote(rows, rows, s_oc.at[k], r_oc.at[k], sib).start()

    near = far_order(p, a)[::-1]

    def slot_rows(k):
        return pl.ds(pl.multiple_of(k * L, L), L)

    def forward_slot(k):
        get = pltpu.make_async_copy(xa.at[k], xs, loc.at[3])
        get.start()
        get.wait()
        mine = lax.div(k, half) == core

        def norm(at):
            rows = xs[pl.ds(at, 16), :].astype(F32)
            center = jnp.mean(rows, axis=1, keepdims=True)
            rows = rows - center
            spread = jnp.mean(rows * rows, axis=1, keepdims=True)
            rows = rows * lax.rsqrt(spread + EPS)
            n2_v[pl.ds(at, 16), :] = (rows * vecs[2:3, :] + vecs[3:4, :]).astype(BF)

            @pl.when(mine)
            def _():
                own_at = pl.multiple_of(lax.rem(k, half) * L + at, 16)
                n1_v[pl.ds(own_at, 16), :] = (rows * vecs[0:1, :] + vecs[1:2, :]).astype(BF)

        tiles(L, norm, 16)
        put = pltpu.make_async_copy(n2_v, n2.at[slot_rows(k)], loc.at[4])
        put.start()

        def unit_tile(n):
            at = pl.ds(n, TILE)
            w = uw_v[:, :, :, :, at].reshape(p.d, TILE)
            v = dot(n2_v[...], w) + ub[:, at]
            phi = 0.5 * (1.0 + lax.erf(v * (1.0 / math.sqrt(2.0))))
            density = jnp.exp(-0.5 * v * v) * (1.0 / math.sqrt(2.0 * math.pi))
            hid_v[slot_rows(k), at] = (v * phi).astype(BF)
            slope_v[slot_rows(k), at] = (phi + v * density).astype(BF)

        tiles(p.ffl, unit_tile)
        put.wait()

    def x_round(i, carry):
        k = pick(near, i)

        @pl.when(i < A - 1)
        def _():
            z_step(0, i)

        cross(0, k)

        @pl.when(i == 0)
        def _():
            send_own(1)
            own_x.wait()
            for _ in range(S - 1):
                drain(uw.at[:, b], r_upb)
            get = pltpu.make_async_copy(uw, uw_v, loc.at[3])
            get.start()
            for _ in range(S - 1):
                drain(qw.at[:, b, :, core], r_qb)
            part = qw.at[:, :, :, core]
            remote(part, part, s_qc, r_qc, sib).start()
            get.wait()

        drain(xa.at[k, pl.ds(0, p.X * p.tok)], r_s.at[0, k])
        forward_slot(k)

        @pl.when(i > 0)
        def _():
            z_step(1, i - 1)

        return carry

    lax.fori_loop(0, A, x_round, 0)
    put_hid = pltpu.make_async_copy(hid_v, hid, loc.at[4])
    put_hid.start()
    put_slope = pltpu.make_async_copy(slope_v, slope, loc.at[5])
    put_slope.start()
    put_n1 = pltpu.make_async_copy(n1_v, n1, loc.at[6])
    put_n1.start()
    put_rows = pltpu.make_async_copy(vecs, rows_out, loc.at[7])
    put_rows.start()
    drain(qw.at[:, :, :, 1 - core], r_qc)
    get_qw = pltpu.make_async_copy(qw, qw_v, loc.at[3])
    get_qw.start()
    get_qw.wait()

    def attend(i):
        own = pl.ds(pl.multiple_of(i * L, L), L)
        cols = [pl.ds(j * HEAD_DIM, HEAD_DIM) for j in range(3)]
        for j in range(3):
            w = qw_v[:, :, :, :, :, cols[j]].reshape(p.d, HEAD_DIM)
            v = dot(n1_v[own, :], w) + qb[:, cols[j]]
            if j < 2:
                v = turn(v, cos_v[...], sin_v[...])
            joint_v[own, cols[j]] = v.astype(BF)
        rows = L // 2
        for h in range(2):
            at = pl.ds(pl.multiple_of(i * L + h * rows, rows), rows)
            keys = pl.ds(pl.multiple_of(i * L, L), (h + 1) * rows)
            probs = probabilities(joint_v[at, cols[0]], joint_v[keys, cols[1]], h * rows, SCALE)
            heads_v[at, :] = dot(probs.astype(BF), joint_v[keys, cols[2]]).astype(BF)

    def g_round(i, carry):
        cross(1, pick(near, i))

        @pl.when(i < half)
        def _():
            attend(i)

        return carry

    lax.fori_loop(0, A, g_round, 0)
    put_heads = pltpu.make_async_copy(heads_v, heads, loc.at[0])
    put_heads.start()
    put_joint = pltpu.make_async_copy(joint_v, joint, loc.at[1])
    put_joint.start()

    drain(dw.at[pl.ds(0, p.ffl)], r_d)
    for k in range(p.m):
        drain(dw.at[pl.ds(0, r)], r_oc.at[k])
    for k in range(A):
        drain(ga.at[k, pl.ds(0, p.X * p.tok)], r_s.at[1, k])

    own_g.wait()
    put_hid.wait()
    put_slope.wait()
    put_n1.wait()
    put_rows.wait()
    put_heads.wait()
    put_joint.wait()
    drain(sm.at[pl.ds(0, p.n - 1)], s_sm)
    for _ in range(A * C - 1):
        drain(uw.at[a, b, c], s_up)
    for _ in range(HEADS - 1):
        drain(qw.at[a, b, xh, core], s_q)
    for bb in range(S):
        od, oc = o_dev(bb)

        @pl.when(jnp.logical_not((od == dp) & (oc == c)))
        def _():
            drain(outw, s_o.at[bb])

        @pl.when(jnp.logical_not((bb == b) & (d_ctx == c)))
        def _():
            drain(down, s_d.at[bb])

    for k in range(p.m):
        drain(dw.at[pl.ds(0, r)], s_oc.at[k])
    for _ in range(S - 1):
        drain(uw.at[:, b], s_upb)
        drain(qw.at[:, b, :, core], s_qb)
    drain(qw.at[:, :, :, core], s_qc)
    for j in range(2):
        for s in range(A - 1):

            @pl.when((a < A - 1) & (a - s >= 0))
            def _():
                drain(x, s_r.at[j, s])

            @pl.when((a > 0) & (a + s <= A - 1))
            def _():
                drain(x, s_l.at[j, s])

        for k in range(A):
            drain(x, s_x.at[j, k])
            drain(xa.at[k, pl.ds(0, p.X * p.tok)], s_s.at[j, k])


def front(p, x, g, qkv, outw, up, down, lens, *vectors):
    dma = pltpu.SemaphoreType.DMA
    A, S, C, r = p.A, p.S, p.C, p.r
    L = C * p.tok
    vm = pltpu.VMEM
    hbm = pl.BlockSpec(memory_space=pl.ANY)
    vmem = pl.BlockSpec(memory_space=pltpu.VMEM)
    half = p.rows // 2
    qw_shape = (A, S, p.X, 2, r, p.hc)
    uw_shape = (A, S, C, r, p.ffl)
    return pl.pallas_call(
        functools.partial(front_kernel, p),
        out_shape=(
            jax.ShapeDtypeStruct((A, L, p.d), BF),
            jax.ShapeDtypeStruct((A, L, p.d), BF),
            jax.ShapeDtypeStruct(qw_shape, BF),
            jax.ShapeDtypeStruct((p.ffl + HEAD_DIM, p.d), BF),
            jax.ShapeDtypeStruct(uw_shape, BF),
            jax.ShapeDtypeStruct((p.n, 16, LANES), F32),
            jax.ShapeDtypeStruct((half, p.d), BF),
            jax.ShapeDtypeStruct((p.rows, p.d), BF),
            jax.ShapeDtypeStruct((p.rows, p.ffl), BF),
            jax.ShapeDtypeStruct((p.rows, p.ffl), BF),
            jax.ShapeDtypeStruct((half, HEAD_DIM), BF),
            jax.ShapeDtypeStruct((half, p.hc), BF),
            jax.ShapeDtypeStruct((8, p.d), F32),
        ),
        in_specs=[vmem] * 6 + [pl.BlockSpec(memory_space=pltpu.SMEM)] + [vmem] * 8,
        out_specs=[hbm] * 13,
        scratch_shapes=[
            vm((16, LANES), F32),
            vm((8, 2 * LANES), F32),
            vm((p.tok, p.d), BF),
            vm((p.n, 16, LANES), F32),
            vm((8, p.d), F32),
            vm((1, p.ffl), F32),
            vm((1, p.hc), F32),
            vm((L, LANES), F32),
            vm((L, LANES), F32),
            vm(uw_shape, BF),
            vm(qw_shape, BF),
            vm((L, p.d), BF),
            vm((half, p.d), BF),
            vm((L, p.d), BF),
            vm((p.rows, p.ffl), BF),
            vm((p.rows, p.ffl), BF),
            vm((half, HEAD_DIM), BF),
            vm((half, p.hc), BF),
            dma((8,)),
            dma,
            dma,
            dma,
            dma,
            dma,
            dma,
            dma,
            dma,
            dma,
            dma,
            dma,
            dma,
            dma((S,)),
            dma,
            dma((p.m,)),
            dma((p.m,)),
            dma((S,)),
            dma,
            dma((2, A - 1)),
            dma((2, A - 1)),
            dma((2, A - 1)),
            dma((2, A - 1)),
            dma((2, A)),
            dma((2, A)),
            dma((2, A)),
            dma((2, A)),
        ],
        compiler_params=pltpu.CompilerParams(
            collective_id=0, has_side_effects=True, vmem_limit_bytes=60 * 1024 * 1024
        ),
        name="front",
    )(x, g, qkv, outw, up, down, lens, *vectors)


def back_kernel(
    p,
    hid,
    heads,
    slope,
    g,
    joint,
    n1,
    n2,
    dw,
    uw,
    qw,
    gains,
    o_sum,
    e_sum,
    q_out,
    u_out,
    d_parts,
    o_parts,
    v_all,
    hid_v,
    heads_v,
    dpre,
    ge,
    joint_v,
    dw_v,
    uw_v,
    qw_v,
    n_v,
    t_v,
    dh_v,
    cos_v,
    sin_v,
    op,
    from_sib,
    from_x,
    came,
    dgrad,
    q_g,
    q_sib,
    q_group,
    o_g,
    o_sib,
    u_parts,
    vec,
    loc,
    n_sem,
    s_v,
    r_v,
    s_s,
    r_s,
    s_x,
    r_x,
    s_c,
    r_c,
    s_q,
    r_q,
    s_qb,
    r_qb,
    s_qa,
    r_qa,
    s_o,
    r_o,
    s_oa,
    r_oa,
    s_u,
    r_u,
    s_ua,
    r_ua,
    s_d,
    r_d,
    free,
):
    A, S, C, X, r, R = p.A, p.S, p.C, p.X, p.r, p.R
    dp, c, a, b, xh, core = place(p)
    me = dp * C + c
    t = a * C + c
    head = a * X + xh
    sib = (dp, xh * 2 + 1 - core)
    xnb = (dp, (1 - xh) * 2 + core)
    far = 1 - xh
    L = C * p.tok
    D, ffl = p.d, p.ffl
    half = A // 2
    ugrad = hid_v

    loads = [
        pltpu.make_async_copy(src, dst, loc.at[k])
        for k, (src, dst) in enumerate(
            (
                (hid, hid_v.at[pl.ds(0, p.rows)]),
                (dw, dw_v),
                (heads, heads_v),
                (g, ge),
                (joint, joint_v),
                (slope, dpre),
                (uw, uw_v),
                (qw, qw_v),
            )
        )
    ]
    for load in loads:
        load.start()
    vec[...] = jnp.zeros_like(vec)
    angle_tables(cos_v, sin_v)
    greet_all(p, me)

    order = far_order(p, a)
    parts = (op, ge)

    def rows_of(side, cc):
        return pl.ds(pl.multiple_of((side * 2 + cc) * p.tok, p.tok), p.tok)

    def send_sib(j, k):
        for side in range(X):
            src = parts[j].at[k, rows_of(side, 1 - core)]
            remote(src, from_sib.at[k, side], s_s.at[j, k], r_s.at[j, k], sib).start()

    def chip_sum(j, k):
        drain(from_sib.at[k], r_s.at[j, k])
        mine = parts[j].at[k, rows_of(far, core)]
        add_rows(mine, (mine, from_sib.at[k, far]), p.tok)
        remote(mine, from_x.at[j, k], s_x.at[j, k], r_x.at[j, k], xnb).start()
        mine = parts[j].at[k, rows_of(xh, core)]
        add_rows(mine, (mine, from_sib.at[k, xh]), p.tok)

    def hop(j, k):
        drain(from_x.at[j, k], r_x.at[j, k])
        mine = parts[j].at[k, rows_of(xh, core)]
        first = jnp.where(k > a, a == 0, a == A - 1)

        @pl.when(first)
        def _():
            add_rows(mine, (mine, from_x.at[j, k]), p.tok)

        @pl.when(jnp.logical_not(first))
        def _():
            drain(came.at[j, k], r_c.at[j, k])
            add_rows(mine, (mine, from_x.at[j, k], came.at[j, k]), p.tok)

        to = jnp.where((k < a) & (k == a - 1), A, k)
        dev = (dp + jnp.where(k > a, S, -S), c)
        remote(mine, came.at[j, to], s_c.at[j, k], r_c.at[j, to], dev).start()

    def last(j, total):
        drain(from_x.at[j, a], r_x.at[j, a])
        mine = parts[j].at[a, rows_of(xh, core)]

        @pl.when(a == 0)
        def _():
            drain(came.at[j, A], r_c.at[j, A])
            add_rows(total, (mine, from_x.at[j, a], came.at[j, A]), p.tok)

        @pl.when(a == A - 1)
        def _():
            drain(came.at[j, a], r_c.at[j, a])
            add_rows(total, (mine, from_x.at[j, a], came.at[j, a]), p.tok)

        @pl.when((a > 0) & (a < A - 1))
        def _():
            drain(came.at[j, a], r_c.at[j, a])
            drain(came.at[j, A], r_c.at[j, A])
            add_rows(
                total, (mine, from_x.at[j, a], came.at[j, a], came.at[j, A]), p.tok
            )

    def slot_rows(k):
        return pl.ds(pl.multiple_of(k * L, L), L)

    def mine_rows(k):
        return pl.ds(pl.multiple_of(lax.rem(k, half) * L, L), L)

    for k in range(3):
        loads[k].wait()

    def out_slot(i):
        k = order[i]
        own = lax.div(k, half) == core

        @pl.when(own)
        def _():
            def tile(n):
                acc = dot(hid_v[slot_rows(k), :], dw_v[0:ffl, pl.ds(n, TILE)])
                acc += dot(heads_v[mine_rows(k), :], dw_v[ffl:, pl.ds(n, TILE)])
                op[k, :, pl.ds(n, TILE)] = acc.astype(BF)

            tiles(D, tile)

        @pl.when(jnp.logical_not(own))
        def _():
            def tile(n):
                acc = dot(hid_v[slot_rows(k), :], dw_v[0:ffl, pl.ds(n, TILE)])
                op[k, :, pl.ds(n, TILE)] = acc.astype(BF)

            tiles(D, tile)

        send_sib(0, k)

    for i in range(A):
        out_slot(i)
        if i > 0:
            chip_sum(0, order[i - 1])

    chip_sum(0, order[A - 1])
    pl.semaphore_signal(free, inc=1, device_id=sib, device_id_type=MESH)

    loads[3].wait()
    loads[4].wait()
    cols = [pl.ds(j * HEAD_DIM, HEAD_DIM) for j in range(3)]
    rows2 = L // 2

    def attend_back(i, carry):
        own = pl.ds(pl.multiple_of(i * L, L), L)
        dh_v[own, :] = dot_t(ge[core * half + i], dw_v[ffl:, :]).astype(BF)
        dq, dk, dv = [], [], []
        for h in range(2):
            at = pl.ds(pl.multiple_of(i * L + h * rows2, rows2), rows2)
            keys = pl.ds(pl.multiple_of(i * L, L), (h + 1) * rows2)
            q, k, v = joint_v[at, cols[0]], joint_v[keys, cols[1]], joint_v[keys, cols[2]]
            dh = dh_v[at, :]
            probs = probabilities(q, k, h * rows2, SCALE)
            d_probs = dot_t(dh, v)
            delta = jnp.sum(probs * d_probs, axis=1, keepdims=True)
            d_scores = (probs * (d_probs - delta)).astype(BF)
            dq.append(dot(d_scores, k) * SCALE)
            dk.append(t_dot(d_scores, q) * SCALE)
            dv.append(t_dot(probs.astype(BF), dh))
        dq = jnp.concatenate(dq, axis=0)
        dk = jnp.concatenate([dk[0] + dk[1][:rows2], dk[1][rows2:]], axis=0)
        dv = jnp.concatenate([dv[0] + dv[1][:rows2], dv[1][rows2:]], axis=0)
        cos, sin = cos_v[...], sin_v[...]
        for j, d_part in enumerate((turn(dq, cos, -sin), turn(dk, cos, -sin), dv)):
            low = d_part.astype(BF)
            joint_v[own, cols[j]] = low
            sums = jnp.sum(low.astype(F32), axis=0, keepdims=True)
            for k in range(HEAD_DIM // LANES):
                at = j * (HEAD_DIM // LANES) + k
                vec[at : at + 1, :] += sums[:, k * LANES : (k + 1) * LANES]
        return carry

    lax.fori_loop(0, half, attend_back, 0)
    hop(0, order[0])

    def n_load(src, i, slot):
        count = src.shape[0]
        return pltpu.make_async_copy(
            src.at[:, pl.ds(pl.multiple_of(i * TILE, TILE), TILE)],
            n_v.at[slot, pl.ds(0, count)],
            n_sem.at[slot],
        )

    def stream(src, use):
        n_load(src, 0, 0).start()

        def step(i, carry):
            slot = lax.rem(i, 2)
            n_load(src, i, slot).wait()

            @pl.when(i + 1 < D // TILE)
            def _():
                n_load(src, i + 1, 1 - slot).start()

            use(i, slot)
            return carry

        lax.fori_loop(0, D // TILE, step, 0)

    pairs = TILE // (2 * r)

    def q_tile(i, slot):
        for j in range(3):
            acc = t_dot(n_v[slot, 0 : p.rows // 2, :], joint_v[:, cols[j]]).astype(BF)
            for k in range(pairs):
                for kk in range(2):
                    at = (2 * k + kk) * r
                    q_g[i * pairs + k, kk, :, cols[j]] = acc[at : at + r]

    stream(n1, q_tile)
    remote(q_g.at[:, 1 - core], q_sib, s_q, r_q, sib).start()

    for k in range(half):
        t_v[:, k * L : (k + 1) * L] = heads_v[k * L : (k + 1) * L, :].astype(F32).T.astype(BF)

    def o_tile(n):
        acc = dot(t_v[:, 0:L], ge[core * half, :, pl.ds(n, TILE)])
        for k in range(1, half):
            acc += dot(t_v[:, k * L : (k + 1) * L], ge[core * half + k, :, pl.ds(n, TILE)])
        acc = acc.astype(BF)
        for k in range(p.m):
            for kk in range(2):
                at = (2 * k + kk) * r
                o_g[k, kk, :, pl.ds(n, TILE)] = acc[at : at + r]

    tiles(D, o_tile)
    remote(o_g.at[:, 1 - core], o_sib, s_o, r_o, sib).start()

    loads[5].wait()
    up_row = p.hc // LANES

    def dpre_slot(k, carry):
        def tile(n):
            dh = dot_t(ge[k], dw_v[pl.ds(n, TILE), :])
            value = (dh * dpre[slot_rows(k), pl.ds(n, TILE)].astype(F32)).astype(BF)
            dpre[slot_rows(k), pl.ds(n, TILE)] = value

        tiles(ffl, tile)
        return carry

    lax.fori_loop(0, A, dpre_slot, 0)

    def sum_rows(i, carry):
        at = pl.ds(pl.multiple_of(i * 64, 64), 64)
        return carry + jnp.sum(dpre[at, :].astype(F32), axis=0, keepdims=True)

    up_bias = lax.fori_loop(0, p.rows // 64, sum_rows, jnp.zeros((1, ffl), F32))
    for i in range(ffl // LANES):
        vec[up_row + i : up_row + i + 1, :] = up_bias[:, i * LANES : (i + 1) * LANES]
    g_row = up_row + ffl // LANES
    share = D // (A * C)

    def sum_g(i, carry):
        at = pl.ds(pl.multiple_of(lax.rem(i * 64, L), 64), 64)
        part = ge[lax.div(i * 64, L), at, pl.ds(pl.multiple_of(t * share, share), share)]
        return carry + jnp.sum(part.astype(F32), axis=0, keepdims=True)

    vec[g_row : g_row + 1, :] = lax.fori_loop(
        0, p.rows // 64, sum_g, jnp.zeros((1, share), F32)
    )

    def down_units(f, carry):
        at = pl.ds(pl.multiple_of(f * TILE, TILE), TILE)
        for k in range(A):
            t_v[:, k * L : (k + 1) * L] = hid_v[k * L : (k + 1) * L, at].astype(F32).T.astype(BF)

        def tile(n):
            acc = dot(t_v[:, 0:L], ge[0, :, pl.ds(n, TILE)])
            for k in range(1, A):
                acc += dot(t_v[:, k * L : (k + 1) * L], ge[k, :, pl.ds(n, TILE)])
            dgrad[at, pl.ds(n, TILE)] = acc.astype(BF)

        tiles(D, tile)
        return carry

    lax.fori_loop(0, ffl // TILE, down_units, 0)
    d_ctx, _ = unit_home(p, b, xh, core)
    for j in range(S):
        if p.P == 1:
            own_b, own_c = j, c
        else:
            own_b, own_c = 2 * (j // 2) + core, xh * 2 + j % 2
        src = dgrad.at[pl.ds(j * R, R)]
        here = (own_b == b) & (own_c == c)

        @pl.when(jnp.logical_not(here))
        def _():
            remote(src, d_parts.at[b], s_d.at[j], r_d, (a * S + own_b, own_c)).start()

        @pl.when(here)
        def _():
            pltpu.make_async_copy(src, d_parts.at[b], r_d).start()

    hop(0, order[1])

    drain(q_sib, r_q)

    def q_add(i, carry):
        mine = q_g.at[i, core]
        add_rows(mine, (mine, q_sib.at[i]), r)
        return carry

    lax.fori_loop(0, A * S * X, q_add, 0)

    def q_rows(aa, bb):
        return q_g.at[pl.ds((aa * S + bb) * X, X), core]

    def q_cross(k, carry):
        bb = lax.rem(b + k, S)
        for aa in range(A):
            remote(q_rows(aa, bb), q_group.at[k - 1, aa], s_qb, r_qb, (a * S + bb, c)).start()
        return carry

    lax.fori_loop(1, S, q_cross, 0)
    drain(o_sib, r_o)
    for k in range(p.m):
        mine = o_g.at[k, core]
        add_rows(mine, (mine, o_sib.at[k]), r)
        owner = lax.div(head * HEAD_DIM, r) + 2 * k + core
        od, oc = lax.div(owner, C), lax.rem(owner, C)
        here = owner == me

        @pl.when(jnp.logical_not(here))
        def _():
            remote(mine, o_parts.at[b], s_oa.at[k], r_oa, (od, oc)).start()

        @pl.when(here)
        def _():
            pltpu.make_async_copy(mine, o_parts.at[b], r_oa).start()

    loads[6].wait()
    loads[7].wait()
    pl.semaphore_wait(free, 1)

    def e_slot(i):
        k = order[i]
        own = lax.div(k, half) == core

        @pl.when(own)
        def _():
            def tile(n):
                acc = dot_t(dpre[slot_rows(k), :], uw_v[pl.ds(n, TILE), :])
                acc1 = dot_t(joint_v[mine_rows(k), :], qw_v[pl.ds(n, TILE), :])
                acc = acc * gains[2:3, pl.ds(n, TILE)] + acc1 * gains[0:1, pl.ds(n, TILE)]
                ge[k, :, pl.ds(n, TILE)] = acc.astype(BF)

            tiles(D, tile)

        @pl.when(jnp.logical_not(own))
        def _():
            def tile(n):
                acc = dot_t(dpre[slot_rows(k), :], uw_v[pl.ds(n, TILE), :])
                acc = acc * gains[2:3, pl.ds(n, TILE)]
                ge[k, :, pl.ds(n, TILE)] = acc.astype(BF)

            tiles(D, tile)

        send_sib(1, k)

    for i in range(A):
        e_slot(i)
        if i > 0:
            chip_sum(1, order[i - 1])
        if i == 2:
            hop(0, order[2])
    chip_sum(1, order[A - 1])

    own_v = pltpu.make_async_copy(vec, v_all.at[me], loc.at[8])
    own_v.start()

    def v_send(k, carry):
        other = lax.rem(me + k, p.n)
        dev = (lax.div(other, C), lax.rem(other, C))
        remote(vec, v_all.at[me], s_v, r_v, dev).start()
        return carry

    lax.fori_loop(1, p.n, v_send, 0)

    for k in range(1, S):
        drain(q_group.at[k - 1], r_qb)
    for k in range(1, S):

        def q_fin(i, carry):
            aa, xx = lax.div(i, X), lax.rem(i, X)
            mine = q_g.at[(aa * S + b) * X + xx, core]
            add_rows(mine, (mine, q_group.at[k - 1, aa, xx]), r)
            return carry

        lax.fori_loop(0, A * X, q_fin, 0)

    def q_piece(hh, j):
        col = pl.multiple_of(j * D + head * HEAD_DIM, HEAD_DIM)
        at = (lax.div(hh, X) * S + b) * X + lax.rem(hh, X)
        return q_g.at[at, core, :, cols[j]], q_out.at[:, pl.ds(col, HEAD_DIM)]

    def q_back(k, carry):
        hh = lax.rem(head + k, HEADS)
        dev = (lax.div(hh, X) * S + b, lax.rem(hh, X) * 2 + core)
        for j in range(3):
            src, dst = q_piece(hh, j)
            remote(src, dst, s_qa, r_qa, dev).start()
        return carry

    lax.fori_loop(1, HEADS, q_back, 0)
    for j in range(3):
        src, dst = q_piece(head, j)
        pltpu.make_async_copy(src, dst, r_qa).start()

    def up_tile(i, slot):
        at = pl.ds(pl.multiple_of(i * TILE, TILE), TILE)
        ugrad[at, :] = t_dot(n_v[slot], dpre[...]).astype(BF)

    stream(n2, up_tile)
    blk = C * r

    def u_rows(aa, bb):
        return ugrad.at[pl.ds(pl.multiple_of((aa * S + bb) * blk, blk), blk)]

    def u_send(k, carry):
        bb = lax.rem(b + k, S)
        for aa in range(A):
            remote(u_rows(aa, bb), u_parts.at[k - 1, aa], s_u, r_u, (a * S + bb, c)).start()
        return carry

    lax.fori_loop(1, S, u_send, 0)

    hop(1, order[0])
    last(0, o_sum)

    for k in range(1, S):
        drain(u_parts.at[k - 1], r_u)
    for k in range(1, S):
        for aa in range(A):
            add_rows(u_rows(aa, b), (u_rows(aa, b), u_parts.at[k - 1, aa]), blk)

    def u_piece(tt, j):
        col = pl.multiple_of(unit_run(p, a, c, j), 128)
        aa, cc = lax.div(tt, C), lax.rem(tt, C)
        at = pl.multiple_of((aa * S + b) * blk + cc * r, r)
        return ugrad.at[pl.ds(at, r), pl.ds(j * p.W, p.W)], u_out.at[:, pl.ds(col, p.W)]

    def u_back(k, carry):
        tt = lax.rem(t + k, A * C)
        for j in range(ffl // p.W):
            src, dst = u_piece(tt, j)
            remote(src, dst, s_ua, r_ua, (lax.div(tt, C) * S + b, lax.rem(tt, C))).start()
        return carry

    lax.fori_loop(1, A * C, u_back, 0)
    for j in range(ffl // p.W):
        src, dst = u_piece(t, j)
        pltpu.make_async_copy(src, dst, r_ua).start()

    for i in range(1, A - 1):
        hop(1, order[i])
    last(1, e_sum)

    drain(u_out, r_ua)
    drain(q_out, r_qa)
    drain(v_all.at[pl.ds(0, p.n - 1)], r_v)
    drain(d_parts, r_d)
    drain(o_parts, r_oa)

    own_v.wait()
    drain(v_all.at[pl.ds(0, p.n - 1)], s_v)
    drain(q_sib, s_q)
    drain(o_sib, s_o)
    for k in range(1, S):
        drain(u_parts.at[0], s_u)
        drain(q_group.at[0], s_qb)
    for _ in range(A * C - 1):
        drain(ugrad.at[pl.ds(0, r)], s_ua)
    for _ in range(HEADS - 1):
        drain(q_g.at[0, 0], s_qa)
    for k in range(p.m):

        @pl.when(lax.div(head * HEAD_DIM, r) + 2 * k + core != me)
        def _():
            drain(o_g.at[k, 0], s_oa.at[k])

    for j in range(S):
        if p.P == 1:
            own_b, own_c = j, c
        else:
            own_b, own_c = 2 * (j // 2) + core, xh * 2 + j % 2

        @pl.when(jnp.logical_not((own_b == b) & (own_c == c)))
        def _():
            drain(d_parts.at[0], s_d.at[j])

    for j in range(2):
        for k in range(A):
            drain(from_sib.at[0], s_s.at[j, k])
            drain(from_x.at[0, 0], s_x.at[j, k])

            @pl.when(k != a)
            def _():
                drain(from_x.at[0, 0], s_c.at[j, k])


def back(p, *args):
    dma = pltpu.SemaphoreType.DMA
    A, S, C, X, r, R = p.A, p.S, p.C, p.X, p.r, p.R
    L = C * p.tok
    vm = pltpu.VMEM
    hbm = pl.BlockSpec(memory_space=pl.ANY)
    vmem = pl.BlockSpec(memory_space=pltpu.VMEM)
    groups = max(S - 1, 1)
    return pl.pallas_call(
        functools.partial(back_kernel, p),
        out_shape=(
            jax.ShapeDtypeStruct((p.tok, p.d), F32),
            jax.ShapeDtypeStruct((p.tok, p.d), F32),
            jax.ShapeDtypeStruct((r, 3 * p.d), BF),
            jax.ShapeDtypeStruct((r, p.ff), BF),
            jax.ShapeDtypeStruct((S, R, p.d), BF),
            jax.ShapeDtypeStruct((S, r, p.d), BF),
            jax.ShapeDtypeStruct((p.n, 16, 128), F32),
        ),
        in_specs=[hbm] * 10 + [vmem],
        out_specs=[vmem] * 2 + [hbm] * 5,
        scratch_shapes=[
            vm((max(p.rows, p.d), p.ffl), BF),
            vm((p.rows // 2, HEAD_DIM), BF),
            vm((p.rows, p.ffl), BF),
            vm((A, L, p.d), BF),
            vm((p.rows // 2, p.hc), BF),
            vm((p.ffl + HEAD_DIM, p.d), BF),
            vm((p.d, p.ffl), BF),
            vm((p.d, p.hc), BF),
            vm((2, p.rows, TILE), BF),
            vm((TILE, p.rows), BF),
            vm((p.rows // 2, HEAD_DIM), BF),
            vm((L, LANES), F32),
            vm((L, LANES), F32),
            vm((A, L, p.d), BF),
            vm((A, X, p.tok, p.d), BF),
            vm((2, A, p.tok, p.d), BF),
            vm((2, A + 1, p.tok, p.d), BF),
            vm((p.ffl, p.d), BF),
            vm((A * S * X, 2, r, p.hc), BF),
            vm((A * S * X, r, p.hc), BF),
            vm((groups, A, X, r, p.hc), BF),
            vm((p.m, 2, r, p.d), BF),
            vm((p.m, r, p.d), BF),
            vm((groups, A, C * r, p.ffl), BF),
            vm((16, 128), F32),
            dma((9,)),
            dma((2,)),
            dma,
            dma,
            dma((2, A)),
            dma((2, A)),
            dma((2, A)),
            dma((2, A)),
            dma((2, A)),
            dma((2, A + 1)),
            dma,
            dma,
            dma,
            dma,
            dma,
            dma,
            dma,
            dma,
            dma((p.m,)),
            dma,
            dma,
            dma,
            dma,
            dma,
            dma((S,)),
            dma,
            pltpu.SemaphoreType.REGULAR,
        ],
        compiler_params=pltpu.CompilerParams(
            collective_id=1, has_side_effects=True, vmem_limit_bytes=67043328
        ),
        name="back",
    )(*args)


def norm_stats(values):
    center = jnp.mean(values, axis=-1, keepdims=True)
    spread = jnp.mean(jnp.square(values - center), axis=-1, keepdims=True)
    inv_std = lax.rsqrt(spread + EPS)
    return (values - center) * inv_std, inv_std


def local(
    dp_size,
    ctx_size,
    layer_input,
    lengths,
    cotangent,
    qkv_weight,
    qkv_bias,
    out_weight,
    out_bias,
    up_weight,
    up_bias,
    down_weight,
    down_bias,
    first_gain,
    first_bias,
    second_gain,
    second_bias,
):
    tok, d = layer_input.shape
    ff = up_weight.shape[1]
    p = Plan(dp_size, ctx_size, tok, d, ff)
    A, S, C, X, r, R = p.A, p.S, p.C, p.X, p.r, p.R
    dp, c, a, b, xh, core = place(p)
    me = dp * C + c
    t = a * C + c
    valid = (c * tok + jnp.arange(tok, dtype=jnp.int32) < lengths[0])[:, None]
    grad_out = jnp.where(valid, cotangent, jnp.zeros_like(cotangent))
    vectors = (
        qkv_bias,
        out_bias,
        up_bias,
        down_bias,
        first_gain,
        first_bias,
        second_gain,
        second_bias,
    )
    (_, g_all, qw, dw, uw, _, n1, n2, hid, slope, heads, joint, full) = front(
        p,
        layer_input,
        cotangent,
        qkv_weight,
        out_weight,
        up_weight,
        down_weight,
        lengths,
        *(v.reshape(1, -1) for v in vectors),
    )
    o_sum, e_sum, q_out, u_out, d_parts, o_parts, v_all = back(
        p,
        hid,
        heads,
        slope,
        g_all,
        joint,
        n1,
        n2,
        dw,
        uw.reshape(d, p.ffl),
        qw.reshape(d, p.hc),
        full,
    )
    g_cols = d // (A * C)
    o_out = jnp.sum(o_parts.astype(F32), axis=0)
    d_out = jnp.sum(d_parts.astype(F32), axis=0)

    xf = layer_input.astype(F32)
    output = jnp.where(valid, xf + o_sum + full[4:5], 0.0).astype(BF)
    xhat_o, inv = norm_stats(xf)
    dx = inv * (
        e_sum
        - jnp.mean(e_sum, axis=-1, keepdims=True)
        - xhat_o * jnp.mean(e_sum * xhat_o, axis=-1, keepdims=True)
    )
    input_grad = (grad_out.astype(F32) + dx).astype(BF)

    v_all = v_all.reshape(A, S, C, 2048)
    v_sum = jnp.sum(v_all, axis=1)
    q_bias = v_sum[..., : p.hc].reshape(A, X, 2, 3, HEAD_DIM).sum(axis=2)
    q_bias = q_bias.reshape(HEADS, 3, HEAD_DIM).transpose(1, 0, 2).reshape(-1)
    u_bias = v_sum[..., p.hc : p.hc + p.ffl]
    if p.P == 1:
        u_bias = u_bias.reshape(A, C, S, R).transpose(0, 2, 1, 3).reshape(-1)
    else:
        u_bias = u_bias.reshape(A, X, 2, S // 2, p.W).transpose(0, 3, 2, 1, 4).reshape(-1)
    g_bias = v_sum[..., p.hc + p.ffl : p.hc + p.ffl + g_cols].reshape(-1)

    def own(vector):
        size = vector.shape[0] // p.n
        return lax.dynamic_slice(vector, (me * size,), (size,))

    def norm_grads(weight, grad, bias_grad, gain, shift):
        weight = weight.astype(F32)
        shift_grad = jnp.sum(weight * bias_grad, axis=1)
        gain_grad = (jnp.sum(weight * grad, axis=1) - shift.astype(F32) * shift_grad) / gain.astype(
            F32
        )
        return gain_grad, shift_grad

    q_grad = q_out.astype(F32)
    u_grad = u_out.astype(F32)
    gain1_grad, bias1_grad = norm_grads(qkv_weight, q_grad, q_bias, first_gain, first_bias)
    gain2_grad, bias2_grad = norm_grads(up_weight, u_grad, u_bias, second_gain, second_bias)
    g_own = own(g_bias)
    return (
        output,
        input_grad,
        q_grad,
        own(q_bias),
        o_out,
        g_own,
        u_grad,
        own(u_bias),
        d_out,
        g_own,
        gain1_grad,
        bias1_grad,
        gain2_grad,
        bias2_grad,
    )


def solution(mesh):
    rows = P(("dp", "ctx"), None)
    vector = P(("dp", "ctx"))
    return jax.shard_map(
        functools.partial(local, mesh.shape["dp"], mesh.shape["ctx"]),
        mesh=mesh,
        in_specs=(
            rows,
            P("dp"),
            rows,
            rows,
            vector,
            rows,
            vector,
            rows,
            vector,
            rows,
            vector,
            vector,
            vector,
            vector,
            vector,
        ),
        out_specs=(
            rows,
            rows,
            rows,
            vector,
            rows,
            vector,
            rows,
            vector,
            rows,
            vector,
            vector,
            vector,
            vector,
            vector,
        ),
        check_vma=False,
    )
```

time: 466 us -> 373 us (0.80)
  the two profiles are of different devices: /device:TPU:2 before, /device:TPU:16 now
where the time goes in v2:
time: 373 us; the launch traced here: 369 us
  Pallas kernels  348 us (93%)
  other arithmetic  12.6 us (3%)
  local copies, waits for them, and re-layouts  6.35 us (2%)
    pallas_call x1, Pallas kernels, back(): pl.pallas_call(functools.partial(back_kernel, p), out_shape=(jax.ShapeDty...  200 us
    pallas_call x1, Pallas kernels, front(): pl.pallas_call(functools.partial(front_kernel, p), out_shape=(jax.ShapeDt...  148 us

profile of v2, /device:TPU:16, one launch (start us, length us, event | category | flops | bytes accessed | tf_op | source)
XLA Modules:
  0.0 368.6 jit_solution(3180928786091846360)
XLA Ops:
  1.3 1.2 reshape.106.qkv_b
  2.5 1.2 reshape.108.up_b
  3.7 147.6 %front.1 = (bf16[4,512,2048]{2,1,0:T(8,128)(2,1)}, bf16[4,512,2048]{2,1,0:T(8,128)(2,1)}, bf16[4,2,2,2,64,768]{5,4,3,2,1,0:T(8,128)(2,1)}, bf16[768,2048]{1,0:T(...) custom-call(bf16[128,2048]{1,0:T(8,128)(2,1)} %x.1, ...), custom_call_target="tpu_custom_call" | custom-call | tf_op jit(solution)/shard_map/front/pallas_call | solution.py:673
  151.4 200.4 %back.1 = (f32[128,2048]{1,0:T(8,128)}, f32[128,2048]{1,0:T(8,128)}, bf16[64,6144]{1,0:T(8,128)(2,1)}, bf16[64,8192]{1,0:T(8,128)(2,1)}, bf16[2,256,2048]{2,1,0:...) custom-call(bf16[2048,512]{1,0:T(8,128)(2,1)} %get-tuple-element.32.hid, ...), custom_call_target="tpu_custom_call" | custom-call | tf_op jit(solution)/shard_map/back/pallas_call | solution.py:1322
  351.8 1.0 reshape.116
  352.9 0.1 reduce_sum.112
  353.0 0.0 copy-start.2
  353.0 0.0 copy-start.5
  353.0 3.5 fusion.1
  356.5 0.0 copy-start.11
  356.5 0.0 copy-start.7
  356.5 0.0 copy-start.8
  356.5 0.0 copy-start.9
  356.5 0.0 copy-start.10
  356.5 0.0 copy-start
  356.7 0.0 copy-done.2
  356.7 1.5 fusion.3
  358.3 0.0 copy-start.12
  358.3 0.0 copy-start.3
  358.3 0.5 convert_divide_fusion
  358.9 0.2 convert_reduce_fusion.1
  359.0 0.3 fusion.13
  359.3 0.3 fusion.17
  359.7 0.8 slice.12
  360.5 1.7 fusion.12
  362.2 0.0 copy-done.12
  362.2 0.6 dynamic_slice.9
  362.8 0.6 dynamic_slice.11
  363.5 0.1 dynamic_slice.10
  363.6 3.6 convert_reduce_fusion
  367.2 0.9 convert_reduce_fusion.2
  368.0 0.5 copy.36
  (28 shorter events, 0.2 us)
Async XLA Ops:
  353.0 3.7 %copy-start.2 = (bf16[64,6144]{1,0:T(8,128)(2,1)S(1)}, bf16[64,6144]{1,0:T(8,128)(2,1)}, u32[]{:S(2)}) copy-start(bf16[64,6144]{1,0:T(8,128)(2,1)} %qkv.1) | copy-start | bytes 2359300
  353.0 3.7 %copy-start.5 = (bf16[64,6144]{1,0:T(8,128)(2,1)S(1)}, bf16[64,6144]{1,0:T(8,128)(2,1)}, u32[]{:S(2)}) copy-start(bf16[64,6144]{1,0:T(8,128)(2,1)} %get-tuple-element.45) | copy-start | bytes 2359300
  356.5 2.8 copy-start.11
  356.5 1.8 copy-start.7
  356.5 1.8 copy-start.8
  356.5 1.8 copy-start.9
  356.5 1.8 copy-start.10
  356.5 2.3 copy-start
  356.7 2.6 copy-start.1
  358.3 4.0 %copy-start.12 = (f32[64]{0:T(128)}, f32[64]{0:T(128)S(1)}, u32[]{:S(2)}) copy-start(f32[64]{0:T(128)S(1)} %get-tuple-element.89) | copy-start | bytes 772
  358.3 2.3 copy-start.3
  358.3 2.3 copy-start.4
  363.6 4.5 %copy-start.13 = (f32[64]{0:T(128)}, f32[64]{0:T(128)S(1)}, u32[]{:S(2)}) copy-start(f32[64]{0:T(128)S(1)} %dynamic_slice.10) | copy-start | bytes 772
  363.6 3.6 copy-start.6

commit v3 on v2

--- a/solution.py
+++ b/solution.py
@@ -226,7 +226,14 @@
     slope_v,
     heads_v,
     joint_v,
+    ux,
+    qx,
     loc,
+    puts,
+    s_ux,
+    r_ux,
+    s_qx,
+    r_qx,
     s_sm,
     r_sm,
     s_up,
@@ -241,6 +248,7 @@
     r_qc,
     s_o,
     r_o,
+    s_ob,
     s_oc,
     r_oc,
     s_d,
@@ -296,89 +304,24 @@
     own_g = pltpu.make_async_copy(gm, ga.at[a, pl.ds(pl.multiple_of(c * p.tok, p.tok), p.tok)], loc.at[2])
     own_g.start()
 
-    def small_send(k, carry):
-        other = lax.rem(me + k, p.n)
-        dev = (lax.div(other, C), lax.rem(other, C))
-        remote(small, sm.at[me], s_sm, r_sm, dev).start()
-        return carry
-
-    lax.fori_loop(1, p.n, small_send, 0)
-
-    def up_piece(aa, cc, j):
-        col = pl.multiple_of(unit_run(p, aa, cc, j), 128)
-        return up.at[:, pl.ds(col, p.W)], uw.at[a, b, c, :, pl.ds(j * p.W, p.W)]
-
-    def up_send(k, carry):
-        tt = lax.rem(t + k, A * C)
-        aa, cc = lax.div(tt, C), lax.rem(tt, C)
-        for j in range(p.ffl // p.W):
-            src, dst = up_piece(aa, cc, j)
-            remote(src, dst, s_up, r_up, (aa * S + b, cc)).start()
-        return carry
-
-    lax.fori_loop(1, A * C, up_send, 0)
-    for j in range(p.ffl // p.W):
-        src, dst = up_piece(a, c, j)
-        pltpu.make_async_copy(src, dst, r_up).start()
-
-    def q_piece(hh, j):
-        col = pl.multiple_of(j * p.d + hh * HEAD_DIM, HEAD_DIM)
-        return (
-            qkv.at[:, pl.ds(col, HEAD_DIM)],
-            qw.at[a, b, xh, core, :, pl.ds(j * HEAD_DIM, HEAD_DIM)],
-        )
-
-    def q_send(k, carry):
-        hh = lax.rem(head + k, HEADS)
-        for j in range(3):
-            src, dst = q_piece(hh, j)
-            dev = (lax.div(hh, p.X) * S + b, lax.rem(hh, p.X) * 2 + core)
-            remote(src, dst, s_q, r_q, dev).start()
-        return carry
-
-    lax.fori_loop(1, HEADS, q_send, 0)
-    for j in range(3):
-        src, dst = q_piece(head, j)
-        pltpu.make_async_copy(src, dst, r_q).start()
-
     row_head = lax.div(me * r, HEAD_DIM)
     row_part = lax.div(lax.rem(me * r, HEAD_DIM), 2 * r)
-    o_dst = dw.at[pl.ds(pl.multiple_of(p.ffl + (row_part * 2 + core) * r, r), r)]
-
-    def o_dev(bb):
-        return lax.div(row_head, p.X) * S + bb, lax.rem(row_head, p.X) * 2 + core
-
-    for bb in range(S):
-        od, oc = o_dev(bb)
-        here = (od == dp) & (oc == c)
-
-        @pl.when(jnp.logical_not(here))
-        def _():
-            remote(outw, o_dst, s_o.at[bb], r_o, (od, oc)).start()
-
-        @pl.when(here)
-        def _():
-            pltpu.make_async_copy(outw, o_dst, r_o).start()
-
-    d_ctx, d_row = unit_home(p, b, xh, core)
-    d_dst = dw.at[pl.ds(pl.multiple_of(d_row, R), R)]
-    for bb in range(S):
-        here = (bb == b) & (d_ctx == c)
-
-        @pl.when(jnp.logical_not(here))
-        def _():
-            remote(down, d_dst, s_d.at[bb], r_d, (a * S + bb, d_ctx)).start()
-
-        @pl.when(here)
-        def _():
-            pltpu.make_async_copy(down, d_dst, r_d).start()
+    o_dp, o_ctx = lax.div(row_head, p.X) * S + b, lax.rem(row_head, p.X) * 2 + core
+    o_here = (o_dp == dp) & (o_ctx == c)
+
+    def o_rows(k, cc):
+        return dw.at[pl.ds(pl.multiple_of(p.ffl + (2 * k + cc) * r, r), r)]
+
+    def o_first(k):
+        owner = lax.div(head * HEAD_DIM, r) + 2 * k + core
+        return lax.rem(lax.div(owner, C), S) == b
 
     streams = ((x, xa), (gm, ga))
 
     def blk(j, k, cc):
         return streams[j][1].at[k, pl.ds(pl.multiple_of(cc * p.tok, p.tok), p.tok)]
 
-    def send_own(j):
+    def send_z(j):
         own, slot = streams[j][0], blk(j, a, c)
 
         @pl.when(a < A - 1)
@@ -389,6 +332,8 @@
         def _():
             remote(own, slot, s_l.at[j, 0], r_l.at[j, 0], left).start()
 
+    def send_x(j):
+        own, slot = streams[j][0], blk(j, a, c)
         remote(own, slot, s_x.at[j, a], r_x.at[j, a], xnb).start()
         remote(own, slot, s_s.at[j, a], r_s.at[j, a], sib).start()
 
@@ -428,14 +373,186 @@
         drain(part, r_x.at[j, k])
         remote(part, part, s_s.at[j, k], r_s.at[j, k], sib).start()
 
-    send_own(0)
-    angle_tables(cos_v, sin_v)
-
-    own_small.wait()
-    drain(sm.at[pl.ds(0, p.n - 1)], r_sm)
-    get_small = pltpu.make_async_copy(sm, sm_v, loc.at[0])
-    get_small.start()
-    get_small.wait()
+    runs = p.ffl // p.W
+
+    def up_cols(aa, cc, j):
+        return up.at[:, pl.ds(pl.multiple_of(unit_run(p, aa, cc, j), LANES), p.W)]
+
+    def up_over(i, carry):
+        aa, kk = lax.div(i, 2), lax.rem(i, 2)
+        for j in range(runs):
+            dst = ux.at[aa, kk, :, pl.ds(j * p.W, p.W)]
+            remote(up_cols(aa, (1 - xh) * 2 + kk, j), dst, s_ux, r_ux, xnb).start()
+        return carry
+
+    def up_along(i, carry):
+        aa, kk = lax.rem(a + 1 + lax.div(i, 2), A), lax.rem(i, 2)
+        cc = xh * 2 + kk
+        here = (aa == a) & (kk == core)
+        for j in range(runs):
+            dst = uw.at[a, b, c, :, pl.ds(j * p.W, p.W)]
+
+            @pl.when(jnp.logical_not(here))
+            def _():
+                remote(up_cols(aa, cc, j), dst, s_up, r_up, (aa * S + b, cc)).start()
+
+            @pl.when(here)
+            def _():
+                pltpu.make_async_copy(up_cols(aa, cc, j), dst, r_up).start()
+
+        return carry
+
+    def up_onward(i, carry):
+        aa, kk = lax.rem(a + 1 + lax.div(i, 2), A), lax.rem(i, 2)
+        here = (aa == a) & (kk == core)
+        src, dst = ux.at[aa, kk], uw.at[a, b, (1 - xh) * 2 + core]
+
+        @pl.when(jnp.logical_not(here))
+        def _():
+            remote(src, dst, s_up, r_up, (aa * S + b, xh * 2 + kk)).start()
+
+        @pl.when(here)
+        def _():
+            pltpu.make_async_copy(src, dst, r_up).start()
+
+        return carry
+
+    def q_cols(aa, xx, j):
+        col = pl.multiple_of(j * p.d + (aa * p.X + xx) * HEAD_DIM, HEAD_DIM)
+        return qkv.at[:, pl.ds(col, HEAD_DIM)]
+
+    def q_over(aa, carry):
+        for j in range(3):
+            dst = qx.at[aa, :, pl.ds(j * HEAD_DIM, HEAD_DIM)]
+            remote(q_cols(aa, 1 - xh, j), dst, s_qx, r_qx, xnb).start()
+        return carry
+
+    def q_along(i, carry):
+        aa = lax.rem(a + 1 + i, A)
+        for j in range(3):
+            dst = qw.at[a, b, xh, core, :, pl.ds(j * HEAD_DIM, HEAD_DIM)]
+
+            @pl.when(aa != a)
+            def _():
+                remote(q_cols(aa, xh, j), dst, s_q, r_q, (aa * S + b, c)).start()
+
+            @pl.when(aa == a)
+            def _():
+                pltpu.make_async_copy(q_cols(aa, xh, j), dst, r_q).start()
+
+        return carry
+
+    def q_onward(i, carry):
+        aa = lax.rem(a + 1 + i, A)
+        src, dst = qx.at[aa], qw.at[a, b, 1 - xh, core]
+
+        @pl.when(aa != a)
+        def _():
+            remote(src, dst, s_q, r_q, (aa * S + b, c)).start()
+
+        @pl.when(aa == a)
+        def _():
+            pltpu.make_async_copy(src, dst, r_q).start()
+
+        return carry
+
+    def up_cross(k, carry):
+        bb = lax.rem(b + k, S)
+        remote(uw.at[:, b], uw.at[:, b], s_upb, r_upb, (a * S + bb, c)).start()
+        return carry
+
+    def q_cross(k, carry):
+        bb = lax.rem(b + k, S)
+        part = qw.at[:, b, :, core]
+        remote(part, part, s_qb, r_qb, (a * S + bb, c)).start()
+        return carry
+
+    def slot_rows(k):
+        return pl.ds(pl.multiple_of(k * L, L), L)
+
+    near = far_order(p, a)[::-1]
+
+    def norm_slot(i):
+        k = near[i]
+        drain(xa.at[k, pl.ds(0, p.X * p.tok)], r_s.at[0, k])
+        get = pltpu.make_async_copy(xa.at[k], xs, loc.at[3])
+        get.start()
+        get.wait()
+        mine = lax.div(k, half) == core
+        step = 32
+
+        def unit_rows(at):
+            rows = xs[pl.ds(at, step), :].astype(F32)
+            rows = rows - jnp.mean(rows, axis=1, keepdims=True)
+            spread = jnp.mean(rows * rows, axis=1, keepdims=True)
+            rows = rows * lax.rsqrt(spread + EPS)
+            to = pl.multiple_of(k * L + at, step)
+            n2_v[pl.ds(to, step), :] = (rows * vecs[2:3, :] + vecs[3:4, :]).astype(BF)
+            return rows
+
+        @pl.when(mine)
+        def _():
+            def both(at):
+                rows = unit_rows(at)
+                to = pl.multiple_of(lax.rem(k, half) * L + at, step)
+                n1_v[pl.ds(to, step), :] = (rows * vecs[0:1, :] + vecs[1:2, :]).astype(BF)
+
+            tiles(L, both, step)
+
+        @pl.when(jnp.logical_not(mine))
+        def _():
+            def one(at):
+                unit_rows(at)
+
+            tiles(L, one, step)
+
+        pltpu.make_async_copy(n2_v.at[slot_rows(k)], n2.at[slot_rows(k)], puts.at[i]).start()
+
+    def units(i):
+        k = near[i]
+
+        def unit_tile(n):
+            at = pl.ds(n, TILE)
+            w = uw_v[:, :, :, :, at].reshape(p.d, TILE)
+            v = dot(n2_v[slot_rows(k), :], w) + ub[:, at]
+            phi = 0.5 * (1.0 + lax.erf(v * (1.0 / math.sqrt(2.0))))
+            density = jnp.exp(-0.5 * v * v) * (1.0 / math.sqrt(2.0 * math.pi))
+            hid_v[slot_rows(k), at] = (v * phi).astype(BF)
+            slope_v[slot_rows(k), at] = (phi + v * density).astype(BF)
+
+        tiles(p.ffl, unit_tile)
+
+    d_ctx, d_row = unit_home(p, b, xh, core)
+    d_dst = dw.at[pl.ds(pl.multiple_of(d_row, R), R)]
+    def small_all():
+        def small_send(k, carry):
+            other = lax.rem(me + k, p.n)
+            dev = (lax.div(other, C), lax.rem(other, C))
+            remote(small, sm.at[me], s_sm, r_sm, dev).start()
+            return carry
+
+        lax.fori_loop(1, p.n, small_send, 0)
+
+    def down_all():
+        for bb in range(S):
+            here = (bb == b) & (d_ctx == c)
+
+            @pl.when(jnp.logical_not(here))
+            def _():
+                remote(down, d_dst, s_d.at[bb], r_d, (a * S + bb, d_ctx)).start()
+
+            @pl.when(here)
+            def _():
+                pltpu.make_async_copy(down, d_dst, r_d).start()
+
+    def out_send():
+        @pl.when(jnp.logical_not(o_here))
+        def _():
+            remote(outw, o_rows(row_part, core), s_o, r_o.at[row_part], (o_dp, o_ctx)).start()
+
+        @pl.when(o_here)
+        def _():
+            pltpu.make_async_copy(outw, o_rows(row_part, core), r_o.at[row_part]).start()
 
     def chunk(which, jj):
         size = vectors[which].shape[1]
@@ -454,129 +571,63 @@
             total = total + good * sm_v[jnp.minimum(i, p.n - 1), pl.ds(at, 1), :]
         return total
 
-    def fill(jj, carry):
-        for k in range(5):
-            vecs[k : k + 1, pl.ds(pl.multiple_of(jj * LANES, LANES), LANES)] = chunk(2 + k, jj)
-        return carry
-
-    lax.fori_loop(0, p.d // LANES, fill, 0)
-    for j in range(p.ffl // LANES):
-        run, rest = j * LANES // p.W, (j * LANES % p.W) // LANES
-        first = lax.div(unit_run(p, a, c, run), LANES) + rest
-        ub[:, j * LANES : (j + 1) * LANES] = chunk(1, first)
-    for j in range(3):
-        for k in range(HEAD_DIM // LANES):
-            first = (j * p.d + head * HEAD_DIM) // LANES + k
-            at = j * HEAD_DIM + k * LANES
-            qb[:, at : at + LANES] = chunk(0, first)
-
-    drain(uw.at[:, b], r_up)
-
-    def up_cross(k, carry):
-        bb = lax.rem(b + k, S)
-        remote(uw.at[:, b], uw.at[:, b], s_upb, r_upb, (a * S + bb, c)).start()
-        return carry
-
-    lax.fori_loop(1, S, up_cross, 0)
-    drain(qw.at[:, b, :, core], r_q)
-
-    def q_cross(k, carry):
-        bb = lax.rem(b + k, S)
-        part = qw.at[:, b, :, core]
-        remote(part, part, s_qb, r_qb, (a * S + bb, c)).start()
-        return carry
-
-    lax.fori_loop(1, S, q_cross, 0)
-    drain(dw.at[pl.ds(p.ffl, p.m * r)], r_o)
-    for k in range(p.m):
-        rows = dw.at[pl.ds(pl.multiple_of(p.ffl + (2 * k + core) * r, r), r)]
-        remote(rows, rows, s_oc.at[k], r_oc.at[k], sib).start()
-
-    near = far_order(p, a)[::-1]
-
-    def slot_rows(k):
-        return pl.ds(pl.multiple_of(k * L, L), L)
-
-    def forward_slot(k):
-        get = pltpu.make_async_copy(xa.at[k], xs, loc.at[3])
+    def vectors_whole():
+        own_small.wait()
+        drain(sm.at[pl.ds(0, p.n - 1)], r_sm)
+        get_small = pltpu.make_async_copy(sm, sm_v, loc.at[0])
+        get_small.start()
+        get_small.wait()
+
+        def fill(jj, carry):
+            for k in range(5):
+                vecs[k : k + 1, pl.ds(pl.multiple_of(jj * LANES, LANES), LANES)] = chunk(2 + k, jj)
+            return carry
+
+        lax.fori_loop(0, p.d // LANES, fill, 0)
+        for j in range(p.ffl // LANES):
+            run, rest = j * LANES // p.W, (j * LANES % p.W) // LANES
+            first = lax.div(unit_run(p, a, c, run), LANES) + rest
+            ub[:, j * LANES : (j + 1) * LANES] = chunk(1, first)
+        for j in range(3):
+            for k in range(HEAD_DIM // LANES):
+                first = (j * p.d + head * HEAD_DIM) // LANES + k
+                at = j * HEAD_DIM + k * LANES
+                qb[:, at : at + LANES] = chunk(0, first)
+
+    def out_onward():
+        for k in range(p.m):
+            drain(o_rows(k, core), r_o.at[k])
+
+            @pl.when(o_first(k))
+            def _():
+                def o_cross(kk, carry):
+                    bb = lax.rem(b + kk, S)
+                    rows = o_rows(k, core)
+                    remote(rows, rows, s_ob.at[k], r_o.at[k], (a * S + bb, c)).start()
+                    return carry
+
+                lax.fori_loop(1, S, o_cross, 0)
+
+            remote(o_rows(k, core), o_rows(k, core), s_oc.at[k], r_oc.at[k], sib).start()
+
+    def load_uw():
+        for _ in range(S - 1):
+            drain(uw.at[:, b], r_upb)
+        get = pltpu.make_async_copy(uw, uw_v, loc.at[3])
         get.start()
         get.wait()
-        mine = lax.div(k, half) == core
-
-        def norm(at):
-            rows = xs[pl.ds(at, 16), :].astype(F32)
-            center = jnp.mean(rows, axis=1, keepdims=True)
-            rows = rows - center
-            spread = jnp.mean(rows * rows, axis=1, keepdims=True)
-            rows = rows * lax.rsqrt(spread + EPS)
-            n2_v[pl.ds(at, 16), :] = (rows * vecs[2:3, :] + vecs[3:4, :]).astype(BF)
-
-            @pl.when(mine)
-            def _():
-                own_at = pl.multiple_of(lax.rem(k, half) * L + at, 16)
-                n1_v[pl.ds(own_at, 16), :] = (rows * vecs[0:1, :] + vecs[1:2, :]).astype(BF)
-
-        tiles(L, norm, 16)
-        put = pltpu.make_async_copy(n2_v, n2.at[slot_rows(k)], loc.at[4])
-        put.start()
-
-        def unit_tile(n):
-            at = pl.ds(n, TILE)
-            w = uw_v[:, :, :, :, at].reshape(p.d, TILE)
-            v = dot(n2_v[...], w) + ub[:, at]
-            phi = 0.5 * (1.0 + lax.erf(v * (1.0 / math.sqrt(2.0))))
-            density = jnp.exp(-0.5 * v * v) * (1.0 / math.sqrt(2.0 * math.pi))
-            hid_v[slot_rows(k), at] = (v * phi).astype(BF)
-            slope_v[slot_rows(k), at] = (phi + v * density).astype(BF)
-
-        tiles(p.ffl, unit_tile)
-        put.wait()
-
-    def x_round(i, carry):
-        k = pick(near, i)
-
-        @pl.when(i < A - 1)
-        def _():
-            z_step(0, i)
-
-        cross(0, k)
-
-        @pl.when(i == 0)
-        def _():
-            send_own(1)
-            own_x.wait()
-            for _ in range(S - 1):
-                drain(uw.at[:, b], r_upb)
-            get = pltpu.make_async_copy(uw, uw_v, loc.at[3])
-            get.start()
-            for _ in range(S - 1):
-                drain(qw.at[:, b, :, core], r_qb)
-            part = qw.at[:, :, :, core]
-            remote(part, part, s_qc, r_qc, sib).start()
-            get.wait()
-
-        drain(xa.at[k, pl.ds(0, p.X * p.tok)], r_s.at[0, k])
-        forward_slot(k)
-
-        @pl.when(i > 0)
-        def _():
-            z_step(1, i - 1)
-
-        return carry
-
-    lax.fori_loop(0, A, x_round, 0)
-    put_hid = pltpu.make_async_copy(hid_v, hid, loc.at[4])
-    put_hid.start()
-    put_slope = pltpu.make_async_copy(slope_v, slope, loc.at[5])
-    put_slope.start()
-    put_n1 = pltpu.make_async_copy(n1_v, n1, loc.at[6])
-    put_n1.start()
-    put_rows = pltpu.make_async_copy(vecs, rows_out, loc.at[7])
-    put_rows.start()
-    drain(qw.at[:, :, :, 1 - core], r_qc)
-    get_qw = pltpu.make_async_copy(qw, qw_v, loc.at[3])
-    get_qw.start()
-    get_qw.wait()
+
+    def send_half_qw():
+        for _ in range(S - 1):
+            drain(qw.at[:, b, :, core], r_qb)
+        part = qw.at[:, :, :, core]
+        remote(part, part, s_qc, r_qc, sib).start()
+
+    def load_qw():
+        drain(qw.at[:, :, :, 1 - core], r_qc)
+        get = pltpu.make_async_copy(qw, qw_v, loc.at[3])
+        get.start()
+        get.wait()
 
     def attend(i):
         own = pl.ds(pl.multiple_of(i * L, L), L)
@@ -594,16 +645,65 @@
             probs = probabilities(joint_v[at, cols[0]], joint_v[keys, cols[1]], h * rows, SCALE)
             heads_v[at, :] = dot(probs.astype(BF), joint_v[keys, cols[2]]).astype(BF)
 
-    def g_round(i, carry):
-        cross(1, pick(near, i))
-
-        @pl.when(i < half)
-        def _():
-            attend(i)
-
-        return carry
-
-    lax.fori_loop(0, A, g_round, 0)
+    send_z(0)
+    send_x(0)
+    small_all()
+    lax.fori_loop(0, 2 * A, up_over, 0)
+    angle_tables(cos_v, sin_v)
+    z_step(0, 0)
+    cross(0, near[0])
+    lax.fori_loop(0, 2 * A, up_along, 0)
+    z_step(0, 1)
+    drain(ux, r_ux)
+    lax.fori_loop(0, 2 * A, up_onward, 0)
+    down_all()
+    cross(0, near[1])
+    vectors_whole()
+    own_x.wait()
+    norm_slot(0)
+    lax.fori_loop(0, A, q_over, 0)
+    send_x(1)
+    out_send()
+    norm_slot(1)
+    lax.fori_loop(0, A, q_along, 0)
+    cross(0, near[2])
+    send_z(1)
+    norm_slot(2)
+    drain(uw.at[:, b], r_up)
+    lax.fori_loop(1, S, up_cross, 0)
+    drain(qx, r_qx)
+    lax.fori_loop(0, A, q_onward, 0)
+    z_step(0, 2)
+    cross(1, near[0])
+    z_step(1, 0)
+    out_onward()
+    load_uw()
+    drain(qw.at[:, b, :, core], r_q)
+    lax.fori_loop(1, S, q_cross, 0)
+    cross(1, near[1])
+    z_step(1, 1)
+    units(0)
+    cross(0, near[3])
+    units(1)
+    send_half_qw()
+    norm_slot(3)
+    put_n1 = pltpu.make_async_copy(n1_v, n1, loc.at[6])
+    put_n1.start()
+    put_rows = pltpu.make_async_copy(vecs, rows_out, loc.at[7])
+    put_rows.start()
+    z_step(1, 2)
+    units(2)
+    load_qw()
+    attend(0)
+    units(3)
+    put_hid = pltpu.make_async_copy(hid_v, hid, loc.at[4])
+    put_hid.start()
+    put_slope = pltpu.make_async_copy(slope_v, slope, loc.at[5])
+    put_slope.start()
+    cross(1, near[2])
+    attend(1)
+    cross(1, near[3])
+
     put_heads = pltpu.make_async_copy(heads_v, heads, loc.at[0])
     put_heads.start()
     put_joint = pltpu.make_async_copy(joint_v, joint, loc.at[1])
@@ -622,21 +722,31 @@
     put_rows.wait()
     put_heads.wait()
     put_joint.wait()
+    for i in range(A):
+        drain(n2_v.at[pl.ds(0, L)], puts.at[i])
     drain(sm.at[pl.ds(0, p.n - 1)], s_sm)
-    for _ in range(A * C - 1):
+    drain(ux, s_ux)
+    drain(qx, s_qx)
+    for _ in range(4 * A - 2):
         drain(uw.at[a, b, c], s_up)
-    for _ in range(HEADS - 1):
+    for _ in range(2 * A - 2):
         drain(qw.at[a, b, xh, core], s_q)
     for bb in range(S):
-        od, oc = o_dev(bb)
-
-        @pl.when(jnp.logical_not((od == dp) & (oc == c)))
-        def _():
-            drain(outw, s_o.at[bb])
 
         @pl.when(jnp.logical_not((bb == b) & (d_ctx == c)))
         def _():
             drain(down, s_d.at[bb])
+
+    @pl.when(jnp.logical_not(o_here))
+    def _():
+        drain(outw, s_o)
+
+    for k in range(p.m):
+
+        @pl.when(o_first(k))
+        def _():
+            for _ in range(S - 1):
+                drain(outw, s_ob.at[k])
 
     for k in range(p.m):
         drain(dw.at[pl.ds(0, r)], s_oc.at[k])
@@ -703,26 +813,34 @@
             vm(qw_shape, BF),
             vm((L, p.d), BF),
             vm((half, p.d), BF),
-            vm((L, p.d), BF),
+            vm((p.rows, p.d), BF),
             vm((p.rows, p.ffl), BF),
             vm((p.rows, p.ffl), BF),
             vm((half, HEAD_DIM), BF),
             vm((half, p.hc), BF),
+            vm((A, 2, r, p.ffl), BF),
+            vm((A, r, p.hc), BF),
             dma((8,)),
-            dma,
-            dma,
-            dma,
-            dma,
-            dma,
-            dma,
-            dma,
-            dma,
-            dma,
-            dma,
-            dma,
-            dma,
-            dma((S,)),
-            dma,
+            dma((A,)),
+            dma,
+            dma,
+            dma,
+            dma,
+            dma,
+            dma,
+            dma,
+            dma,
+            dma,
+            dma,
+            dma,
+            dma,
+            dma,
+            dma,
+            dma,
+            dma,
+            dma,
+            dma((p.m,)),
+            dma((p.m,)),
             dma((p.m,)),
             dma((p.m,)),
             dma((S,)),
@@ -950,6 +1068,115 @@
     pl.semaphore_signal(free, inc=1, device_id=sib, device_id_type=MESH)
 
     loads[3].wait()
+    loads[5].wait()
+    up_row = p.hc // LANES
+
+    def dpre_slot(k, carry):
+        def tile(n):
+            dh = dot_t(ge[k], dw_v[pl.ds(n, TILE), :])
+            value = (dh * dpre[slot_rows(k), pl.ds(n, TILE)].astype(F32)).astype(BF)
+            dpre[slot_rows(k), pl.ds(n, TILE)] = value
+
+        tiles(ffl, tile)
+        return carry
+
+    lax.fori_loop(0, A, dpre_slot, 0)
+
+    def sum_rows(i, carry):
+        at = pl.ds(pl.multiple_of(i * 64, 64), 64)
+        return carry + jnp.sum(dpre[at, :].astype(F32), axis=0, keepdims=True)
+
+    up_bias = lax.fori_loop(0, p.rows // 64, sum_rows, jnp.zeros((1, ffl), F32))
+    for i in range(ffl // LANES):
+        vec[up_row + i : up_row + i + 1, :] = up_bias[:, i * LANES : (i + 1) * LANES]
+    g_row = up_row + ffl // LANES
+    share = D // (A * C)
+
+    def sum_g(i, carry):
+        at = pl.ds(pl.multiple_of(lax.rem(i * 64, L), 64), 64)
+        part = ge[lax.div(i * 64, L), at, pl.ds(pl.multiple_of(t * share, share), share)]
+        return carry + jnp.sum(part.astype(F32), axis=0, keepdims=True)
+
+    vec[g_row : g_row + 1, :] = lax.fori_loop(
+        0, p.rows // 64, sum_g, jnp.zeros((1, share), F32)
+    )
+
+    def down_units(f, carry):
+        at = pl.ds(pl.multiple_of(f * TILE, TILE), TILE)
+        for k in range(A):
+            t_v[:, k * L : (k + 1) * L] = hid_v[k * L : (k + 1) * L, at].astype(F32).T.astype(BF)
+
+        def tile(n):
+            acc = dot(t_v[:, 0:L], ge[0, :, pl.ds(n, TILE)])
+            for k in range(1, A):
+                acc += dot(t_v[:, k * L : (k + 1) * L], ge[k, :, pl.ds(n, TILE)])
+            dgrad[at, pl.ds(n, TILE)] = acc.astype(BF)
+
+        tiles(D, tile)
+        return carry
+
+    lax.fori_loop(0, ffl // TILE, down_units, 0)
+    d_ctx, _ = unit_home(p, b, xh, core)
+    for j in range(S):
+        if p.P == 1:
+            own_b, own_c = j, c
+        else:
+            own_b, own_c = 2 * (j // 2) + core, xh * 2 + j % 2
+        src = dgrad.at[pl.ds(j * R, R)]
+        here = (own_b == b) & (own_c == c)
+
+        @pl.when(jnp.logical_not(here))
+        def _():
+            remote(src, d_parts.at[b], s_d.at[j], r_d, (a * S + own_b, own_c)).start()
+
+        @pl.when(here)
+        def _():
+            pltpu.make_async_copy(src, d_parts.at[b], r_d).start()
+
+    def n_load(src, i, slot):
+        count = src.shape[0]
+        return pltpu.make_async_copy(
+            src.at[:, pl.ds(pl.multiple_of(i * TILE, TILE), TILE)],
+            n_v.at[slot, pl.ds(0, count)],
+            n_sem.at[slot],
+        )
+
+    def stream(src, use):
+        n_load(src, 0, 0).start()
+
+        def step(i, carry):
+            slot = lax.rem(i, 2)
+            n_load(src, i, slot).wait()
+
+            @pl.when(i + 1 < D // TILE)
+            def _():
+                n_load(src, i + 1, 1 - slot).start()
+
+            use(i, slot)
+            return carry
+
+        lax.fori_loop(0, D // TILE, step, 0)
+
+    def up_tile(i, slot):
+        at = pl.ds(pl.multiple_of(i * TILE, TILE), TILE)
+        ugrad[at, :] = t_dot(n_v[slot], dpre[...]).astype(BF)
+
+    stream(n2, up_tile)
+    blk = C * r
+
+    def u_rows(aa, bb):
+        return ugrad.at[pl.ds(pl.multiple_of((aa * S + bb) * blk, blk), blk)]
+
+    def u_send(k, carry):
+        bb = lax.rem(b + k, S)
+        for aa in range(A):
+            remote(u_rows(aa, bb), u_parts.at[k - 1, aa], s_u, r_u, (a * S + bb, c)).start()
+        return carry
+
+    lax.fori_loop(1, S, u_send, 0)
+
+    hop(0, order[0])
+
     loads[4].wait()
     cols = [pl.ds(j * HEAD_DIM, HEAD_DIM) for j in range(3)]
     rows2 = L // 2
@@ -984,45 +1211,6 @@
         return carry
 
     lax.fori_loop(0, half, attend_back, 0)
-    hop(0, order[0])
-
-    def n_load(src, i, slot):
-        count = src.shape[0]
-        return pltpu.make_async_copy(
-            src.at[:, pl.ds(pl.multiple_of(i * TILE, TILE), TILE)],
-            n_v.at[slot, pl.ds(0, count)],
-            n_sem.at[slot],
-        )
-
-    def stream(src, use):
-        n_load(src, 0, 0).start()
-
-        def step(i, carry):
-            slot = lax.rem(i, 2)
-            n_load(src, i, slot).wait()
-
-            @pl.when(i + 1 < D // TILE)
-            def _():
-                n_load(src, i + 1, 1 - slot).start()
-
-            use(i, slot)
-            return carry
-
-        lax.fori_loop(0, D // TILE, step, 0)
-
-    pairs = TILE // (2 * r)
-
-    def q_tile(i, slot):
-        for j in range(3):
-            acc = t_dot(n_v[slot, 0 : p.rows // 2, :], joint_v[:, cols[j]]).astype(BF)
-            for k in range(pairs):
-                for kk in range(2):
-                    at = (2 * k + kk) * r
-                    q_g[i * pairs + k, kk, :, cols[j]] = acc[at : at + r]
-
-    stream(n1, q_tile)
-    remote(q_g.at[:, 1 - core], q_sib, s_q, r_q, sib).start()
-
     for k in range(half):
         t_v[:, k * L : (k + 1) * L] = heads_v[k * L : (k + 1) * L, :].astype(F32).T.astype(BF)
 
@@ -1039,72 +1227,81 @@
     tiles(D, o_tile)
     remote(o_g.at[:, 1 - core], o_sib, s_o, r_o, sib).start()
 
-    loads[5].wait()
-    up_row = p.hc // LANES
-
-    def dpre_slot(k, carry):
-        def tile(n):
-            dh = dot_t(ge[k], dw_v[pl.ds(n, TILE), :])
-            value = (dh * dpre[slot_rows(k), pl.ds(n, TILE)].astype(F32)).astype(BF)
-            dpre[slot_rows(k), pl.ds(n, TILE)] = value
-
-        tiles(ffl, tile)
-        return carry
-
-    lax.fori_loop(0, A, dpre_slot, 0)
-
-    def sum_rows(i, carry):
-        at = pl.ds(pl.multiple_of(i * 64, 64), 64)
-        return carry + jnp.sum(dpre[at, :].astype(F32), axis=0, keepdims=True)
-
-    up_bias = lax.fori_loop(0, p.rows // 64, sum_rows, jnp.zeros((1, ffl), F32))
-    for i in range(ffl // LANES):
-        vec[up_row + i : up_row + i + 1, :] = up_bias[:, i * LANES : (i + 1) * LANES]
-    g_row = up_row + ffl // LANES
-    share = D // (A * C)
-
-    def sum_g(i, carry):
-        at = pl.ds(pl.multiple_of(lax.rem(i * 64, L), 64), 64)
-        part = ge[lax.div(i * 64, L), at, pl.ds(pl.multiple_of(t * share, share), share)]
-        return carry + jnp.sum(part.astype(F32), axis=0, keepdims=True)
-
-    vec[g_row : g_row + 1, :] = lax.fori_loop(
-        0, p.rows // 64, sum_g, jnp.zeros((1, share), F32)
-    )
-
-    def down_units(f, carry):
-        at = pl.ds(pl.multiple_of(f * TILE, TILE), TILE)
-        for k in range(A):
-            t_v[:, k * L : (k + 1) * L] = hid_v[k * L : (k + 1) * L, at].astype(F32).T.astype(BF)
-
-        def tile(n):
-            acc = dot(t_v[:, 0:L], ge[0, :, pl.ds(n, TILE)])
-            for k in range(1, A):
-                acc += dot(t_v[:, k * L : (k + 1) * L], ge[k, :, pl.ds(n, TILE)])
-            dgrad[at, pl.ds(n, TILE)] = acc.astype(BF)
-
-        tiles(D, tile)
-        return carry
-
-    lax.fori_loop(0, ffl // TILE, down_units, 0)
-    d_ctx, _ = unit_home(p, b, xh, core)
-    for j in range(S):
-        if p.P == 1:
-            own_b, own_c = j, c
-        else:
-            own_b, own_c = 2 * (j // 2) + core, xh * 2 + j % 2
-        src = dgrad.at[pl.ds(j * R, R)]
-        here = (own_b == b) & (own_c == c)
-
-        @pl.when(jnp.logical_not(here))
-        def _():
-            remote(src, d_parts.at[b], s_d.at[j], r_d, (a * S + own_b, own_c)).start()
-
-        @pl.when(here)
-        def _():
-            pltpu.make_async_copy(src, d_parts.at[b], r_d).start()
-
     hop(0, order[1])
+
+    loads[6].wait()
+    loads[7].wait()
+    pl.semaphore_wait(free, 1)
+
+    def e_slot(i):
+        k = order[i]
+        own = lax.div(k, half) == core
+
+        @pl.when(own)
+        def _():
+            def tile(n):
+                acc = dot_t(dpre[slot_rows(k), :], uw_v[pl.ds(n, TILE), :])
+                acc1 = dot_t(joint_v[mine_rows(k), :], qw_v[pl.ds(n, TILE), :])
+                acc = acc * gains[2:3, pl.ds(n, TILE)] + acc1 * gains[0:1, pl.ds(n, TILE)]
+                ge[k, :, pl.ds(n, TILE)] = acc.astype(BF)
+
+            tiles(D, tile)
+
+        @pl.when(jnp.logical_not(own))
+        def _():
+            def tile(n):
+                acc = dot_t(dpre[slot_rows(k), :], uw_v[pl.ds(n, TILE), :])
+                acc = acc * gains[2:3, pl.ds(n, TILE)]
+                ge[k, :, pl.ds(n, TILE)] = acc.astype(BF)
+
+            tiles(D, tile)
+
+        send_sib(1, k)
+
+    for i in range(A):
+        e_slot(i)
+        if i > 0:
+            chip_sum(1, order[i - 1])
+        if i == 2:
+            hop(0, order[2])
+    chip_sum(1, order[A - 1])
+
+    pairs = TILE // (2 * r)
+
+    def q_tile(i, slot):
+        for j in range(3):
+            acc = t_dot(n_v[slot, 0 : p.rows // 2, :], joint_v[:, cols[j]]).astype(BF)
+            for k in range(pairs):
+                for kk in range(2):
+                    at = (2 * k + kk) * r
+                    q_g[i * pairs + k, kk, :, cols[j]] = acc[at : at + r]
+
+    stream(n1, q_tile)
+    remote(q_g.at[:, 1 - core], q_sib, s_q, r_q, sib).start()
+
+    for k in range(1, S):
+        drain(u_parts.at[k - 1], r_u)
+    for k in range(1, S):
+        for aa in range(A):
+            add_rows(u_rows(aa, b), (u_rows(aa, b), u_parts.at[k - 1, aa]), blk)
+
+    def u_piece(tt, j):
+        col = pl.multiple_of(unit_run(p, a, c, j), 128)
+        aa, cc = lax.div(tt, C), lax.rem(tt, C)
+        at = pl.multiple_of((aa * S + b) * blk + cc * r, r)
+        return ugrad.at[pl.ds(at, r), pl.ds(j * p.W, p.W)], u_out.at[:, pl.ds(col, p.W)]
+
+    def u_back(k, carry):
+        tt = lax.rem(t + k, A * C)
+        for j in range(ffl // p.W):
+            src, dst = u_piece(tt, j)
+            remote(src, dst, s_ua, r_ua, (lax.div(tt, C) * S + b, lax.rem(tt, C))).start()
+        return carry
+
+    lax.fori_loop(1, A * C, u_back, 0)
+    for j in range(ffl // p.W):
+        src, dst = u_piece(t, j)
+        pltpu.make_async_copy(src, dst, r_ua).start()
 
     drain(q_sib, r_q)
 
@@ -1141,42 +1338,7 @@
         def _():
             pltpu.make_async_copy(mine, o_parts.at[b], r_oa).start()
 
-    loads[6].wait()
-    loads[7].wait()
-    pl.semaphore_wait(free, 1)
-
-    def e_slot(i):
-        k = order[i]
-        own = lax.div(k, half) == core
-
-        @pl.when(own)
-        def _():
-            def tile(n):
-                acc = dot_t(dpre[slot_rows(k), :], uw_v[pl.ds(n, TILE), :])
-                acc1 = dot_t(joint_v[mine_rows(k), :], qw_v[pl.ds(n, TILE), :])
-                acc = acc * gains[2:3, pl.ds(n, TILE)] + acc1 * gains[0:1, pl.ds(n, TILE)]
-                ge[k, :, pl.ds(n, TILE)] = acc.astype(BF)
-
-            tiles(D, tile)
-
-        @pl.when(jnp.logical_not(own))
-        def _():
-            def tile(n):
-                acc = dot_t(dpre[slot_rows(k), :], uw_v[pl.ds(n, TILE), :])
-                acc = acc * gains[2:3, pl.ds(n, TILE)]
-                ge[k, :, pl.ds(n, TILE)] = acc.astype(BF)
-
-            tiles(D, tile)
-
-        send_sib(1, k)
-
-    for i in range(A):
-        e_slot(i)
-        if i > 0:
-            chip_sum(1, order[i - 1])
-        if i == 2:
-            hop(0, order[2])
-    chip_sum(1, order[A - 1])
+    last(0, o_sum)
 
     own_v = pltpu.make_async_copy(vec, v_all.at[me], loc.at[8])
     own_v.start()
@@ -1188,6 +1350,9 @@
         return carry
 
     lax.fori_loop(1, p.n, v_send, 0)
+
+    hop(1, order[0])
+    hop(1, order[1])
 
     for k in range(1, S):
         drain(q_group.at[k - 1], r_qb)
@@ -1219,52 +1384,7 @@
         src, dst = q_piece(head, j)
         pltpu.make_async_copy(src, dst, r_qa).start()
 
-    def up_tile(i, slot):
-        at = pl.ds(pl.multiple_of(i * TILE, TILE), TILE)
-        ugrad[at, :] = t_dot(n_v[slot], dpre[...]).astype(BF)
-
-    stream(n2, up_tile)
-    blk = C * r
-
-    def u_rows(aa, bb):
-        return ugrad.at[pl.ds(pl.multiple_of((aa * S + bb) * blk, blk), blk)]
-
-    def u_send(k, carry):
-        bb = lax.rem(b + k, S)
-        for aa in range(A):
-            remote(u_rows(aa, bb), u_parts.at[k - 1, aa], s_u, r_u, (a * S + bb, c)).start()
-        return carry
-
-    lax.fori_loop(1, S, u_send, 0)
-
-    hop(1, order[0])
-    last(0, o_sum)
-
-    for k in range(1, S):
-        drain(u_parts.at[k - 1], r_u)
-    for k in range(1, S):
-        for aa in range(A):
-            add_rows(u_rows(aa, b), (u_rows(aa, b), u_parts.at[k - 1, aa]), blk)
-
-    def u_piece(tt, j):
-        col = pl.multiple_of(unit_run(p, a, c, j), 128)
-        aa, cc = lax.div(tt, C), lax.rem(tt, C)
-        at = pl.multiple_of((aa * S + b) * blk + cc * r, r)
-        return ugrad.at[pl.ds(at, r), pl.ds(j * p.W, p.W)], u_out.at[:, pl.ds(col, p.W)]
-
-    def u_back(k, carry):
-        tt = lax.rem(t + k, A * C)
-        for j in range(ffl // p.W):
-            src, dst = u_piece(tt, j)
-            remote(src, dst, s_ua, r_ua, (lax.div(tt, C) * S + b, lax.rem(tt, C))).start()
-        return carry
-
-    lax.fori_loop(1, A * C, u_back, 0)
-    for j in range(ffl // p.W):
-        src, dst = u_piece(t, j)
-        pltpu.make_async_copy(src, dst, r_ua).start()
-
-    for i in range(1, A - 1):
+    for i in range(2, A - 1):
         hop(1, order[i])
     last(1, e_sum)
 

time: 373 us -> 337 us (0.903)
  Pallas kernels: 348 us -> 313 us
    pallas_call x1, Pallas kernels: 200 us -> 171 us  [back(): pl.pallas_call(functools.partial(back_kernel, p), out_shape=(jax.ShapeDty...]
    pallas_call x1, Pallas kernels: 148 us -> 142 us  [front(): pl.pallas_call(functools.partial(front_kernel, p), out_shape=(jax.ShapeDt...]
where the time goes in v3:
time: 337 us; the launch traced here: 333 us
  Pallas kernels  313 us (93%)
  other arithmetic  12.6 us (4%)
  local copies, waits for them, and re-layouts  6.35 us (2%)
    pallas_call x1, Pallas kernels, back(): pl.pallas_call(functools.partial(back_kernel, p), out_shape=(jax.ShapeDty...  171 us
    pallas_call x1, Pallas kernels, front(): pl.pallas_call(functools.partial(front_kernel, p), out_shape=(jax.ShapeDt...  142 us

profile of v3, /device:TPU:16, one launch (start us, length us, event | category | flops | bytes accessed | tf_op | source)
XLA Modules:
  0.0 333.0 jit_solution(10267902153444669870)
XLA Ops:
  1.3 1.2 reshape.106.qkv_b
  2.5 1.2 reshape.108.up_b
  3.7 141.7 %front.1 = (bf16[4,512,2048]{2,1,0:T(8,128)(2,1)}, bf16[4,512,2048]{2,1,0:T(8,128)(2,1)}, bf16[4,2,2,2,64,768]{5,4,3,2,1,0:T(8,128)(2,1)}, bf16[768,2048]{1,0:T(...) custom-call(bf16[128,2048]{1,0:T(8,128)(2,1)} %x.1, ...), custom_call_target="tpu_custom_call" | custom-call | tf_op jit(solution)/shard_map/front/pallas_call | solution.py:783
  145.4 170.8 %back.1 = (f32[128,2048]{1,0:T(8,128)}, f32[128,2048]{1,0:T(8,128)}, bf16[64,6144]{1,0:T(8,128)(2,1)}, bf16[64,8192]{1,0:T(8,128)(2,1)}, bf16[2,256,2048]{2,1,0:...) custom-call(bf16[2048,512]{1,0:T(8,128)(2,1)} %get-tuple-element.32.hid, ...), custom_call_target="tpu_custom_call" | custom-call | tf_op jit(solution)/shard_map/back/pallas_call | solution.py:1442
  316.2 1.0 reshape.116
  317.3 0.1 reduce_sum.112
  317.4 0.0 copy-start.2
  317.4 0.0 copy-start.5
  317.4 3.5 %fusion.1 = (f32[64]{0:T(128)S(1)}, f32[64]{0:T(128)S(1)}, f32[64,8192]{1,0:T(8,128)}) fusion(bf16[64,8192]{1,0:T(8,128)(2,1)} %up.1, f32[8192]{0:T(1024)S(1)} %bitcast.25, bf16[64,8192]{1,0:T(8,128)(2,1)} %get-tuple-element.48), kind=kLoop, calls=%fused_computation.4 | loop fusion | flops 3145600 | bytes 4227584 | tf_op jit(solution)/shard_map/reduce_sum | solution.py:1617
  320.9 0.0 copy-start.11
  320.9 0.0 copy-start.7
  320.9 0.0 copy-start.8
  320.9 0.0 copy-start.9
  321.0 0.0 copy-start.10
  321.0 0.0 copy-start
  321.1 0.0 copy-done.2
  321.1 1.5 fusion.3
  322.7 0.0 copy-start.12
  322.7 0.0 copy-start.3
  322.8 0.5 convert_divide_fusion
  323.3 0.2 convert_reduce_fusion.1
  323.4 0.3 fusion.13
  323.7 0.0 copy-done.11
  323.8 0.3 fusion.17
  324.1 0.8 slice.12
  325.0 1.7 fusion.12
  326.6 0.6 dynamic_slice.9
  327.3 0.6 dynamic_slice.11
  327.9 0.1 dynamic_slice.10
  328.0 3.6 %convert_reduce_fusion = f32[256,2048]{1,0:T(8,128)} fusion(bf16[2,256,2048]{2,1,0:T(8,128)(2,1)} %get-tuple-element.49), kind=kLoop, calls=%fused_computation | loop fusion | flops 1572864 | bytes 4194304 | tf_op jit(solution)/shard_map/reduce_sum | solution.py:1588
  331.6 0.9 convert_reduce_fusion.2
  332.5 0.5 copy.36
  (28 shorter events, 0.2 us)
Async XLA Ops:
  317.4 3.7 %copy-start.2 = (bf16[64,6144]{1,0:T(8,128)(2,1)S(1)}, bf16[64,6144]{1,0:T(8,128)(2,1)}, u32[]{:S(2)}) copy-start(bf16[64,6144]{1,0:T(8,128)(2,1)} %qkv.1) | copy-start | bytes 2359300
  317.4 3.7 %copy-start.5 = (bf16[64,6144]{1,0:T(8,128)(2,1)S(1)}, bf16[64,6144]{1,0:T(8,128)(2,1)}, u32[]{:S(2)}) copy-start(bf16[64,6144]{1,0:T(8,128)(2,1)} %get-tuple-element.45) | copy-start | bytes 2359300
  320.9 2.8 copy-start.11
  320.9 1.8 copy-start.7
  320.9 1.8 copy-start.8
  320.9 1.8 copy-start.9
  321.0 1.8 copy-start.10
  321.0 2.3 copy-start
  321.1 2.6 copy-start.1
  322.7 4.0 %copy-start.12 = (f32[64]{0:T(128)}, f32[64]{0:T(128)S(1)}, u32[]{:S(2)}) copy-start(f32[64]{0:T(128)S(1)} %get-tuple-element.89) | copy-start | bytes 772
  322.7 2.3 copy-start.3
  322.7 2.3 copy-start.4
  328.0 4.5 %copy-start.13 = (f32[64]{0:T(128)}, f32[64]{0:T(128)S(1)}, u32[]{:S(2)}) copy-start(f32[64]{0:T(128)S(1)} %dynamic_slice.10) | copy-start | bytes 772
  328.0 3.6 %copy-start.6 = (bf16[2,64,2048]{2,1,0:T(8,128)(2,1)S(1)}, bf16[2,64,2048]{2,1,0:T(8,128)(2,1)}, u32[]{:S(2)}) copy-start(bf16[2,64,2048]{2,1,0:T(8,128)(2,1)} %get-tuple-element.47) | copy-start | bytes 1572868

commit v4 on v3

--- a/solution.py
+++ b/solution.py
@@ -881,20 +881,24 @@
     d_parts,
     o_parts,
     v_all,
+    u_z,
+    q_z,
     hid_v,
     heads_v,
     dpre,
-    ge,
+    g_v,
     joint_v,
     dw_v,
     uw_v,
     qw_v,
     n_v,
-    t_v,
+    hid_t,
+    heads_t,
     dh_v,
     cos_v,
     sin_v,
-    op,
+    own,
+    to_sib,
     from_sib,
     from_x,
     came,
@@ -905,9 +909,11 @@
     o_g,
     o_sib,
     u_parts,
+    g_sum,
     vec,
     loc,
     n_sem,
+    g_sem,
     s_v,
     r_v,
     s_s,
@@ -920,6 +926,8 @@
     r_q,
     s_qb,
     r_qb,
+    s_qz,
+    r_qz,
     s_qa,
     r_qa,
     s_o,
@@ -928,6 +936,8 @@
     r_oa,
     s_u,
     r_u,
+    s_uz,
+    r_uz,
     s_ua,
     r_ua,
     s_d,
@@ -946,6 +956,7 @@
     D, ffl = p.d, p.ffl
     half = A // 2
     ugrad = hid_v
+    blk = C * r
 
     loads = [
         pltpu.make_async_copy(src, dst, loc.at[k])
@@ -954,7 +965,6 @@
                 (hid, hid_v.at[pl.ds(0, p.rows)]),
                 (dw, dw_v),
                 (heads, heads_v),
-                (g, ge),
                 (joint, joint_v),
                 (slope, dpre),
                 (uw, uw_v),
@@ -968,222 +978,165 @@
     angle_tables(cos_v, sin_v)
     greet_all(p, me)
 
-    order = far_order(p, a)
-    parts = (op, ge)
-
-    def rows_of(side, cc):
-        return pl.ds(pl.multiple_of((side * 2 + cc) * p.tok, p.tok), p.tok)
-
-    def send_sib(j, k):
+    low = a < half
+    order = [
+        jnp.where(low, A - 1, 0),
+        jnp.where(low, A - 2, 1),
+        jnp.where(low, 1 - a, A + 1 - a),
+        a,
+    ]
+    inner = (a == 1) | (a == A - 2)
+
+    def slot_rows(k):
+        return pl.ds(pl.multiple_of(k * L, L), L)
+
+    def blocks(src, base):
+        rows = []
+        for cc in (core, 1 - core):
+            for side in range(X):
+                at = pl.multiple_of(base + (side * 2 + cc) * p.tok, p.tok)
+                rows.append(src[pl.ds(at, p.tok), :])
+        return jnp.concatenate(rows, axis=0)
+
+    def keep(j, k, n, acc):
+        acc = acc.astype(BF)
         for side in range(X):
-            src = parts[j].at[k, rows_of(side, 1 - core)]
-            remote(src, from_sib.at[k, side], s_s.at[j, k], r_s.at[j, k], sib).start()
+            own[j, k, side, :, pl.ds(n, TILE)] = acc[side * p.tok : (side + 1) * p.tok]
+            to_sib[k, side, :, pl.ds(n, TILE)] = acc[
+                (X + side) * p.tok : (X + side + 1) * p.tok
+            ]
+
+    def partial(j, i):
+        k = order[i]
+        mine = lax.div(k, half) == core
+        base = pl.multiple_of(lax.rem(k, half) * L, L)
+        if j == 0 and i == 0:
+            for n in range(3):
+                loads[n].wait()
+        if j == 1:
+            if i == 0:
+                loads[5].wait()
+                loads[6].wait()
+                pl.semaphore_wait(free, 1)
+            drain(from_sib.at[k], s_s.at[0, k])
+        units = blocks(dpre if j else hid_v, k * L)
+
+        @pl.when(mine)
+        def _():
+            heads_rows = blocks(joint_v if j else heads_v, base)
+
+            def tile(n):
+                at = pl.ds(n, TILE)
+                if j == 0:
+                    acc = dot(units, dw_v[0:ffl, at]) + dot(heads_rows, dw_v[ffl:, at])
+                else:
+                    acc = dot_t(units, uw_v[at, :]) * gains[2:3, at]
+                    acc += dot_t(heads_rows, qw_v[at, :]) * gains[0:1, at]
+                keep(j, k, n, acc)
+
+            tiles(D, tile)
+
+        @pl.when(jnp.logical_not(mine))
+        def _():
+            def tile(n):
+                at = pl.ds(n, TILE)
+                if j == 0:
+                    acc = dot(units, dw_v[0:ffl, at])
+                else:
+                    acc = dot_t(units, uw_v[at, :]) * gains[2:3, at]
+                keep(j, k, n, acc)
+
+            tiles(D, tile)
+
+        remote(to_sib.at[k], from_sib.at[k], s_s.at[j, k], r_s.at[j, k], sib).start()
 
     def chip_sum(j, k):
         drain(from_sib.at[k], r_s.at[j, k])
-        mine = parts[j].at[k, rows_of(far, core)]
+        mine = own.at[j, k, far]
         add_rows(mine, (mine, from_sib.at[k, far]), p.tok)
         remote(mine, from_x.at[j, k], s_x.at[j, k], r_x.at[j, k], xnb).start()
-        mine = parts[j].at[k, rows_of(xh, core)]
+        mine = own.at[j, k, xh]
         add_rows(mine, (mine, from_sib.at[k, xh]), p.tok)
 
-    def hop(j, k):
-        drain(from_x.at[j, k], r_x.at[j, k])
-        mine = parts[j].at[k, rows_of(xh, core)]
-        first = jnp.where(k > a, a == 0, a == A - 1)
-
-        @pl.when(first)
-        def _():
-            add_rows(mine, (mine, from_x.at[j, k]), p.tok)
-
-        @pl.when(jnp.logical_not(first))
-        def _():
-            drain(came.at[j, k], r_c.at[j, k])
-            add_rows(mine, (mine, from_x.at[j, k], came.at[j, k]), p.tok)
-
-        to = jnp.where((k < a) & (k == a - 1), A, k)
-        dev = (dp + jnp.where(k > a, S, -S), c)
-        remote(mine, came.at[j, to], s_c.at[j, k], r_c.at[j, to], dev).start()
+    def hop(j, i, joins):
+        k = order[i]
+        across = i < 2
+        if joins:
+            run = inner
+        else:
+            run = jnp.logical_not(inner) if across else a >= 0
+
+        @pl.when(run)
+        def _():
+            drain(from_x.at[j, k], r_x.at[j, k])
+            mine = own.at[j, k, xh]
+            if joins:
+                drain(came.at[j, 0], r_c.at[j, lax.rem(k, 2)])
+                add_rows(mine, (mine, from_x.at[j, k], came.at[j, lax.rem(k, 2)]), p.tok)
+                to, at = k, 2
+            else:
+                add_rows(mine, (mine, from_x.at[j, k]), p.tok)
+                if across:
+                    to, at = jnp.where(a == 0, 1, A - 2), lax.rem(k, 2)
+                else:
+                    to, at = k, 3
+            dev = (to * S + b, c)
+            remote(mine, came.at[j, at], s_c.at[j, k], r_c.at[j, at], dev).start()
 
     def last(j, total):
         drain(from_x.at[j, a], r_x.at[j, a])
-        mine = parts[j].at[a, rows_of(xh, core)]
-
-        @pl.when(a == 0)
-        def _():
-            drain(came.at[j, A], r_c.at[j, A])
-            add_rows(total, (mine, from_x.at[j, a], came.at[j, A]), p.tok)
-
-        @pl.when(a == A - 1)
-        def _():
-            drain(came.at[j, a], r_c.at[j, a])
-            add_rows(total, (mine, from_x.at[j, a], came.at[j, a]), p.tok)
-
-        @pl.when((a > 0) & (a < A - 1))
-        def _():
-            drain(came.at[j, a], r_c.at[j, a])
-            drain(came.at[j, A], r_c.at[j, A])
-            add_rows(
-                total, (mine, from_x.at[j, a], came.at[j, a], came.at[j, A]), p.tok
-            )
-
-    def slot_rows(k):
-        return pl.ds(pl.multiple_of(k * L, L), L)
-
-    def mine_rows(k):
-        return pl.ds(pl.multiple_of(lax.rem(k, half) * L, L), L)
-
-    for k in range(3):
-        loads[k].wait()
-
-    def out_slot(i):
-        k = order[i]
-        own = lax.div(k, half) == core
-
-        @pl.when(own)
-        def _():
-            def tile(n):
-                acc = dot(hid_v[slot_rows(k), :], dw_v[0:ffl, pl.ds(n, TILE)])
-                acc += dot(heads_v[mine_rows(k), :], dw_v[ffl:, pl.ds(n, TILE)])
-                op[k, :, pl.ds(n, TILE)] = acc.astype(BF)
-
-            tiles(D, tile)
-
-        @pl.when(jnp.logical_not(own))
-        def _():
-            def tile(n):
-                acc = dot(hid_v[slot_rows(k), :], dw_v[0:ffl, pl.ds(n, TILE)])
-                op[k, :, pl.ds(n, TILE)] = acc.astype(BF)
-
-            tiles(D, tile)
-
-        send_sib(0, k)
-
-    for i in range(A):
-        out_slot(i)
-        if i > 0:
-            chip_sum(0, order[i - 1])
-
-    chip_sum(0, order[A - 1])
-    pl.semaphore_signal(free, inc=1, device_id=sib, device_id_type=MESH)
-
-    loads[3].wait()
-    loads[5].wait()
-    up_row = p.hc // LANES
-
-    def dpre_slot(k, carry):
-        def tile(n):
-            dh = dot_t(ge[k], dw_v[pl.ds(n, TILE), :])
-            value = (dh * dpre[slot_rows(k), pl.ds(n, TILE)].astype(F32)).astype(BF)
-            dpre[slot_rows(k), pl.ds(n, TILE)] = value
-
-        tiles(ffl, tile)
-        return carry
-
-    lax.fori_loop(0, A, dpre_slot, 0)
-
-    def sum_rows(i, carry):
-        at = pl.ds(pl.multiple_of(i * 64, 64), 64)
-        return carry + jnp.sum(dpre[at, :].astype(F32), axis=0, keepdims=True)
-
-    up_bias = lax.fori_loop(0, p.rows // 64, sum_rows, jnp.zeros((1, ffl), F32))
-    for i in range(ffl // LANES):
-        vec[up_row + i : up_row + i + 1, :] = up_bias[:, i * LANES : (i + 1) * LANES]
-    g_row = up_row + ffl // LANES
-    share = D // (A * C)
-
-    def sum_g(i, carry):
-        at = pl.ds(pl.multiple_of(lax.rem(i * 64, L), 64), 64)
-        part = ge[lax.div(i * 64, L), at, pl.ds(pl.multiple_of(t * share, share), share)]
-        return carry + jnp.sum(part.astype(F32), axis=0, keepdims=True)
-
-    vec[g_row : g_row + 1, :] = lax.fori_loop(
-        0, p.rows // 64, sum_g, jnp.zeros((1, share), F32)
-    )
-
-    def down_units(f, carry):
-        at = pl.ds(pl.multiple_of(f * TILE, TILE), TILE)
+        drain(came.at[j, 2], r_c.at[j, 2])
+        drain(came.at[j, 3], r_c.at[j, 3])
+        mine = own.at[j, a, xh]
+        add_rows(total, (mine, from_x.at[j, a], came.at[j, 2], came.at[j, 3]), p.tok)
+
+    def unit_grads():
+        loads[4].wait()
         for k in range(A):
-            t_v[:, k * L : (k + 1) * L] = hid_v[k * L : (k + 1) * L, at].astype(F32).T.astype(BF)
-
-        def tile(n):
-            acc = dot(t_v[:, 0:L], ge[0, :, pl.ds(n, TILE)])
-            for k in range(1, A):
-                acc += dot(t_v[:, k * L : (k + 1) * L], ge[k, :, pl.ds(n, TILE)])
-            dgrad[at, pl.ds(n, TILE)] = acc.astype(BF)
-
-        tiles(D, tile)
-        return carry
-
-    lax.fori_loop(0, ffl // TILE, down_units, 0)
-    d_ctx, _ = unit_home(p, b, xh, core)
-    for j in range(S):
-        if p.P == 1:
-            own_b, own_c = j, c
-        else:
-            own_b, own_c = 2 * (j // 2) + core, xh * 2 + j % 2
-        src = dgrad.at[pl.ds(j * R, R)]
-        here = (own_b == b) & (own_c == c)
-
-        @pl.when(jnp.logical_not(here))
-        def _():
-            remote(src, d_parts.at[b], s_d.at[j], r_d, (a * S + own_b, own_c)).start()
-
-        @pl.when(here)
-        def _():
-            pltpu.make_async_copy(src, d_parts.at[b], r_d).start()
-
-    def n_load(src, i, slot):
-        count = src.shape[0]
-        return pltpu.make_async_copy(
-            src.at[:, pl.ds(pl.multiple_of(i * TILE, TILE), TILE)],
-            n_v.at[slot, pl.ds(0, count)],
-            n_sem.at[slot],
-        )
-
-    def stream(src, use):
-        n_load(src, 0, 0).start()
+            rows = slice(k * L, (k + 1) * L)
+            for f in range(ffl // TILE):
+                at = slice(f * TILE, (f + 1) * TILE)
+                hid_t[at, rows] = hid_v[rows, at].astype(F32).T.astype(BF)
+        for k in range(half):
+            rows = slice(k * L, (k + 1) * L)
+            heads_t[:, rows] = heads_v[rows, :].astype(F32).T.astype(BF)
+
+        def g_load(i, slot):
+            at = pl.ds(pl.multiple_of(i * TILE, TILE), TILE)
+            return pltpu.make_async_copy(g.at[at], g_v.at[slot], g_sem.at[slot])
+
+        g_load(0, 0).start()
 
         def step(i, carry):
             slot = lax.rem(i, 2)
-            n_load(src, i, slot).wait()
-
-            @pl.when(i + 1 < D // TILE)
-            def _():
-                n_load(src, i + 1, 1 - slot).start()
-
-            use(i, slot)
+            g_load(i, slot).wait()
+
+            @pl.when(i + 1 < p.rows // TILE)
+            def _():
+                g_load(i + 1, 1 - slot).start()
+
+            rows = pl.ds(pl.multiple_of(i * TILE, TILE), TILE)
+            for f in range(ffl // TILE):
+                at = pl.ds(f * TILE, TILE)
+                d_unit = dot_t(g_v[slot], dw_v[f * TILE : (f + 1) * TILE, :])
+                dpre[rows, at] = (d_unit * dpre[rows, at].astype(F32)).astype(BF)
+            first = core * half * L
+
+            @pl.when((i * TILE >= first) & (i * TILE < first + half * L))
+            def _():
+                at = pl.ds(pl.multiple_of(i * TILE - first, TILE), TILE)
+                dh_v[at, :] = dot_t(g_v[slot], dw_v[ffl:, :]).astype(BF)
+
             return carry
 
-        lax.fori_loop(0, D // TILE, step, 0)
-
-    def up_tile(i, slot):
-        at = pl.ds(pl.multiple_of(i * TILE, TILE), TILE)
-        ugrad[at, :] = t_dot(n_v[slot], dpre[...]).astype(BF)
-
-    stream(n2, up_tile)
-    blk = C * r
-
-    def u_rows(aa, bb):
-        return ugrad.at[pl.ds(pl.multiple_of((aa * S + bb) * blk, blk), blk)]
-
-    def u_send(k, carry):
-        bb = lax.rem(b + k, S)
-        for aa in range(A):
-            remote(u_rows(aa, bb), u_parts.at[k - 1, aa], s_u, r_u, (a * S + bb, c)).start()
-        return carry
-
-    lax.fori_loop(1, S, u_send, 0)
-
-    hop(0, order[0])
-
-    loads[4].wait()
+        lax.fori_loop(0, p.rows // TILE, step, 0)
+        loads[3].wait()
+
     cols = [pl.ds(j * HEAD_DIM, HEAD_DIM) for j in range(3)]
     rows2 = L // 2
 
     def attend_back(i, carry):
-        own = pl.ds(pl.multiple_of(i * L, L), L)
-        dh_v[own, :] = dot_t(ge[core * half + i], dw_v[ffl:, :]).astype(BF)
+        rows = pl.ds(pl.multiple_of(i * L, L), L)
         dq, dk, dv = [], [], []
         for h in range(2):
             at = pl.ds(pl.multiple_of(i * L + h * rows2, rows2), rows2)
@@ -1203,68 +1156,36 @@
         cos, sin = cos_v[...], sin_v[...]
         for j, d_part in enumerate((turn(dq, cos, -sin), turn(dk, cos, -sin), dv)):
             low = d_part.astype(BF)
-            joint_v[own, cols[j]] = low
+            joint_v[rows, cols[j]] = low
             sums = jnp.sum(low.astype(F32), axis=0, keepdims=True)
             for k in range(HEAD_DIM // LANES):
                 at = j * (HEAD_DIM // LANES) + k
                 vec[at : at + 1, :] += sums[:, k * LANES : (k + 1) * LANES]
         return carry
 
-    lax.fori_loop(0, half, attend_back, 0)
-    for k in range(half):
-        t_v[:, k * L : (k + 1) * L] = heads_v[k * L : (k + 1) * L, :].astype(F32).T.astype(BF)
-
-    def o_tile(n):
-        acc = dot(t_v[:, 0:L], ge[core * half, :, pl.ds(n, TILE)])
-        for k in range(1, half):
-            acc += dot(t_v[:, k * L : (k + 1) * L], ge[core * half + k, :, pl.ds(n, TILE)])
-        acc = acc.astype(BF)
-        for k in range(p.m):
-            for kk in range(2):
-                at = (2 * k + kk) * r
-                o_g[k, kk, :, pl.ds(n, TILE)] = acc[at : at + r]
-
-    tiles(D, o_tile)
-    remote(o_g.at[:, 1 - core], o_sib, s_o, r_o, sib).start()
-
-    hop(0, order[1])
-
-    loads[6].wait()
-    loads[7].wait()
-    pl.semaphore_wait(free, 1)
-
-    def e_slot(i):
-        k = order[i]
-        own = lax.div(k, half) == core
-
-        @pl.when(own)
-        def _():
-            def tile(n):
-                acc = dot_t(dpre[slot_rows(k), :], uw_v[pl.ds(n, TILE), :])
-                acc1 = dot_t(joint_v[mine_rows(k), :], qw_v[pl.ds(n, TILE), :])
-                acc = acc * gains[2:3, pl.ds(n, TILE)] + acc1 * gains[0:1, pl.ds(n, TILE)]
-                ge[k, :, pl.ds(n, TILE)] = acc.astype(BF)
-
-            tiles(D, tile)
-
-        @pl.when(jnp.logical_not(own))
-        def _():
-            def tile(n):
-                acc = dot_t(dpre[slot_rows(k), :], uw_v[pl.ds(n, TILE), :])
-                acc = acc * gains[2:3, pl.ds(n, TILE)]
-                ge[k, :, pl.ds(n, TILE)] = acc.astype(BF)
-
-            tiles(D, tile)
-
-        send_sib(1, k)
-
-    for i in range(A):
-        e_slot(i)
-        if i > 0:
-            chip_sum(1, order[i - 1])
-        if i == 2:
-            hop(0, order[2])
-    chip_sum(1, order[A - 1])
+    def n_load(src, i, slot):
+        count = src.shape[0]
+        return pltpu.make_async_copy(
+            src.at[:, pl.ds(pl.multiple_of(i * TILE, TILE), TILE)],
+            n_v.at[slot, pl.ds(0, count)],
+            n_sem.at[slot],
+        )
+
+    def stream(src, use, low, high):
+        n_load(src, low, low % 2).start()
+
+        def step(i, carry):
+            slot = lax.rem(i, 2)
+            n_load(src, i, slot).wait()
+
+            @pl.when(i + 1 < high)
+            def _():
+                n_load(src, i + 1, 1 - slot).start()
+
+            use(i, slot)
+            return carry
+
+        lax.fori_loop(low, high, step, 0)
 
     pairs = TILE // (2 * r)
 
@@ -1276,116 +1197,238 @@
                     at = (2 * k + kk) * r
                     q_g[i * pairs + k, kk, :, cols[j]] = acc[at : at + r]
 
-    stream(n1, q_tile)
-    remote(q_g.at[:, 1 - core], q_sib, s_q, r_q, sib).start()
-
-    for k in range(1, S):
-        drain(u_parts.at[k - 1], r_u)
-    for k in range(1, S):
-        for aa in range(A):
-            add_rows(u_rows(aa, b), (u_rows(aa, b), u_parts.at[k - 1, aa]), blk)
-
-    def u_piece(tt, j):
-        col = pl.multiple_of(unit_run(p, a, c, j), 128)
-        aa, cc = lax.div(tt, C), lax.rem(tt, C)
-        at = pl.multiple_of((aa * S + b) * blk + cc * r, r)
-        return ugrad.at[pl.ds(at, r), pl.ds(j * p.W, p.W)], u_out.at[:, pl.ds(col, p.W)]
-
-    def u_back(k, carry):
-        tt = lax.rem(t + k, A * C)
-        for j in range(ffl // p.W):
-            src, dst = u_piece(tt, j)
-            remote(src, dst, s_ua, r_ua, (lax.div(tt, C) * S + b, lax.rem(tt, C))).start()
-        return carry
-
-    lax.fori_loop(1, A * C, u_back, 0)
-    for j in range(ffl // p.W):
-        src, dst = u_piece(t, j)
-        pltpu.make_async_copy(src, dst, r_ua).start()
-
-    drain(q_sib, r_q)
-
-    def q_add(i, carry):
-        mine = q_g.at[i, core]
-        add_rows(mine, (mine, q_sib.at[i]), r)
-        return carry
-
-    lax.fori_loop(0, A * S * X, q_add, 0)
+    def up_tile(i, slot):
+        at = pl.ds(pl.multiple_of(i * TILE, TILE), TILE)
+        ugrad[at, :] = t_dot(n_v[slot], dpre[...]).astype(BF)
+
+    def down_tile(i, slot):
+        at = pl.ds(pl.multiple_of(i * TILE, TILE), TILE)
+        g_sum[:, at] = jnp.sum(n_v[slot].astype(F32), axis=0, keepdims=True)
+        for f in range(ffl // TILE):
+            rows = slice(f * TILE, (f + 1) * TILE)
+            dgrad[rows, at] = dot(hid_t[rows, :], n_v[slot]).astype(BF)
+        first = pl.multiple_of(core * half * L, L)
+        acc = dot(heads_t[...], n_v[slot, pl.ds(first, half * L), :]).astype(BF)
+        for k in range(p.m):
+            for kk in range(2):
+                to = (2 * k + kk) * r
+                o_g[k, kk, :, at] = acc[to : to + r]
+
+    def down_owner(j):
+        if p.P == 1:
+            return j, c
+        return 2 * (j // 2) + core, xh * 2 + j % 2
+
+    def down_send():
+        for j in range(S):
+            own_b, own_c = down_owner(j)
+            src = dgrad.at[pl.ds(j * R, R)]
+            here = (own_b == b) & (own_c == c)
+
+            @pl.when(jnp.logical_not(here))
+            def _():
+                remote(src, d_parts.at[b], s_d.at[j], r_d, (a * S + own_b, own_c)).start()
+
+            @pl.when(here)
+            def _():
+                pltpu.make_async_copy(src, d_parts.at[b], r_d).start()
+
+        remote(o_g.at[:, 1 - core], o_sib, s_o, r_o, sib).start()
+
+    def u_rows(aa, bb):
+        return ugrad.at[pl.ds(pl.multiple_of((aa * S + bb) * blk, blk), blk)]
+
+    def up_send():
+        def one(k, carry):
+            bb = lax.rem(b + k, S)
+            for aa in range(A):
+                remote(u_rows(aa, bb), u_parts.at[k - 1, aa], s_u, r_u, (a * S + bb, c)).start()
+            return carry
+
+        lax.fori_loop(1, S, one, 0)
+
+    def up_along():
+        for k in range(1, S):
+            drain(u_parts.at[k - 1], r_u)
+        for k in range(1, S):
+
+            def add(aa, carry):
+                add_rows(u_rows(aa, b), (u_rows(aa, b), u_parts.at[k - 1, aa]), blk)
+                return carry
+
+            lax.fori_loop(0, A, add, 0)
+        for k in range(1, A):
+            aa = lax.rem(a + k, A)
+            remote(u_rows(aa, b), u_z.at[k - 1], s_uz, r_uz, (aa * S + b, c)).start()
+
+    def up_home():
+        drain(u_z, r_uz)
+        for k in range(A):
+            source = lax.rem(a - k + A, A)
+            for step in range(C):
+                cc = lax.rem(c + 1 + step, C)
+                row = pl.multiple_of(cc * r, r)
+                for j in range(ffl // p.W):
+                    at = pl.ds(j * p.W, p.W)
+                    if k == 0:
+                        src = ugrad.at[
+                            pl.ds(pl.multiple_of((a * S + b) * blk + cc * r, r), r), at
+                        ]
+                    else:
+                        src = u_z.at[k - 1, pl.ds(row, r), at]
+                    col = pl.multiple_of(unit_run(p, source, c, j), LANES)
+                    dst = u_out.at[:, pl.ds(col, p.W)]
+                    if step < C - 1:
+                        remote(src, dst, s_ua, r_ua, (dp, cc)).start()
+                    else:
+                        pltpu.make_async_copy(src, dst, r_ua).start()
 
     def q_rows(aa, bb):
         return q_g.at[pl.ds((aa * S + bb) * X, X), core]
 
-    def q_cross(k, carry):
-        bb = lax.rem(b + k, S)
-        for aa in range(A):
-            remote(q_rows(aa, bb), q_group.at[k - 1, aa], s_qb, r_qb, (a * S + bb, c)).start()
-        return carry
-
-    lax.fori_loop(1, S, q_cross, 0)
-    drain(o_sib, r_o)
-    for k in range(p.m):
-        mine = o_g.at[k, core]
-        add_rows(mine, (mine, o_sib.at[k]), r)
-        owner = lax.div(head * HEAD_DIM, r) + 2 * k + core
-        od, oc = lax.div(owner, C), lax.rem(owner, C)
-        here = owner == me
-
-        @pl.when(jnp.logical_not(here))
-        def _():
-            remote(mine, o_parts.at[b], s_oa.at[k], r_oa, (od, oc)).start()
-
-        @pl.when(here)
-        def _():
-            pltpu.make_async_copy(mine, o_parts.at[b], r_oa).start()
-
+    def q_cross():
+        drain(q_sib, r_q)
+
+        def add(i, carry):
+            mine = q_g.at[i, core]
+            add_rows(mine, (mine, q_sib.at[i]), r)
+            return carry
+
+        lax.fori_loop(0, A * S * X, add, 0)
+
+        def one(k, carry):
+            bb = lax.rem(b + k, S)
+            for aa in range(A):
+                remote(q_rows(aa, bb), q_group.at[k - 1, aa], s_qb, r_qb, (a * S + bb, c)).start()
+            return carry
+
+        lax.fori_loop(1, S, one, 0)
+
+    def q_along():
+        for k in range(1, S):
+            drain(q_group.at[k - 1], r_qb)
+        for k in range(1, S):
+
+            def add(i, carry):
+                aa, xx = lax.div(i, X), lax.rem(i, X)
+                mine = q_g.at[(aa * S + b) * X + xx, core]
+                add_rows(mine, (mine, q_group.at[k - 1, aa, xx]), r)
+                return carry
+
+            lax.fori_loop(0, A * X, add, 0)
+        for k in range(1, A):
+            aa = lax.rem(a + k, A)
+            remote(q_rows(aa, b), q_z.at[k - 1], s_qz, r_qz, (aa * S + b, c)).start()
+
+    def q_home():
+        drain(q_z, r_qz)
+        for k in range(A):
+            source = lax.rem(a - k + A, A)
+            for xx in (far, xh):
+                for j in range(3):
+                    if k == 0:
+                        src = q_g.at[(a * S + b) * X + xx, core, :, cols[j]]
+                    else:
+                        src = q_z.at[k - 1, xx, :, cols[j]]
+                    col = pl.multiple_of(j * D + (source * X + xh) * HEAD_DIM, HEAD_DIM)
+                    dst = q_out.at[:, pl.ds(col, HEAD_DIM)]
+                    if xx is far:
+                        remote(src, dst, s_qa, r_qa, xnb).start()
+                    else:
+                        pltpu.make_async_copy(src, dst, r_qa).start()
+
+    def out_owner(k):
+        return lax.div(head * HEAD_DIM, r) + 2 * k + core
+
+    def out_home():
+        drain(o_sib, r_o)
+        for k in range(p.m):
+            mine = o_g.at[k, core]
+            add_rows(mine, (mine, o_sib.at[k]), r)
+            od, oc = lax.div(out_owner(k), C), lax.rem(out_owner(k), C)
+
+            @pl.when(out_owner(k) != me)
+            def _():
+                remote(mine, o_parts.at[b], s_oa.at[k], r_oa, (od, oc)).start()
+
+            @pl.when(out_owner(k) == me)
+            def _():
+                pltpu.make_async_copy(mine, o_parts.at[b], r_oa).start()
+
+    own_v = pltpu.make_async_copy(vec, v_all.at[me], loc.at[7])
+
+    def sums_send():
+        up_row = p.hc // LANES
+
+        def sum_rows(i, carry):
+            at = pl.ds(pl.multiple_of(i * 64, 64), 64)
+            return carry + jnp.sum(dpre[at, :].astype(F32), axis=0, keepdims=True)
+
+        sums = lax.fori_loop(0, p.rows // 64, sum_rows, jnp.zeros((1, ffl), F32))
+        for i in range(ffl // LANES):
+            vec[up_row + i : up_row + i + 1, :] = sums[:, i * LANES : (i + 1) * LANES]
+        share = D // (A * C)
+        g_row = up_row + ffl // LANES
+        vec[g_row : g_row + 1, :] = g_sum[:, pl.ds(pl.multiple_of(t * share, share), share)]
+        own_v.start()
+
+        def one(k, carry):
+            other = lax.rem(me + k, p.n)
+            dev = (lax.div(other, C), lax.rem(other, C))
+            remote(vec, v_all.at[me], s_v, r_v, dev).start()
+            return carry
+
+        lax.fori_loop(1, p.n, one, 0)
+
+    def give_back():
+        pl.semaphore_signal(free, inc=1, device_id=sib, device_id_type=MESH)
+
+    partial(0, 0)
+    partial(0, 1)
+    chip_sum(0, order[0])
+    partial(0, 2)
+    chip_sum(0, order[1])
+    partial(0, 3)
+    chip_sum(0, order[2])
+    chip_sum(0, order[3])
+    give_back()
+    unit_grads()
+    hop(0, 0, False)
+    stream(n2, up_tile, 0, 4)
+    hop(0, 1, False)
+    stream(n2, up_tile, 4, 8)
+    up_send()
+    lax.fori_loop(0, half, attend_back, 0)
+    partial(1, 0)
+    partial(1, 1)
+    chip_sum(1, order[0])
+    hop(0, 0, True)
+    hop(0, 2, False)
+    partial(1, 2)
+    chip_sum(1, order[1])
+    partial(1, 3)
+    chip_sum(1, order[2])
+    hop(0, 1, True)
+    chip_sum(1, order[3])
+    up_along()
+    stream(n1, q_tile, 0, 4)
+    hop(1, 0, False)
+    stream(n1, q_tile, 4, 8)
+    remote(q_g.at[:, 1 - core], q_sib, s_q, r_q, sib).start()
+    q_cross()
+    stream(g, down_tile, 0, 4)
+    hop(1, 1, False)
     last(0, o_sum)
-
-    own_v = pltpu.make_async_copy(vec, v_all.at[me], loc.at[8])
-    own_v.start()
-
-    def v_send(k, carry):
-        other = lax.rem(me + k, p.n)
-        dev = (lax.div(other, C), lax.rem(other, C))
-        remote(vec, v_all.at[me], s_v, r_v, dev).start()
-        return carry
-
-    lax.fori_loop(1, p.n, v_send, 0)
-
-    hop(1, order[0])
-    hop(1, order[1])
-
-    for k in range(1, S):
-        drain(q_group.at[k - 1], r_qb)
-    for k in range(1, S):
-
-        def q_fin(i, carry):
-            aa, xx = lax.div(i, X), lax.rem(i, X)
-            mine = q_g.at[(aa * S + b) * X + xx, core]
-            add_rows(mine, (mine, q_group.at[k - 1, aa, xx]), r)
-            return carry
-
-        lax.fori_loop(0, A * X, q_fin, 0)
-
-    def q_piece(hh, j):
-        col = pl.multiple_of(j * D + head * HEAD_DIM, HEAD_DIM)
-        at = (lax.div(hh, X) * S + b) * X + lax.rem(hh, X)
-        return q_g.at[at, core, :, cols[j]], q_out.at[:, pl.ds(col, HEAD_DIM)]
-
-    def q_back(k, carry):
-        hh = lax.rem(head + k, HEADS)
-        dev = (lax.div(hh, X) * S + b, lax.rem(hh, X) * 2 + core)
-        for j in range(3):
-            src, dst = q_piece(hh, j)
-            remote(src, dst, s_qa, r_qa, dev).start()
-        return carry
-
-    lax.fori_loop(1, HEADS, q_back, 0)
-    for j in range(3):
-        src, dst = q_piece(head, j)
-        pltpu.make_async_copy(src, dst, r_qa).start()
-
-    for i in range(2, A - 1):
-        hop(1, order[i])
+    stream(g, down_tile, 4, 8)
+    down_send()
+    hop(1, 2, False)
+    hop(1, 0, True)
+    q_along()
+    out_home()
+    sums_send()
+    hop(1, 1, True)
+    up_home()
+    q_home()
     last(1, e_sum)
 
     drain(u_out, r_ua)
@@ -1401,29 +1444,28 @@
     for k in range(1, S):
         drain(u_parts.at[0], s_u)
         drain(q_group.at[0], s_qb)
-    for _ in range(A * C - 1):
-        drain(ugrad.at[pl.ds(0, r)], s_ua)
-    for _ in range(HEADS - 1):
+    drain(u_z, s_uz)
+    drain(q_z, s_qz)
+    for _ in range(A):
+        drain(ugrad.at[pl.ds(0, (C - 1) * r)], s_ua)
         drain(q_g.at[0, 0], s_qa)
     for k in range(p.m):
 
-        @pl.when(lax.div(head * HEAD_DIM, r) + 2 * k + core != me)
+        @pl.when(out_owner(k) != me)
         def _():
             drain(o_g.at[k, 0], s_oa.at[k])
 
     for j in range(S):
-        if p.P == 1:
-            own_b, own_c = j, c
-        else:
-            own_b, own_c = 2 * (j // 2) + core, xh * 2 + j % 2
+        own_b, own_c = down_owner(j)
 
         @pl.when(jnp.logical_not((own_b == b) & (own_c == c)))
         def _():
             drain(d_parts.at[0], s_d.at[j])
 
+    for k in range(A):
+        drain(from_sib.at[0], s_s.at[1, k])
     for j in range(2):
         for k in range(A):
-            drain(from_sib.at[0], s_s.at[j, k])
             drain(from_x.at[0, 0], s_x.at[j, k])
 
             @pl.when(k != a)
@@ -1448,28 +1490,32 @@
             jax.ShapeDtypeStruct((r, p.ff), BF),
             jax.ShapeDtypeStruct((S, R, p.d), BF),
             jax.ShapeDtypeStruct((S, r, p.d), BF),
-            jax.ShapeDtypeStruct((p.n, 16, 128), F32),
+            jax.ShapeDtypeStruct((p.n, 16, LANES), F32),
+            jax.ShapeDtypeStruct((A - 1, C * r, p.ffl), BF),
+            jax.ShapeDtypeStruct((A - 1, X, r, p.hc), BF),
         ),
         in_specs=[hbm] * 10 + [vmem],
-        out_specs=[vmem] * 2 + [hbm] * 5,
+        out_specs=[vmem] * 2 + [hbm] * 7,
         scratch_shapes=[
             vm((max(p.rows, p.d), p.ffl), BF),
             vm((p.rows // 2, HEAD_DIM), BF),
             vm((p.rows, p.ffl), BF),
-            vm((A, L, p.d), BF),
+            vm((2, TILE, p.d), BF),
             vm((p.rows // 2, p.hc), BF),
             vm((p.ffl + HEAD_DIM, p.d), BF),
             vm((p.d, p.ffl), BF),
             vm((p.d, p.hc), BF),
             vm((2, p.rows, TILE), BF),
-            vm((TILE, p.rows), BF),
+            vm((p.ffl, p.rows), BF),
+            vm((HEAD_DIM, p.rows // 2), BF),
             vm((p.rows // 2, HEAD_DIM), BF),
             vm((L, LANES), F32),
             vm((L, LANES), F32),
-            vm((A, L, p.d), BF),
+            vm((2, A, X, p.tok, p.d), BF),
+            vm((A, X, p.tok, p.d), BF),
             vm((A, X, p.tok, p.d), BF),
             vm((2, A, p.tok, p.d), BF),
-            vm((2, A + 1, p.tok, p.d), BF),
+            vm((2, 4, p.tok, p.d), BF),
             vm((p.ffl, p.d), BF),
             vm((A * S * X, 2, r, p.hc), BF),
             vm((A * S * X, r, p.hc), BF),
@@ -1477,8 +1523,10 @@
             vm((p.m, 2, r, p.d), BF),
             vm((p.m, r, p.d), BF),
             vm((groups, A, C * r, p.ffl), BF),
-            vm((16, 128), F32),
-            dma((9,)),
+            vm((1, p.d), F32),
+            vm((16, LANES), F32),
+            dma((8,)),
+            dma((2,)),
             dma((2,)),
             dma,
             dma,
@@ -1487,7 +1535,9 @@
             dma((2, A)),
             dma((2, A)),
             dma((2, A)),
-            dma((2, A + 1)),
+            dma((2, 4)),
+            dma,
+            dma,
             dma,
             dma,
             dma,
@@ -1497,6 +1547,8 @@
             dma,
             dma,
             dma((p.m,)),
+            dma,
+            dma,
             dma,
             dma,
             dma,
@@ -1569,12 +1621,12 @@
         lengths,
         *(v.reshape(1, -1) for v in vectors),
     )
-    o_sum, e_sum, q_out, u_out, d_parts, o_parts, v_all = back(
+    o_sum, e_sum, q_out, u_out, d_parts, o_parts, v_all, _, _ = back(
         p,
         hid,
         heads,
         slope,
-        g_all,
+        g_all.reshape(p.rows, d),
         joint,
         n1,
         n2,

time: 337 us -> 321 us (0.953)
  Pallas kernels: 313 us -> 295 us
    pallas_call x1, Pallas kernels: 171 us -> 154 us  [back(): pl.pallas_call(functools.partial(back_kernel, p), out_shape=(jax.ShapeDty...]
where the time goes in v4:
time: 321 us; the launch traced here: 316 us
  Pallas kernels  295 us (92%)
  other arithmetic  12.6 us (4%)
  local copies, waits for them, and re-layouts  6.35 us (2%)
    pallas_call x1, Pallas kernels, back(): pl.pallas_call(functools.partial(back_kernel, p), out_shape=(jax.ShapeDty...  154 us
    pallas_call x1, Pallas kernels, front(): pl.pallas_call(functools.partial(front_kernel, p), out_shape=(jax.ShapeDt...  142 us

profile of v4, /device:TPU:16, one launch (start us, length us, event | category | flops | bytes accessed | tf_op | source)
XLA Modules:
  0.0 315.9 jit_solution(1616582547927206068)
XLA Ops:
  1.3 1.2 reshape.109.qkv_b
  2.5 1.2 reshape.111.up_b
  3.7 141.7 %front.1 = (bf16[4,512,2048]{2,1,0:T(8,128)(2,1)}, bf16[4,512,2048]{2,1,0:T(8,128)(2,1)}, bf16[4,2,2,2,64,768]{5,4,3,2,1,0:T(8,128)(2,1)}, bf16[768,2048]{1,0:T(...) custom-call(bf16[128,2048]{1,0:T(8,128)(2,1)} %x.1, ...), custom_call_target="tpu_custom_call" | custom-call | tf_op jit(solution)/shard_map/front/pallas_call | solution.py:783
  145.4 153.7 %back.1 = (f32[128,2048]{1,0:T(8,128)}, f32[128,2048]{1,0:T(8,128)}, bf16[64,6144]{1,0:T(8,128)(2,1)}, bf16[64,8192]{1,0:T(8,128)(2,1)}, bf16[2,256,2048]{2,1,0:...) custom-call(bf16[2048,512]{1,0:T(8,128)(2,1)} %get-tuple-element.32., ...), custom_call_target="tpu_custom_call" | custom-call | tf_op jit(solution)/shard_map/back/pallas_call | solution.py:1484
  299.1 1.0 reshape.120
  300.2 0.1 reduce_sum.112
  300.3 0.0 copy-start.2
  300.3 3.5 %fusion.1 = (f32[64]{0:T(128)S(1)}, f32[64]{0:T(128)S(1)}, f32[64,8192]{1,0:T(8,128)}) fusion(bf16[64,8192]{1,0:T(8,128)(2,1)} %up.1, f32[8192]{0:T(1024)S(1)} %bitcast.27, bf16[64,8192]{1,0:T(8,128)(2,1)} %get-tuple-element.48), kind=kLoop, calls=%fused_computation.4 | loop fusion | flops 3145600 | bytes 4227584 | tf_op jit(solution)/shard_map/reduce_sum | solution.py:1669
  303.8 0.0 copy-start.11
  303.8 0.0 copy-start.7
  303.8 0.0 copy-start.8
  303.8 0.0 copy-start.9
  303.8 0.0 copy-start.10
  303.8 0.0 copy-start
  304.0 1.5 fusion.3
  305.6 0.0 copy-start.12
  305.6 0.0 copy-start.3
  305.6 0.5 convert_divide_fusion
  306.2 0.0 copy-done
  306.2 0.2 convert_reduce_fusion.1
  306.3 0.3 fusion.13
  306.6 0.3 fusion.17
  307.0 0.8 slice.12
  307.8 0.0 copy-done.3
  307.8 0.0 copy-done.4
  307.9 1.7 fusion.12
  309.5 0.6 dynamic_slice.9
  310.2 0.6 dynamic_slice.11
  310.8 0.1 dynamic_slice.10
  310.9 3.6 %convert_reduce_fusion = f32[256,2048]{1,0:T(8,128)} fusion(bf16[2,256,2048]{2,1,0:T(8,128)(2,1)} %get-tuple-element.49), kind=kLoop, calls=%fused_computation | loop fusion | flops 1572864 | bytes 4194304 | tf_op jit(solution)/shard_map/reduce_sum | solution.py:1640
  314.5 0.9 convert_reduce_fusion.2
  315.3 0.5 copy.36
  (28 shorter events, 0.2 us)
Async XLA Ops:
  300.3 3.7 %copy-start.2 = (bf16[64,6144]{1,0:T(8,128)(2,1)S(1)}, bf16[64,6144]{1,0:T(8,128)(2,1)}, u32[]{:S(2)}) copy-start(bf16[64,6144]{1,0:T(8,128)(2,1)} %qkv.1) | copy-start | bytes 2359300
  300.3 3.7 %copy-start.5 = (bf16[64,6144]{1,0:T(8,128)(2,1)S(1)}, bf16[64,6144]{1,0:T(8,128)(2,1)}, u32[]{:S(2)}) copy-start(bf16[64,6144]{1,0:T(8,128)(2,1)} %get-tuple-element.45) | copy-start | bytes 2359300
  303.8 2.8 copy-start.11
  303.8 1.8 copy-start.7
  303.8 1.8 copy-start.8
  303.8 1.8 copy-start.9
  303.8 1.8 copy-start.10
  303.8 2.3 copy-start
  304.0 2.6 copy-start.1
  305.6 4.0 %copy-start.12 = (f32[64]{0:T(128)}, f32[64]{0:T(128)S(1)}, u32[]{:S(2)}) copy-start(f32[64]{0:T(128)S(1)} %get-tuple-element.89) | copy-start | bytes 772
  305.6 2.3 copy-start.3
  305.6 2.3 copy-start.4
  310.9 4.5 %copy-start.13 = (f32[64]{0:T(128)}, f32[64]{0:T(128)S(1)}, u32[]{:S(2)}) copy-start(f32[64]{0:T(128)S(1)} %dynamic_slice.10) | copy-start | bytes 772
  310.9 3.6 %copy-start.6 = (bf16[2,64,2048]{2,1,0:T(8,128)(2,1)S(1)}, bf16[2,64,2048]{2,1,0:T(8,128)(2,1)}, u32[]{:S(2)}) copy-start(bf16[2,64,2048]{2,1,0:T(8,128)(2,1)} %get-tuple-element.47) | copy-start | bytes 1572868

commit v5 on v4

--- a/solution.py
+++ b/solution.py
@@ -337,6 +337,19 @@
         remote(own, slot, s_x.at[j, a], r_x.at[j, a], xnb).start()
         remote(own, slot, s_s.at[j, a], r_s.at[j, a], sib).start()
 
+    last_slot = jnp.where(a < A // 2, A - 1, 0)
+
+    def send_on(j, k, part):
+        if j == 0:
+            remote(part, part, s_x.at[j, k], r_x.at[j, k], xnb).start()
+        else:
+
+            @pl.when(k != last_slot)
+            def _():
+                remote(part, part, s_x.at[j, k], r_x.at[j, k], xnb).start()
+
+        remote(part, part, s_s.at[j, k], r_s.at[j, k], sib).start()
+
     def z_step(j, s):
         @pl.when(a - 1 - s >= 0)
         def _():
@@ -349,8 +362,7 @@
                 nxt = jnp.minimum(s + 1, A - 2)
                 remote(part, part, s_r.at[j, nxt], r_r.at[j, nxt], right).start()
 
-            remote(part, part, s_x.at[j, k], r_x.at[j, k], xnb).start()
-            remote(part, part, s_s.at[j, k], r_s.at[j, k], sib).start()
+            send_on(j, k, part)
 
         @pl.when(a + 1 + s <= A - 1)
         def _():
@@ -363,8 +375,7 @@
                 nxt = jnp.minimum(s + 1, A - 2)
                 remote(part, part, s_l.at[j, nxt], r_l.at[j, nxt], left).start()
 
-            remote(part, part, s_x.at[j, k], r_x.at[j, k], xnb).start()
-            remote(part, part, s_s.at[j, k], r_s.at[j, k], sib).start()
+            send_on(j, k, part)
 
     xc = (1 - xh) * 2 + core
 
@@ -594,12 +605,16 @@
                 at = j * HEAD_DIM + k * LANES
                 qb[:, at : at + LANES] = chunk(0, first)
 
-    def out_onward():
+    def out_onward(k):
+        remote(o_rows(k, core), o_rows(k, core), s_oc.at[k], r_oc.at[k], sib).start()
+
+    def out_first():
         for k in range(p.m):
-            drain(o_rows(k, core), r_o.at[k])
 
             @pl.when(o_first(k))
             def _():
+                drain(o_rows(k, core), r_o.at[k])
+
                 def o_cross(kk, carry):
                     bb = lax.rem(b + kk, S)
                     rows = o_rows(k, core)
@@ -607,8 +622,15 @@
                     return carry
 
                 lax.fori_loop(1, S, o_cross, 0)
-
-            remote(o_rows(k, core), o_rows(k, core), s_oc.at[k], r_oc.at[k], sib).start()
+                out_onward(k)
+
+    def out_rest():
+        for k in range(p.m):
+
+            @pl.when(jnp.logical_not(o_first(k)))
+            def _():
+                drain(o_rows(k, core), r_o.at[k])
+                out_onward(k)
 
     def load_uw():
         for _ in range(S - 1):
@@ -647,62 +669,62 @@
 
     send_z(0)
     send_x(0)
+    angle_tables(cos_v, sin_v)
     small_all()
     lax.fori_loop(0, 2 * A, up_over, 0)
-    angle_tables(cos_v, sin_v)
     z_step(0, 0)
     cross(0, near[0])
     lax.fori_loop(0, 2 * A, up_along, 0)
+    down_all()
     z_step(0, 1)
     drain(ux, r_ux)
     lax.fori_loop(0, 2 * A, up_onward, 0)
-    down_all()
+    lax.fori_loop(0, A, q_over, 0)
     cross(0, near[1])
     vectors_whole()
     own_x.wait()
     norm_slot(0)
-    lax.fori_loop(0, A, q_over, 0)
+    lax.fori_loop(0, A, q_along, 0)
     send_x(1)
+    norm_slot(1)
+    drain(qx, r_qx)
+    lax.fori_loop(0, A, q_onward, 0)
     out_send()
-    norm_slot(1)
-    lax.fori_loop(0, A, q_along, 0)
     cross(0, near[2])
     send_z(1)
-    norm_slot(2)
     drain(uw.at[:, b], r_up)
     lax.fori_loop(1, S, up_cross, 0)
-    drain(qx, r_qx)
-    lax.fori_loop(0, A, q_onward, 0)
+    drain(qw.at[:, b, :, core], r_q)
+    lax.fori_loop(1, S, q_cross, 0)
+    norm_slot(2)
     z_step(0, 2)
     cross(1, near[0])
     z_step(1, 0)
-    out_onward()
-    load_uw()
-    drain(qw.at[:, b, :, core], r_q)
-    lax.fori_loop(1, S, q_cross, 0)
-    cross(1, near[1])
-    z_step(1, 1)
-    units(0)
+    out_first()
     cross(0, near[3])
-    units(1)
-    send_half_qw()
     norm_slot(3)
     put_n1 = pltpu.make_async_copy(n1_v, n1, loc.at[6])
     put_n1.start()
     put_rows = pltpu.make_async_copy(vecs, rows_out, loc.at[7])
     put_rows.start()
-    z_step(1, 2)
-    units(2)
+    load_uw()
+    send_half_qw()
+    units(0)
+    z_step(1, 1)
+    cross(1, near[1])
+    units(1)
     load_qw()
     attend(0)
+    units(2)
+    z_step(1, 2)
+    attend(1)
+    cross(1, near[2])
     units(3)
     put_hid = pltpu.make_async_copy(hid_v, hid, loc.at[4])
     put_hid.start()
     put_slope = pltpu.make_async_copy(slope_v, slope, loc.at[5])
     put_slope.start()
-    cross(1, near[2])
-    attend(1)
-    cross(1, near[3])
+    out_rest()
 
     put_heads = pltpu.make_async_copy(heads_v, heads, loc.at[0])
     put_heads.start()
@@ -713,7 +735,15 @@
     for k in range(p.m):
         drain(dw.at[pl.ds(0, r)], r_oc.at[k])
     for k in range(A):
-        drain(ga.at[k, pl.ds(0, p.X * p.tok)], r_s.at[1, k])
+
+        @pl.when(k != last_slot)
+        def _():
+            drain(ga.at[k, pl.ds(0, p.X * p.tok)], r_s.at[1, k])
+
+        @pl.when(k == last_slot)
+        def _():
+            drain(ga.at[k, pl.ds(0, p.tok)], r_s.at[1, k])
+
 
     own_g.wait()
     put_hid.wait()
@@ -766,8 +796,19 @@
                 drain(x, s_l.at[j, s])
 
         for k in range(A):
-            drain(x, s_x.at[j, k])
-            drain(xa.at[k, pl.ds(0, p.X * p.tok)], s_s.at[j, k])
+            if j == 0:
+                drain(x, s_x.at[j, k])
+                drain(xa.at[k, pl.ds(0, p.X * p.tok)], s_s.at[j, k])
+                continue
+
+            @pl.when(k != last_slot)
+            def _():
+                drain(x, s_x.at[j, k])
+                drain(xa.at[k, pl.ds(0, p.X * p.tok)], s_s.at[j, k])
+
+            @pl.when(k == last_slot)
+            def _():
+                drain(x, s_s.at[j, k])
 
 
 def front(p, x, g, qkv, outw, up, down, lens, *vectors):
@@ -866,7 +907,7 @@
     hid,
     heads,
     slope,
-    g,
+    g_in,
     joint,
     n1,
     n2,
@@ -883,6 +924,7 @@
     v_all,
     u_z,
     q_z,
+    g,
     hid_v,
     heads_v,
     dpre,
@@ -942,6 +984,8 @@
     r_ua,
     s_d,
     r_d,
+    s_g,
+    r_g,
     free,
 ):
     A, S, C, X, r, R = p.A, p.S, p.C, p.X, p.r, p.R
@@ -977,6 +1021,17 @@
     vec[...] = jnp.zeros_like(vec)
     angle_tables(cos_v, sin_v)
     greet_all(p, me)
+    last_slot = jnp.where(a < half, A - 1, 0)
+
+    def g_rows(cc):
+        return g.at[pl.ds(pl.multiple_of(last_slot * L + cc * p.tok, p.tok), p.tok)]
+
+    remote(g_rows(c), g_rows(c), s_g.at[0], r_g.at[0], xnb).start()
+    x_ctx = far * 2 + core
+
+    def g_forward():
+        drain(g_rows(x_ctx), r_g.at[0])
+        remote(g_rows(x_ctx), g_rows(x_ctx), s_g.at[1], r_g.at[1], sib).start()
 
     low = a < half
     order = [
@@ -1105,6 +1160,7 @@
             at = pl.ds(pl.multiple_of(i * TILE, TILE), TILE)
             return pltpu.make_async_copy(g.at[at], g_v.at[slot], g_sem.at[slot])
 
+        drain(g_rows(far * 2 + 1 - core), r_g.at[1])
         g_load(0, 0).start()
 
         def step(i, carry):
@@ -1389,6 +1445,7 @@
     partial(0, 2)
     chip_sum(0, order[1])
     partial(0, 3)
+    g_forward()
     chip_sum(0, order[2])
     chip_sum(0, order[3])
     give_back()
@@ -1418,7 +1475,6 @@
     q_cross()
     stream(g, down_tile, 0, 4)
     hop(1, 1, False)
-    last(0, o_sum)
     stream(g, down_tile, 4, 8)
     down_send()
     hop(1, 2, False)
@@ -1429,6 +1485,7 @@
     hop(1, 1, True)
     up_home()
     q_home()
+    last(0, o_sum)
     last(1, e_sum)
 
     drain(u_out, r_ua)
@@ -1438,6 +1495,8 @@
     drain(o_parts, r_oa)
 
     own_v.wait()
+    for k in range(2):
+        drain(g_rows(c), s_g.at[k])
     drain(v_all.at[pl.ds(0, p.n - 1)], s_v)
     drain(q_sib, s_q)
     drain(o_sib, s_o)
@@ -1493,9 +1552,11 @@
             jax.ShapeDtypeStruct((p.n, 16, LANES), F32),
             jax.ShapeDtypeStruct((A - 1, C * r, p.ffl), BF),
             jax.ShapeDtypeStruct((A - 1, X, r, p.hc), BF),
+            jax.ShapeDtypeStruct((p.rows, p.d), BF),
         ),
+        input_output_aliases={3: 9},
         in_specs=[hbm] * 10 + [vmem],
-        out_specs=[vmem] * 2 + [hbm] * 7,
+        out_specs=[vmem] * 2 + [hbm] * 8,
         scratch_shapes=[
             vm((max(p.rows, p.d), p.ffl), BF),
             vm((p.rows // 2, HEAD_DIM), BF),
@@ -1556,6 +1617,8 @@
             dma,
             dma((S,)),
             dma,
+            dma((2,)),
+            dma((2,)),
             pltpu.SemaphoreType.REGULAR,
         ],
         compiler_params=pltpu.CompilerParams(
@@ -1621,7 +1684,7 @@
         lengths,
         *(v.reshape(1, -1) for v in vectors),
     )
-    o_sum, e_sum, q_out, u_out, d_parts, o_parts, v_all, _, _ = back(
+    o_sum, e_sum, q_out, u_out, d_parts, o_parts, v_all, _, _, _ = back(
         p,
         hid,
         heads,

time: 321 us -> 312 us (0.972)
  Pallas kernels: 295 us -> 288 us
    pallas_call x1, Pallas kernels: 142 us -> 134 us  [front(): pl.pallas_call(functools.partial(front_kernel, p), out_shape=(jax.ShapeDt...]
where the time goes in v5:
time: 312 us; the launch traced here: 308 us
  Pallas kernels  288 us (92%)
  other arithmetic  12.6 us (4%)
  local copies, waits for them, and re-layouts  6.35 us (2%)
    pallas_call x1, Pallas kernels, back(): pl.pallas_call(functools.partial(back_kernel, p), out_shape=(jax.ShapeDty...  154 us
    pallas_call x1, Pallas kernels, front(): pl.pallas_call(functools.partial(front_kernel, p), out_shape=(jax.ShapeDt...  134 us

profile of v5, /device:TPU:16, one launch (start us, length us, event | category | flops | bytes accessed | tf_op | source)
XLA Modules:
  0.0 308.1 jit_solution(8983392052772208232)
XLA Ops:
  1.3 1.2 reshape.109.qkv_b
  2.5 1.2 reshape.111.up_b
  3.7 133.5 %front.1 = (bf16[4,512,2048]{2,1,0:T(8,128)(2,1)}, bf16[4,512,2048]{2,1,0:T(8,128)(2,1)}, bf16[4,2,2,2,64,768]{5,4,3,2,1,0:T(8,128)(2,1)}, bf16[768,2048]{1,0:T(...) custom-call(bf16[128,2048]{1,0:T(8,128)(2,1)} %x.1, ...), custom_call_target="tpu_custom_call" | custom-call | tf_op jit(solution)/shard_map/front/pallas_call | solution.py:824
  137.3 154.1 %back.1 = (f32[128,2048]{1,0:T(8,128)}, f32[128,2048]{1,0:T(8,128)}, bf16[64,6144]{1,0:T(8,128)(2,1)}, bf16[64,8192]{1,0:T(8,128)(2,1)}, bf16[2,256,2048]{2,1,0:...) custom-call(bf16[2048,512]{1,0:T(8,128)(2,1)} %get-tuple-element.32., ...), custom_call_target="tpu_custom_call", output_to_operand_aliasing={{9}: (3, {})} | custom-call | tf_op jit(solution)/shard_map/back/pallas_call | solution.py:1543
  291.4 1.0 reshape.120
  292.4 0.1 reduce_sum.112
  292.5 0.0 copy-start.2
  292.5 3.5 %fusion.1 = (f32[64]{0:T(128)S(1)}, f32[64]{0:T(128)S(1)}, f32[64,8192]{1,0:T(8,128)}) fusion(bf16[64,8192]{1,0:T(8,128)(2,1)} %up.1, f32[8192]{0:T(1024)S(1)} %bitcast.27, bf16[64,8192]{1,0:T(8,128)(2,1)} %get-tuple-element.48), kind=kLoop, calls=%fused_computation.4 | loop fusion | flops 3145600 | bytes 4227584 | tf_op jit(solution)/shard_map/reduce_sum | solution.py:1732
  296.0 0.0 copy-start.11
  296.0 0.0 copy-start.7
  296.0 0.0 copy-start.8
  296.1 0.0 copy-start.9
  296.1 0.0 copy-start.10
  296.1 0.0 copy-start
  296.2 0.0 copy-done.2
  296.2 0.0 copy-done.5
  296.2 0.0 copy-start.1
  296.3 1.5 fusion.3
  297.8 0.0 copy-start.12
  297.8 0.0 copy-start.3
  297.9 0.5 convert_divide_fusion
  298.4 0.2 convert_reduce_fusion.1
  298.6 0.3 fusion.13
  298.9 0.3 fusion.17
  299.2 0.8 slice.12
  300.1 1.7 fusion.12
  301.8 0.6 dynamic_slice.9
  302.4 0.6 dynamic_slice.11
  303.0 0.1 dynamic_slice.10
  303.1 3.6 %convert_reduce_fusion = f32[256,2048]{1,0:T(8,128)} fusion(bf16[2,256,2048]{2,1,0:T(8,128)(2,1)} %get-tuple-element.49), kind=kLoop, calls=%fused_computation | loop fusion | flops 1572864 | bytes 4194304 | tf_op jit(solution)/shard_map/reduce_sum | solution.py:1703
  306.7 0.9 convert_reduce_fusion.2
  307.6 0.5 copy.38
  (28 shorter events, 0.2 us)
Async XLA Ops:
  292.5 3.7 %copy-start.2 = (bf16[64,6144]{1,0:T(8,128)(2,1)S(1)}, bf16[64,6144]{1,0:T(8,128)(2,1)}, u32[]{:S(2)}) copy-start(bf16[64,6144]{1,0:T(8,128)(2,1)} %qkv.1) | copy-start | bytes 2359300
  292.5 3.7 %copy-start.5 = (bf16[64,6144]{1,0:T(8,128)(2,1)S(1)}, bf16[64,6144]{1,0:T(8,128)(2,1)}, u32[]{:S(2)}) copy-start(bf16[64,6144]{1,0:T(8,128)(2,1)} %get-tuple-element.45) | copy-start | bytes 2359300
  296.0 2.8 copy-start.11
  296.0 1.8 copy-start.7
  296.0 1.8 copy-start.8
  296.1 1.8 copy-start.9
  296.1 1.8 copy-start.10
  296.1 2.3 copy-start
  296.2 2.6 copy-start.1
  297.8 4.0 %copy-start.12 = (f32[64]{0:T(128)}, f32[64]{0:T(128)S(1)}, u32[]{:S(2)}) copy-start(f32[64]{0:T(128)S(1)} %get-tuple-element.89) | copy-start | bytes 772
  297.8 2.3 copy-start.3
  297.8 2.3 copy-start.4
  303.1 4.5 %copy-start.13 = (f32[64]{0:T(128)}, f32[64]{0:T(128)S(1)}, u32[]{:S(2)}) copy-start(f32[64]{0:T(128)S(1)} %dynamic_slice.10) | copy-start | bytes 772
  303.1 3.6 %copy-start.6 = (bf16[2,64,2048]{2,1,0:T(8,128)(2,1)S(1)}, bf16[2,64,2048]{2,1,0:T(8,128)(2,1)}, u32[]{:S(2)}) copy-start(bf16[2,64,2048]{2,1,0:T(8,128)(2,1)} %get-tuple-element.47) | copy-start | bytes 1572868

commit v6 on v5

--- a/solution.py
+++ b/solution.py
@@ -289,9 +289,9 @@
         value = v[...].astype(F32)
         if k == len(vectors) - 1:
             value = value + down_b[...].astype(F32)
-        pads[k : k + 1, 0 : v.shape[1]] = value
+        pads[k, 0 : v.shape[0]] = value
     for k, v in enumerate(vectors):
-        placed = pltpu.roll(pads[k : k + 1, :], lax.rem(v.shape[1] * me, LANES), 1)
+        placed = pltpu.roll(pads[k : k + 1, :], lax.rem(v.shape[0] * me, LANES), 1)
         small[2 * k : 2 * k + 1, :] = placed[:, :LANES]
         small[2 * k + 1 : 2 * k + 2, :] = placed[:, LANES:]
     small[2 * len(vectors) :, :] = jnp.zeros((2, LANES), F32)
@@ -566,7 +566,7 @@
             pltpu.make_async_copy(outw, o_rows(row_part, core), r_o.at[row_part]).start()
 
     def chunk(which, jj):
-        size = vectors[which].shape[1]
+        size = vectors[which].shape[0]
         if size % LANES == 0:
             count = 1
         elif LANES % size == 0:
@@ -1628,11 +1628,222 @@
     )(*args)
 
 
-def norm_stats(values):
-    center = jnp.mean(values, axis=-1, keepdims=True)
-    spread = jnp.mean(jnp.square(values - center), axis=-1, keepdims=True)
-    inv_std = lax.rsqrt(spread + EPS)
-    return (values - center) * inv_std, inv_std
+def finish_kernel(
+    p,
+    lens,
+    x,
+    g,
+    o_sum,
+    e_sum,
+    full,
+    q_part,
+    u_part,
+    d_parts,
+    o_parts,
+    sums,
+    qkv_w,
+    up_w,
+    gain1,
+    bias1,
+    gain2,
+    bias2,
+    out,
+    grad,
+    q_grad,
+    u_grad,
+    d_grad,
+    o_grad,
+    q_own,
+    u_own,
+    g_own,
+    g_same,
+    gain1_grad,
+    bias1_grad,
+    gain2_grad,
+    bias2_grad,
+    q_bias,
+    u_bias,
+    g_bias,
+    row_sums,
+):
+    A, S, C, X = p.A, p.S, p.C, p.X
+    step = pl.program_id(0)
+
+    @pl.when(step == 0)
+    def _():
+        up_row = p.hc // LANES
+        g_row = up_row + p.ffl // LANES
+        share = p.d // (A * C)
+        for aa in range(A):
+            for cc in range(C):
+                for row in range(up_row, g_row + 1):
+                    total = sums[aa * S * C + cc, row : row + 1, :]
+                    for bb in range(1, S):
+                        total = total + sums[(aa * S + bb) * C + cc, row : row + 1, :]
+                    if row == g_row:
+                        at = (aa * C + cc) * share
+                        g_bias[:, at : at + share] = total[:, :share]
+                        continue
+                    unit = (row - up_row) * LANES
+                    run = unit // p.W
+                    if p.P == 1:
+                        first = p.R * ((aa * S + run) * C + cc)
+                    else:
+                        first = p.R * ((aa * S + 2 * run + cc % 2) * C + cc // 2 * 2)
+                    at = first + unit % p.W
+                    u_bias[:, at : at + LANES] = total
+            for xx in range(X):
+                for row in range(up_row):
+                    total = jnp.zeros((1, LANES), F32)
+                    for bb in range(S):
+                        for kk in range(2):
+                            total = total + sums[(aa * S + bb) * C + xx * 2 + kk, row : row + 1, :]
+                    j, rest = row * LANES // HEAD_DIM, row * LANES % HEAD_DIM
+                    at = j * p.d + (aa * X + xx) * HEAD_DIM + rest
+                    q_bias[:, at : at + LANES] = total
+        me = lax.axis_index("dp") * C + lax.axis_index("ctx")
+
+        def own(vector, size):
+            span = max(size * i % LANES + size for i in range(p.n))
+            span = (span + LANES - 1) // LANES * LANES
+            rest = lax.rem(size * me, LANES)
+            at = pl.multiple_of(size * me - rest, LANES)
+            piece = pltpu.roll(vector[:, pl.ds(at, span)], lax.rem(span - rest, span), 1)
+            return piece[0, :size]
+
+        q_own[...] = own(q_bias, 3 * p.d // p.n)
+        u_own[...] = own(u_bias, p.ff // p.n)
+        g_own[...] = own(g_bias, p.d // p.n)
+        g_same[...] = own(g_bias, p.d // p.n)
+
+    rows = x.shape[0]
+    sub = 16
+    first = lax.axis_index("ctx") * p.tok + step * rows
+    length = lens[0]
+
+    def tokens(at):
+        here = pl.ds(at, sub)
+        row = lax.broadcasted_iota(jnp.int32, (sub, p.d), 0) + (at + first)
+        live = row < length
+        xf = x[here, :].astype(F32)
+        total = xf + o_sum[here, :] + full[4:5, :]
+        out[here, :] = jnp.where(live, total, 0.0).astype(BF)
+        mid = xf - jnp.mean(xf, axis=1, keepdims=True)
+        inv = lax.rsqrt(jnp.mean(mid * mid, axis=1, keepdims=True) + EPS)
+        xhat = mid * inv
+        e = e_sum[here, :]
+        e_mean = jnp.mean(e, axis=1, keepdims=True)
+        dx = inv * (e - e_mean - xhat * jnp.mean(e * xhat, axis=1, keepdims=True))
+        go = jnp.where(live, g[here, :].astype(F32), 0.0)
+        grad[here, :] = (go + dx).astype(BF)
+
+    tiles(rows, tokens, sub)
+
+    count = q_part.shape[0]
+    lane = lax.broadcasted_iota(jnp.int32, (count, LANES), 1)
+    kept = jnp.zeros((count, LANES), F32)
+    for k, (part, weight, bias, result) in enumerate(
+        ((q_part, qkv_w, q_bias, q_grad), (u_part, up_w, u_bias, u_grad))
+    ):
+        with_grad = jnp.zeros((part.shape[0], LANES), F32)
+        with_bias = jnp.zeros((part.shape[0], LANES), F32)
+        for n in range(0, part.shape[1], LANES):
+            at = slice(n, n + LANES)
+            value = part[:, at].astype(F32)
+            result[:, at] = value
+            w = weight[:, at].astype(F32)
+            with_grad = with_grad + w * value
+            with_bias = with_bias + w * bias[:, at]
+        for o, t in enumerate((with_grad, with_bias)):
+            kept = jnp.where(lane == 2 * k + o, jnp.sum(t, axis=1, keepdims=True), kept)
+    row_sums[pl.ds(pl.multiple_of(step * count, count), count), :] = kept
+
+    @pl.when(step == pl.num_programs(0) - 1)
+    def _():
+        turned = row_sums[...].T
+        for k, (gain, shift, to_gain, to_shift) in enumerate(
+            ((gain1, bias1, gain1_grad, bias1_grad), (gain2, bias2, gain2_grad, bias2_grad))
+        ):
+            with_grad, with_bias = turned[2 * k, : p.r], turned[2 * k + 1, : p.r]
+            to_gain[...] = (with_grad - shift[...].astype(F32) * with_bias) / gain[...].astype(F32)
+            to_shift[...] = with_bias
+
+    for parts, result in ((d_parts, d_grad), (o_parts, o_grad)):
+
+        def add(at):
+            here = pl.ds(at, sub)
+            total = parts[0, here, :].astype(F32)
+            for k in range(1, S):
+                total = total + parts[k, here, :].astype(F32)
+            result[here, :] = total
+
+        tiles(result.shape[0], add, sub)
+
+
+def finish(p, *args):
+    steps = max(1, p.r // 16)
+    D, r, R = p.d, p.r, p.R
+
+    def rows(count, width):
+        return pl.BlockSpec((count // steps, width), lambda i: (i, 0))
+
+    def parts(count):
+        return pl.BlockSpec((p.S, count // steps, D), lambda i: (0, i, 0))
+
+    def whole(*shape):
+        return pl.BlockSpec(shape, lambda i: (0,) * len(shape))
+
+    tok = rows(p.tok, D)
+    return pl.pallas_call(
+        functools.partial(finish_kernel, p),
+        grid=(steps,),
+        out_shape=(
+            jax.ShapeDtypeStruct((p.tok, D), BF),
+            jax.ShapeDtypeStruct((p.tok, D), BF),
+            jax.ShapeDtypeStruct((r, 3 * D), F32),
+            jax.ShapeDtypeStruct((r, p.ff), F32),
+            jax.ShapeDtypeStruct((R, D), F32),
+            jax.ShapeDtypeStruct((r, D), F32),
+            jax.ShapeDtypeStruct((3 * D // p.n,), F32),
+            jax.ShapeDtypeStruct((p.ff // p.n,), F32),
+            *[jax.ShapeDtypeStruct((r,), F32)] * 6,
+        ),
+        in_specs=[
+            pl.BlockSpec(memory_space=pltpu.SMEM),
+            tok,
+            tok,
+            tok,
+            tok,
+            whole(8, D),
+            rows(r, 3 * D),
+            rows(r, p.ff),
+            parts(R),
+            parts(r),
+            whole(p.n, 16, LANES),
+            rows(r, 3 * D),
+            rows(r, p.ff),
+            *[whole(r)] * 4,
+        ],
+        out_specs=[
+            tok,
+            tok,
+            rows(r, 3 * D),
+            rows(r, p.ff),
+            rows(R, D),
+            rows(r, D),
+            whole(3 * D // p.n),
+            whole(p.ff // p.n),
+            *[whole(r)] * 6,
+        ],
+        scratch_shapes=[
+            pltpu.VMEM((1, 3 * D), F32),
+            pltpu.VMEM((1, p.ff), F32),
+            pltpu.VMEM((1, D), F32),
+            pltpu.VMEM((r, LANES), F32),
+        ],
+        compiler_params=pltpu.CompilerParams(dimension_semantics=("arbitrary",)),
+        name="finish",
+    )(*args)
 
 
 def local(
@@ -1661,8 +1872,6 @@
     dp, c, a, b, xh, core = place(p)
     me = dp * C + c
     t = a * C + c
-    valid = (c * tok + jnp.arange(tok, dtype=jnp.int32) < lengths[0])[:, None]
-    grad_out = jnp.where(valid, cotangent, jnp.zeros_like(cotangent))
     vectors = (
         qkv_bias,
         out_bias,
@@ -1682,7 +1891,7 @@
         up_weight,
         down_weight,
         lengths,
-        *(v.reshape(1, -1) for v in vectors),
+        *vectors,
     )
     o_sum, e_sum, q_out, u_out, d_parts, o_parts, v_all, _, _, _ = back(
         p,
@@ -1698,59 +1907,52 @@
         qw.reshape(d, p.hc),
         full,
     )
-    g_cols = d // (A * C)
-    o_out = jnp.sum(o_parts.astype(F32), axis=0)
-    d_out = jnp.sum(d_parts.astype(F32), axis=0)
-
-    xf = layer_input.astype(F32)
-    output = jnp.where(valid, xf + o_sum + full[4:5], 0.0).astype(BF)
-    xhat_o, inv = norm_stats(xf)
-    dx = inv * (
-        e_sum
-        - jnp.mean(e_sum, axis=-1, keepdims=True)
-        - xhat_o * jnp.mean(e_sum * xhat_o, axis=-1, keepdims=True)
+    (
+        output,
+        input_grad,
+        q_grad,
+        u_grad,
+        d_grad,
+        o_grad,
+        q_bias,
+        u_bias,
+        g_bias,
+        g_same,
+        gain1_grad,
+        bias1_grad,
+        gain2_grad,
+        bias2_grad,
+    ) = finish(
+        p,
+        lengths,
+        layer_input,
+        cotangent,
+        o_sum,
+        e_sum,
+        full,
+        q_out,
+        u_out,
+        d_parts,
+        o_parts,
+        v_all,
+        qkv_weight,
+        up_weight,
+        first_gain,
+        first_bias,
+        second_gain,
+        second_bias,
     )
-    input_grad = (grad_out.astype(F32) + dx).astype(BF)
-
-    v_all = v_all.reshape(A, S, C, 2048)
-    v_sum = jnp.sum(v_all, axis=1)
-    q_bias = v_sum[..., : p.hc].reshape(A, X, 2, 3, HEAD_DIM).sum(axis=2)
-    q_bias = q_bias.reshape(HEADS, 3, HEAD_DIM).transpose(1, 0, 2).reshape(-1)
-    u_bias = v_sum[..., p.hc : p.hc + p.ffl]
-    if p.P == 1:
-        u_bias = u_bias.reshape(A, C, S, R).transpose(0, 2, 1, 3).reshape(-1)
-    else:
-        u_bias = u_bias.reshape(A, X, 2, S // 2, p.W).transpose(0, 3, 2, 1, 4).reshape(-1)
-    g_bias = v_sum[..., p.hc + p.ffl : p.hc + p.ffl + g_cols].reshape(-1)
-
-    def own(vector):
-        size = vector.shape[0] // p.n
-        return lax.dynamic_slice(vector, (me * size,), (size,))
-
-    def norm_grads(weight, grad, bias_grad, gain, shift):
-        weight = weight.astype(F32)
-        shift_grad = jnp.sum(weight * bias_grad, axis=1)
-        gain_grad = (jnp.sum(weight * grad, axis=1) - shift.astype(F32) * shift_grad) / gain.astype(
-            F32
-        )
-        return gain_grad, shift_grad
-
-    q_grad = q_out.astype(F32)
-    u_grad = u_out.astype(F32)
-    gain1_grad, bias1_grad = norm_grads(qkv_weight, q_grad, q_bias, first_gain, first_bias)
-    gain2_grad, bias2_grad = norm_grads(up_weight, u_grad, u_bias, second_gain, second_bias)
-    g_own = own(g_bias)
     return (
         output,
         input_grad,
         q_grad,
-        own(q_bias),
-        o_out,
-        g_own,
+        q_bias,
+        o_grad,
+        g_bias,
         u_grad,
-        own(u_bias),
-        d_out,
-        g_own,
+        u_bias,
+        d_grad,
+        g_same,
         gain1_grad,
         bias1_grad,
         gain2_grad,

time: 312 us -> 302 us (0.968)
  other arithmetic: 12.6 us -> 0 us
  Pallas kernels: 288 us -> 297 us
  local copies, waits for them, and re-layouts: 6.35 us -> 0 us
    reduce_sum x9 -> x0, other arithmetic: 10.4 us -> none  [the longest x2 5.03 us: norm_grads(): shift_grad = jnp.sum(weight * bias_grad, axis=1)]
    pallas_call x0 -> x1, Pallas kernels: none -> 9.46 us  [finish(): pl.pallas_call(functools.partial(finish_kernel, p), grid=(steps,), out_sh...]
    reshape x5 -> x0, local copies, waits for them, and re-layouts: 3.52 us -> none  [the longest x2 2.44 us: local(): v.reshape(1, -1)]
where the time goes in v6:
time: 302 us; the launch traced here: 299 us
  Pallas kernels  297 us (98%)
    pallas_call x1, Pallas kernels, back(): pl.pallas_call(functools.partial(back_kernel, p), out_shape=(jax.ShapeDty...  154 us
    pallas_call x1, Pallas kernels, front(): pl.pallas_call(functools.partial(front_kernel, p), out_shape=(jax.ShapeDt...  134 us
    pallas_call x1, Pallas kernels, finish(): pl.pallas_call(functools.partial(finish_kernel, p), grid=(steps,), out_sh...  9.46 us

profile of v6, /device:TPU:16, one launch (start us, length us, event | category | flops | bytes accessed | tf_op | source)
XLA Modules:
  0.0 298.6 jit_solution(2946140584584392249)
XLA Ops:
  1.3 133.6 %front.1 = (bf16[4,512,2048]{2,1,0:T(8,128)(2,1)}, bf16[4,512,2048]{2,1,0:T(8,128)(2,1)}, bf16[4,2,2,2,64,768]{5,4,3,2,1,0:T(8,128)(2,1)}, bf16[768,2048]{1,0:T(...) custom-call(bf16[128,2048]{1,0:T(8,128)(2,1)} %x.3, ...), custom_call_target="tpu_custom_call" | custom-call | tf_op jit(solution)/shard_map/front/pallas_call | solution.py:824
  134.9 154.1 %back.1 = (f32[128,2048]{1,0:T(8,128)}, f32[128,2048]{1,0:T(8,128)}, bf16[64,6144]{1,0:T(8,128)(2,1)}, bf16[64,8192]{1,0:T(8,128)(2,1)}, bf16[2,256,2048]{2,1,0:...) custom-call(bf16[2048,512]{1,0:T(8,128)(2,1)} %get-tuple-element.46., ...), custom_call_target="tpu_custom_call", output_to_operand_aliasing={{9}: (3, {})} | custom-call | tf_op jit(solution)/shard_map/back/pallas_call | solution.py:1543
  288.9 9.5 %finish.1 = (bf16[128,2048]{1,0:T(8,128)(2,1)}, bf16[128,2048]{1,0:T(8,128)(2,1)}, f32[64,6144]{1,0:T(8,128)}, f32[64,8192]{1,0:T(8,128)}, f32[256,2048]{1,0:T(8...) custom-call(s32[1]{0:T(128)S(6)} %copy.31.lens, ...), custom_call_target="tpu_custom_call" | custom-call | tf_op jit(solution)/shard_map/finish/pallas_call | solution.py:1797

commit v7 on v6

--- a/solution.py
+++ b/solution.py
@@ -210,6 +210,7 @@
     rows_out,
     small,
     pads,
+    g_v,
     gm,
     sm_v,
     vecs,
@@ -274,35 +275,15 @@
     L = C * p.tok
     half = A // 2
 
-    length = lens[0]
-
-    def mask(at):
-        row = lax.broadcasted_iota(jnp.int32, (32, p.d), 0) + (at + c * p.tok)
-        rows = g[pl.ds(at, 32), :].astype(F32)
-        gm[pl.ds(at, 32), :] = jnp.where(row < length, rows, 0.0).astype(BF)
-
-    tiles(p.tok, mask, 32)
-
-    pads[...] = jnp.zeros_like(pads)
+    get_g = pltpu.make_async_copy(g, g_v, loc.at[2])
+    get_g.start()
     vectors = (qkv_b, up_b, gain1, bias1, gain2, bias2, out_b)
-    for k, v in enumerate(vectors):
-        value = v[...].astype(F32)
-        if k == len(vectors) - 1:
-            value = value + down_b[...].astype(F32)
-        pads[k, 0 : v.shape[0]] = value
-    for k, v in enumerate(vectors):
-        placed = pltpu.roll(pads[k : k + 1, :], lax.rem(v.shape[0] * me, LANES), 1)
-        small[2 * k : 2 * k + 1, :] = placed[:, :LANES]
-        small[2 * k + 1 : 2 * k + 2, :] = placed[:, LANES:]
-    small[2 * len(vectors) :, :] = jnp.zeros((2, LANES), F32)
     greet_all(p, me)
 
     own_small = pltpu.make_async_copy(small, sm.at[me], loc.at[0])
-    own_small.start()
     own_x = pltpu.make_async_copy(x, xa.at[a, pl.ds(pl.multiple_of(c * p.tok, p.tok), p.tok)], loc.at[1])
     own_x.start()
     own_g = pltpu.make_async_copy(gm, ga.at[a, pl.ds(pl.multiple_of(c * p.tok, p.tok), p.tok)], loc.at[2])
-    own_g.start()
 
     row_head = lax.div(me * r, HEAD_DIM)
     row_part = lax.div(lax.rem(me * r, HEAD_DIM), 2 * r)
@@ -669,9 +650,33 @@
 
     send_z(0)
     send_x(0)
-    angle_tables(cos_v, sin_v)
+
+    get_g.wait()
+    length = lens[0]
+
+    def mask(at):
+        row = lax.broadcasted_iota(jnp.int32, (32, p.d), 0) + (at + c * p.tok)
+        rows = g_v[pl.ds(at, 32), :].astype(F32)
+        gm[pl.ds(at, 32), :] = jnp.where(row < length, rows, 0.0).astype(BF)
+
+    tiles(p.tok, mask, 32)
+
+    pads[...] = jnp.zeros_like(pads)
+    for k, v in enumerate(vectors):
+        value = v[...].astype(F32)
+        if k == len(vectors) - 1:
+            value = value + down_b[...].astype(F32)
+        pads[k, 0 : v.shape[0]] = value
+    for k, v in enumerate(vectors):
+        placed = pltpu.roll(pads[k : k + 1, :], lax.rem(v.shape[0] * me, LANES), 1)
+        small[2 * k : 2 * k + 1, :] = placed[:, :LANES]
+        small[2 * k + 1 : 2 * k + 2, :] = placed[:, LANES:]
+    small[2 * len(vectors) :, :] = jnp.zeros((2, LANES), F32)
+    own_small.start()
+    own_g.start()
     small_all()
     lax.fori_loop(0, 2 * A, up_over, 0)
+    angle_tables(cos_v, sin_v)
     z_step(0, 0)
     cross(0, near[0])
     lax.fori_loop(0, 2 * A, up_along, 0)
@@ -838,11 +843,12 @@
             jax.ShapeDtypeStruct((half, p.hc), BF),
             jax.ShapeDtypeStruct((8, p.d), F32),
         ),
-        in_specs=[vmem] * 6 + [pl.BlockSpec(memory_space=pltpu.SMEM)] + [vmem] * 8,
+        in_specs=[hbm] * 6 + [pl.BlockSpec(memory_space=pltpu.SMEM)] + [vmem] * 8,
         out_specs=[hbm] * 13,
         scratch_shapes=[
             vm((16, LANES), F32),
             vm((8, 2 * LANES), F32),
+            vm((p.tok, p.d), BF),
             vm((p.tok, p.d), BF),
             vm((p.n, 16, LANES), F32),
             vm((8, p.d), F32),
@@ -1018,16 +1024,16 @@
     ]
     for load in loads:
         load.start()
+    greet_all(p, me)
+    last_slot = jnp.where(a < half, A - 1, 0)
+
+    def g_rows(cc):
+        return g.at[pl.ds(pl.multiple_of(last_slot * L + cc * p.tok, p.tok), p.tok)]
+
+    remote(g_rows(c), g_rows(c), s_g.at[0], r_g.at[0], xnb).start()
+    x_ctx = far * 2 + core
     vec[...] = jnp.zeros_like(vec)
     angle_tables(cos_v, sin_v)
-    greet_all(p, me)
-    last_slot = jnp.where(a < half, A - 1, 0)
-
-    def g_rows(cc):
-        return g.at[pl.ds(pl.multiple_of(last_slot * L + cc * p.tok, p.tok), p.tok)]
-
-    remote(g_rows(c), g_rows(c), s_g.at[0], r_g.at[0], xnb).start()
-    x_ctx = far * 2 + core
 
     def g_forward():
         drain(g_rows(x_ctx), r_g.at[0])
@@ -1717,7 +1723,7 @@
         g_same[...] = own(g_bias, p.d // p.n)
 
     rows = x.shape[0]
-    sub = 16
+    sub = 32
     first = lax.axis_index("ctx") * p.tok + step * rows
     length = lens[0]
 
@@ -1770,18 +1776,20 @@
 
     for parts, result in ((d_parts, d_grad), (o_parts, o_grad)):
 
+        size = min(sub, result.shape[0])
+
         def add(at):
-            here = pl.ds(at, sub)
+            here = pl.ds(at, size)
             total = parts[0, here, :].astype(F32)
             for k in range(1, S):
                 total = total + parts[k, here, :].astype(F32)
             result[here, :] = total
 
-        tiles(result.shape[0], add, sub)
+        tiles(result.shape[0], add, size)
 
 
 def finish(p, *args):
-    steps = max(1, p.r // 16)
+    steps = max(1, p.r // 32)
     D, r, R = p.d, p.r, p.R
 
     def rows(count, width):

time: 302 us -> 299 us (0.990)
  Pallas kernels: 297 us -> 293 us
where the time goes in v7:
time: 299 us; the launch traced here: 295 us
  Pallas kernels  293 us (98%)
    pallas_call x1, Pallas kernels, back(): pl.pallas_call(functools.partial(back_kernel, p), out_shape=(jax.ShapeDty...  154 us
    pallas_call x1, Pallas kernels, front(): pl.pallas_call(functools.partial(front_kernel, p), out_shape=(jax.ShapeDt...  132 us
    pallas_call x1, Pallas kernels, finish(): pl.pallas_call(functools.partial(finish_kernel, p), grid=(steps,), out_sh...  7.42 us

profile of v7, /device:TPU:16, one launch (start us, length us, event | category | flops | bytes accessed | tf_op | source)
XLA Modules:
  0.0 294.6 jit_solution(16706416765372340131)
XLA Ops:
  1.3 132.0 %front.1 = (bf16[4,512,2048]{2,1,0:T(8,128)(2,1)}, bf16[4,512,2048]{2,1,0:T(8,128)(2,1)}, bf16[4,2,2,2,64,768]{5,4,3,2,1,0:T(8,128)(2,1)}, bf16[768,2048]{1,0:T(...) custom-call(bf16[128,2048]{1,0:T(8,128)(2,1)} %x.3, ...), custom_call_target="tpu_custom_call" | custom-call | tf_op jit(solution)/shard_map/front/pallas_call | solution.py:829
  133.3 153.7 %back.1 = (f32[128,2048]{1,0:T(8,128)}, f32[128,2048]{1,0:T(8,128)}, bf16[64,6144]{1,0:T(8,128)(2,1)}, bf16[64,8192]{1,0:T(8,128)(2,1)}, bf16[2,256,2048]{2,1,0:...) custom-call(bf16[2048,512]{1,0:T(8,128)(2,1)} %get-tuple-element.46., ...), custom_call_target="tpu_custom_call", output_to_operand_aliasing={{9}: (3, {})} | custom-call | tf_op jit(solution)/shard_map/back/pallas_call | solution.py:1549
  287.0 7.4 %finish.1 = (bf16[128,2048]{1,0:T(8,128)(2,1)}, bf16[128,2048]{1,0:T(8,128)(2,1)}, f32[64,6144]{1,0:T(8,128)}, f32[64,8192]{1,0:T(8,128)}, f32[256,2048]{1,0:T(8...) custom-call(s32[1]{0:T(128)S(6)} %copy.31.lens, ...), custom_call_target="tpu_custom_call" | custom-call | tf_op jit(solution)/shard_map/finish/pallas_call | solution.py:1805

commit v8 on v7

--- a/solution.py
+++ b/solution.py
@@ -681,10 +681,10 @@
     cross(0, near[0])
     lax.fori_loop(0, 2 * A, up_along, 0)
     down_all()
-    z_step(0, 1)
     drain(ux, r_ux)
     lax.fori_loop(0, 2 * A, up_onward, 0)
     lax.fori_loop(0, A, q_over, 0)
+    z_step(0, 1)
     cross(0, near[1])
     vectors_whole()
     own_x.wait()
@@ -704,9 +704,9 @@
     norm_slot(2)
     z_step(0, 2)
     cross(1, near[0])
-    z_step(1, 0)
     out_first()
     cross(0, near[3])
+    z_step(1, 0)
     norm_slot(3)
     put_n1 = pltpu.make_async_copy(n1_v, n1, loc.at[6])
     put_n1.start()
@@ -1467,8 +1467,8 @@
     chip_sum(1, order[0])
     hop(0, 0, True)
     hop(0, 2, False)
+    chip_sum(1, order[1])
     partial(1, 2)
-    chip_sum(1, order[1])
     partial(1, 3)
     chip_sum(1, order[2])
     hop(0, 1, True)

time: 299 us -> 291 us (0.973)
  Pallas kernels: 293 us -> 287 us
    pallas_call x1, Pallas kernels: 132 us -> 121 us  [front(): pl.pallas_call(functools.partial(front_kernel, p), out_shape=(jax.ShapeDt...]
    pallas_call x1, Pallas kernels: 154 us -> 159 us  [back(): pl.pallas_call(functools.partial(back_kernel, p), out_shape=(jax.ShapeDty...]
where the time goes in v8:
time: 291 us; the launch traced here: 289 us
  Pallas kernels  287 us (99%)
    pallas_call x1, Pallas kernels, back(): pl.pallas_call(functools.partial(back_kernel, p), out_shape=(jax.ShapeDty...  159 us
    pallas_call x1, Pallas kernels, front(): pl.pallas_call(functools.partial(front_kernel, p), out_shape=(jax.ShapeDt...  121 us
    pallas_call x1, Pallas kernels, finish(): pl.pallas_call(functools.partial(finish_kernel, p), grid=(steps,), out_sh...  7.42 us

profile of v8, /device:TPU:16, one launch (start us, length us, event | category | flops | bytes accessed | tf_op | source)
XLA Modules:
  0.0 288.8 jit_solution(17780507483185849071)
XLA Ops:
  1.3 120.7 %front.1 = (bf16[4,512,2048]{2,1,0:T(8,128)(2,1)}, bf16[4,512,2048]{2,1,0:T(8,128)(2,1)}, bf16[4,2,2,2,64,768]{5,4,3,2,1,0:T(8,128)(2,1)}, bf16[768,2048]{1,0:T(...) custom-call(bf16[128,2048]{1,0:T(8,128)(2,1)} %x.3, ...), custom_call_target="tpu_custom_call" | custom-call | tf_op jit(solution)/shard_map/front/pallas_call | solution.py:829
  122.0 159.3 %back.1 = (f32[128,2048]{1,0:T(8,128)}, f32[128,2048]{1,0:T(8,128)}, bf16[64,6144]{1,0:T(8,128)(2,1)}, bf16[64,8192]{1,0:T(8,128)(2,1)}, bf16[2,256,2048]{2,1,0:...) custom-call(bf16[2048,512]{1,0:T(8,128)(2,1)} %get-tuple-element.46., ...), custom_call_target="tpu_custom_call", output_to_operand_aliasing={{9}: (3, {})} | custom-call | tf_op jit(solution)/shard_map/back/pallas_call | solution.py:1549
  281.3 7.4 %finish.1 = (bf16[128,2048]{1,0:T(8,128)(2,1)}, bf16[128,2048]{1,0:T(8,128)(2,1)}, f32[64,6144]{1,0:T(8,128)}, f32[64,8192]{1,0:T(8,128)}, f32[256,2048]{1,0:T(8...) custom-call(s32[1]{0:T(128)S(6)} %copy.31.lens, ...), custom_call_target="tpu_custom_call" | custom-call | tf_op jit(solution)/shard_map/finish/pallas_call | solution.py:1805

commit v9 on v8

--- a/solution.py
+++ b/solution.py
@@ -128,7 +128,7 @@
 
 
 def add_rows(dst, parts, rows):
-    step = 16
+    step = min(rows, 32)
 
     def body(k, carry):
         at = pl.ds(pl.multiple_of(k * step, step), step)

time: 291 us -> 290 us (level)
  no operation moved by 1% of the time
where the time goes in v9:
time: 290 us; the launch traced here: 288 us
  Pallas kernels  287 us (99%)
    pallas_call x1, Pallas kernels, back(): pl.pallas_call(functools.partial(back_kernel, p), out_shape=(jax.ShapeDty...  159 us
    pallas_call x1, Pallas kernels, front(): pl.pallas_call(functools.partial(front_kernel, p), out_shape=(jax.ShapeDt...  121 us
    pallas_call x1, Pallas kernels, finish(): pl.pallas_call(functools.partial(finish_kernel, p), grid=(steps,), out_sh...  7.42 us

profile of v9, /device:TPU:16, one launch (start us, length us, event | category | flops | bytes accessed | tf_op | source)
XLA Modules:
  0.0 288.4 jit_solution(5960046587181633209)
XLA Ops:
  1.3 120.7 %front.1 = (bf16[4,512,2048]{2,1,0:T(8,128)(2,1)}, bf16[4,512,2048]{2,1,0:T(8,128)(2,1)}, bf16[4,2,2,2,64,768]{5,4,3,2,1,0:T(8,128)(2,1)}, bf16[768,2048]{1,0:T(...) custom-call(bf16[128,2048]{1,0:T(8,128)(2,1)} %x.3, ...), custom_call_target="tpu_custom_call" | custom-call | tf_op jit(solution)/shard_map/front/pallas_call | solution.py:829
  122.0 158.9 %back.1 = (f32[128,2048]{1,0:T(8,128)}, f32[128,2048]{1,0:T(8,128)}, bf16[64,6144]{1,0:T(8,128)(2,1)}, bf16[64,8192]{1,0:T(8,128)(2,1)}, bf16[2,256,2048]{2,1,0:...) custom-call(bf16[2048,512]{1,0:T(8,128)(2,1)} %get-tuple-element.46., ...), custom_call_target="tpu_custom_call", output_to_operand_aliasing={{9}: (3, {})} | custom-call | tf_op jit(solution)/shard_map/back/pallas_call | solution.py:1549
  280.9 7.4 %finish.1 = (bf16[128,2048]{1,0:T(8,128)(2,1)}, bf16[128,2048]{1,0:T(8,128)(2,1)}, f32[64,6144]{1,0:T(8,128)}, f32[64,8192]{1,0:T(8,128)}, f32[256,2048]{1,0:T(8...) custom-call(s32[1]{0:T(128)S(6)} %copy.31.lens, ...), custom_call_target="tpu_custom_call" | custom-call | tf_op jit(solution)/shard_map/finish/pallas_call | solution.py:1805
